TPU v7x, 512 devices: a whole 4x4x16 slice. The times are simulated.
512 devices in a mesh: gx: 32 (over z_hi, x, y), gy: 16 (over z_lo, core).
Axes of the slice: x: 4, y: 4, z: 16 (z_hi: 2, z_lo: 8; z = z_hi * 8 + z_lo), core: 2. Of those that a mesh axis runs over, the one named last changes fastest.
Arguments:
- particles: float32 [32, 16, 128, 8, 128], P('gx', 'gy'), may hold values from -4 to 4, as said below
- send_list: int32 [32, 16, 4, 64], P('gx', 'gy'), may hold values from 0 to 127, as said below
- move_count: int32 [32, 16, 2, 4], P('gx', 'gy'), may hold values from 0 to 16, as said below
- tile_pairs: int32 [32, 16, 512, 2], P('gx', 'gy'), may hold values from 0 to 383, as said below
- tile_count: int32 [32, 16], P('gx', 'gy'), may hold values from 128 to 512, as said below
- drag_tiles: int32 [32, 16, 384, 4], P('gx', 'gy'), may hold values from 0 to 99, as said below
- cell_slot: int32 [32, 16, 384, 128], P('gx', 'gy'), may hold values from 0 to 511
- fluid_velocity: float32 [3, 256, 128, 128], P(None, 'gx', 'gy'), may hold values from -6 to 6
- pressure_init: float32 [256, 128, 128], P('gx', 'gy'), may hold values from -6 to 6
- source: float32 [256, 128, 128], P('gx', 'gy'), may hold values from -6 to 6
- solid_old: float32 [256, 128, 128], P('gx', 'gy'), may hold values from 0 to 0.5
- screening: float32 [256, 128, 128], P('gx', 'gy'), may hold values from 0.5 to 2
Outputs:
- pressure: float32 [256, 128, 128], P('gx', 'gy')
- drag_sum: float32 [3, 256, 128, 128], P(None, 'gx', 'gy')
- block_force: float32 [32, 16, 384, 3, 128], P('gx', 'gy')
Inputs may be any that keep to these rules, and one draw needn't show every extreme that they name: `particles`: positions lie in 0 to 3, radii in 0.3 to 0.7, drag coefficients in 0.5 to 4. `send_list`: row d of a device sends toward the neighbour of higher gx (d 0), lower gx (1), higher gy (2), lower gy (3). Its first move_count[0, d] entries are blocks that move there, all different over the four rows; the others are copies, and every slot is sent. `move_count`: entry [0, d] counts blocks leaving in direction d of send_list; entry [1, d] equals entry [0, d] of the neighbour that feeds received group d (lower gx, higher gx, lower gy, higher gy). Counts toward or from outside the grid are 0; 16 is reached in every draw. `tile_pairs`: the first block of every tile slot is owned by the device after migration; the second is an own block or a slot received from a neighbour inside the grid. `tile_count`: devices at the lowest and highest gy use all 512 tiles. `drag_tiles`: the 4 columns of a block are different.
All inputs are finite; a program needn't handle non-finite values.
Results may differ from a plain program's by a relative error of at most 0.0003.
Values sent between devices are 32-bit elements; how exact they have to be, the bound alone decides.
No kernel may reach another device: no remote copies, remote signals or barrier semaphores. Data moves between devices by JAX's collectives and lax.ppermute only.
A program may use at most 64 MiB of HBM per device.

v0:
```python
import jax
import jax.numpy as jnp
from jax import lax
from jax.sharding import PartitionSpec as P

ITERS = 4


topmost_value = lax.Precision.HIGHEST
stiffness = 0.5
density_ratio = 2.0
tile_group = 32
block_groups = 6


def extended_2(block, sides, width):
    for axis, dim in sides:
        count = lax.axis_size(axis)
        forward = [(i, i + 1) for i in range(count - 1)]
        backward = [(target, source) for source, target in forward]
        low = lax.ppermute(
            lax.slice_in_dim(block, block.shape[dim] - width, None, axis=dim), axis, forward
        )
        high = lax.ppermute(lax.slice_in_dim(block, 0, width, axis=dim), axis, backward)
        block = jnp.concatenate([low, block, high], axis=dim)
    return block


def ownership(send_rows, leave_count, arrive_count, block_count):
    slot_count = send_rows.shape[1]
    slot_iota = jnp.arange(slot_count, dtype=jnp.int32)
    leaving = (send_rows[:, :, None] == jnp.arange(block_count, dtype=jnp.int32)[None, None, :]) & (
        slot_iota[None, :, None] < leave_count[:, None, None]
    )
    stayed = jnp.logical_not(jnp.any(leaving, axis=(0, 1)))
    arrived = slot_iota[None, :] < arrive_count[:, None]
    return jnp.concatenate([stayed, arrived.reshape(-1)]).astype(jnp.float32)


def contact_forces(block_pool, tile_rows, tile_total):
    slot_total = tile_rows.shape[0]
    grouped = tile_rows.reshape(slot_total // tile_group, tile_group, 2)
    marks = (
        (jnp.arange(slot_total, dtype=jnp.int32) < tile_total)
        .astype(jnp.float32)
        .reshape(-1, tile_group)
    )

    def tile_step(force_total, step_item):
        pair_group, mark_group = step_item
        first_side = block_pool[pair_group[:, 0], 0:4, :]
        second_side = block_pool[pair_group[:, 1], 0:4, :]
        distance = (first_side[:, 0, :, None] - second_side[:, 0, None, :]) ** 2
        distance = distance + (first_side[:, 1, :, None] - second_side[:, 1, None, :]) ** 2
        distance = distance + (first_side[:, 2, :, None] - second_side[:, 2, None, :]) ** 2
        reach = first_side[:, 3, :, None] + second_side[:, 3, None, :]
        weight = jnp.maximum(1.0 - distance / (reach * reach), 0.0) * mark_group[:, None, None]
        pulled = jnp.einsum("tab,tcb->tca", weight, second_side[:, 0:3, :], precision=topmost_value)
        pushed = first_side[:, 0:3, :] * jnp.sum(weight, axis=2)[:, None, :]
        return (force_total.at[pair_group[:, 0]].add(stiffness * (pushed - pulled)), None)

    start_force = jnp.zeros((block_pool.shape[0], 3, block_pool.shape[2]), jnp.float32)
    force_total, unused = lax.scan(tile_step, start_force, (grouped, marks))
    return force_total


def couple(block_pool, owned_mask, tile_ids, slot_ids, columns):
    depth_count = columns.shape[2]
    column_count = columns.shape[0]
    tile_width = tile_ids.shape[1]
    per_group = block_pool.shape[0] // block_groups

    def group_advance(deposit, step_item):
        block_state, owned_rows, group_tiles, group_slots = step_item
        depth_ids = group_slots % depth_count
        slot_tile = group_slots // depth_count
        depth_pick = (
            depth_ids[:, :, None] == jnp.arange(depth_count, dtype=jnp.int32)[None, None, :]
        ).astype(jnp.float32)
        slot_selection = (
            slot_tile[:, :, None] == jnp.arange(tile_width, dtype=jnp.int32)[None, None, :]
        ).astype(jnp.float32)
        local_flow = columns[group_tiles]
        depth_position = jnp.einsum(
            "gkcz,gpz->gkcp", local_flow, depth_pick, precision=topmost_value
        )
        fluid_sampled_locally = jnp.einsum(
            "hxdq,hqx->hdq", depth_position, slot_selection, precision=topmost_value
        )
        drag_force = (
            block_state[:, 7:8, :]
            * (fluid_sampled_locally - block_state[:, 4:7, :])
            * owned_rows[:, None, None]
        )
        volume = block_state[:, 3:4, :] ** 3 * owned_rows[:, None, None]
        loading_contributions = jnp.concatenate([drag_force, volume], axis=1)
        slot_breakdown = jnp.einsum(
            "bfm,bmd->bdfm", loading_contributions, slot_selection, precision=topmost_value
        )
        spread = jnp.einsum("gkcp,gpz->gkcz", slot_breakdown, depth_pick, precision=topmost_value)
        column_pick = (
            group_tiles[:, :, None] == jnp.arange(column_count, dtype=jnp.int32)[None, None, :]
        ).astype(jnp.float32)
        deposit = deposit + jnp.einsum(
            "gkn,gkcz->ncz", column_pick, spread, precision=topmost_value
        )
        return (deposit, drag_force)

    step_items = (
        block_pool.reshape(block_groups, per_group, block_pool.shape[1], block_pool.shape[2]),
        owned_mask.reshape(block_groups, per_group),
        tile_ids.reshape(block_groups, per_group, tile_width),
        slot_ids.reshape(block_groups, per_group, slot_ids.shape[1]),
    )
    start_deposit = jnp.zeros((column_count, 4, depth_count), jnp.float32)
    deposit, drag_force = lax.scan(group_advance, start_deposit, step_items)
    return (drag_force.reshape(block_pool.shape[0], 3, block_pool.shape[2]), deposit)


def relax(padded, relax_gain, offset):
    full = jnp.pad(padded, ((0, 0), (0, 0), (1, 1)))
    neighbours = full[2:, 1:-1, 1:-1] + full[:-2, 1:-1, 1:-1]
    neighbours = neighbours + full[1:-1, 2:, 1:-1] + full[1:-1, :-2, 1:-1]
    neighbours = neighbours + full[1:-1, 1:-1, 2:] + full[1:-1, 1:-1, :-2]
    return relax_gain * neighbours + offset


def fold_rims(spread):
    core = spread[:, 2:-2, 2:-2]
    core = core.at[:, 0, :].add(spread[:, 0, 2:-2])
    core = core.at[:, -1, :].add(spread[:, -1, 2:-2])
    core = core.at[:, :, 0].add(spread[:, 2:-2, 0])
    core = core.at[:, :, -1].add(spread[:, 2:-2, -1])
    core = core.at[:, 0, 0].add(spread[:, 0, 0])
    core = core.at[:, 0, -1].add(spread[:, 0, -1])
    core = core.at[:, -1, 0].add(spread[:, -1, 0])
    core = core.at[:, -1, -1].add(spread[:, -1, -1])
    return core


def body(
    particles,
    send_list,
    move_count,
    tile_pairs,
    tile_count,
    drag_tiles,
    cell_slot,
    fluid_velocity,
    pressure_init,
    source,
    solid_old,
    screening,
):
    own_blocks = particles[0, 0]
    send_rows = send_list[0, 0]
    outgoing = own_blocks[send_rows]
    axial_out = jnp.stack([outgoing[1], outgoing[0]])
    radial_out = jnp.stack([outgoing[3], outgoing[2]])
    axial_in = extended_2(axial_out, (("gx", 0),), 1)
    radial_in = extended_2(radial_out, (("gy", 0),), 1)
    block_pool = jnp.concatenate(
        [own_blocks, axial_in[0], axial_in[3], radial_in[0], radial_in[3]], axis=0
    )
    owned_mask = ownership(send_rows, move_count[0, 0, 0], move_count[0, 0, 1], own_blocks.shape[0])
    contact = contact_forces(block_pool, tile_pairs[0, 0], tile_count[0, 0])
    cells_x = pressure_init.shape[0]
    cells_y = pressure_init.shape[1]
    depth_count = pressure_init.shape[2]
    column_count = (cells_x + 2) * (cells_y + 2)
    flow_rim = extended_2(fluid_velocity, (("gx", 1), ("gy", 2)), 1)
    columns = flow_rim.reshape(3, column_count, depth_count).transpose(1, 0, 2)
    drag_force, deposit = couple(block_pool, owned_mask, drag_tiles[0, 0], cell_slot[0, 0], columns)
    block_force = contact + drag_force
    extended = deposit.transpose(1, 0, 2).reshape(4, cells_x + 2, cells_y + 2, depth_count)
    gathered = extended_2(extended, (("gx", 1), ("gy", 2)), 1)
    loads = fold_rims(gathered)
    drag_sum = loads[0:3]
    relax_gain = 1.0 / (6.0 + screening)
    offset = relax_gain * (source + density_ratio * (loads[3] - solid_old))
    pressure = pressure_init
    for sweep_turn in range(ITERS):
        padded = extended_2(pressure, (("gx", 0), ("gy", 1)), 1)
        pressure = relax(padded, relax_gain, offset)
    return (pressure, drag_sum, block_force[None, None])


def solution(mesh):
    in_specs = (
        P("gx", "gy", None, None, None),
        P("gx", "gy", None, None),
        P("gx", "gy", None, None),
        P("gx", "gy", None, None),
        P("gx", "gy"),
        P("gx", "gy", None, None),
        P("gx", "gy", None, None),
        P(None, "gx", "gy", None),
        P("gx", "gy", None),
        P("gx", "gy", None),
        P("gx", "gy", None),
        P("gx", "gy", None),
    )
    out_specs = (P("gx", "gy", None), P(None, "gx", "gy", None), P("gx", "gy", None, None, None))
    return jax.shard_map(body, mesh=mesh, in_specs=in_specs, out_specs=out_specs, check_vma=False)
```

profile of v0, /device:TPU:127, one launch (start us, length us, event | category | flops | bytes accessed | tf_op | source)
XLA Modules:
  0.0 492.8 jit_solution(1266490336090331505)
XLA Ops:
  4.2 12.3 %collective-permute-start.4 = (f32[1,64,8,128]{3,2,1,0:T(8,128)}, f32[1,64,8,128]{3,2,1,0:T(8,128)S(1)}, u32[]{:S(2)}, u32[]{:S(2)}) collective-permute-start(f32[1,64,8,128]{3,2,1,0:T(8,128)} %get-tuple-element.393), channel_id=1, source_target_pairs={{0,16},{16,32},{32,48},{48,64},{64,80},{80,96},{96,112},{112,128},... | collective-permute-start | bytes 786440 | tf_op jit(solution)/shard_map/ppermute | solution.py:21
  18.4 3.5 collective-permute-start.6
  21.9 16.6 %collective-permute-start.8 = (f32[3,1,8,128]{3,2,1,0:T(8,128)S(1)}, f32[3,1,8,128]{3,2,1,0:T(8,128)S(1)}, u32[]{:S(2)}, u32[]{:S(2)}) collective-permute-start(f32[3,1,8,128]{3,2,1,0:T(8,128)S(1)} %get-tuple-element.401), channel_id=1, source_target_pairs={{0,16},{16,32},{32,48},{48,64},{64,80},{80,96},{96,112},{112,128},... | collective-permute-start | bytes 36872 | tf_op jit(solution)/shard_map/ppermute | solution.py:21
  43.1 3.4 collective-permute-start
  46.5 13.9 %collective-permute-done = f32[1,8,128]{2,1,0:T(8,128)S(1)} collective-permute-done((f32[1,8,128]{2,1,0:T(8,128)S(1)}, f32[1,8,128]{2,1,0:T(8,128)S(1)}, u32[]{:S(2)}, u32[]{:S(2)}) %collective-permute-start) | collective-permute-done | bytes 4128 | tf_op jit(solution)/shard_map/ppermute | solution.py:24
  62.3 15.4 %collective-permute-done.9 = f32[3,1,8,128]{3,2,1,0:T(8,128)S(1)} collective-permute-done((f32[3,1,8,128]{3,2,1,0:T(8,128)S(1)}, f32[3,1,8,128]{3,2,1,0:T(8,128)S(1)}, u32[]{:S(2)}, u32[]{:S(2)}) %collective-permute-start.9) | collective-permute-done | bytes 12320 | tf_op jit(solution)/shard_map/ppermute | solution.py:24
  77.7 5.5 %collective-permute-start.10 = (f32[3,10,1,128]{3,2,1,0:T(1,128)S(1)}, f32[3,10,1,128]{3,2,1,0:T(1,128)S(1)}, u32[]{:S(2)}, u32[]{:S(2)}) collective-permute-start(f32[3,10,1,128]{3,2,1,0:T(1,128)S(1)} %get-tuple-element.398), channel_id=1, source_target_pairs={{0,1},{1,2},{2,3},{3,4},{4,5},{5,6},{6,7},{7,8},{8,9},{9,10},{10,1... | collective-permute-start | bytes 46088 | tf_op jit(solution)/shard_map/ppermute | solution.py:21
  91.7 4.9 collective-permute-start.3
  96.7 73.5 %while.34 = (s32[]{:T(128)}, f32[100,4,128]{2,0,1:T(8,128)S(1)}, f32[6,64,3,128]{3,1,0,2:T(8,128)}, s32[6,64,4]{1,0,2:T(8,128)S(1)}, s32[6,64,128]{2,1,0:T(8,128...) while((s32[]{:T(128)}, f32[100,4,128]{2,0,1:T(8,128)S(1)}, ...), condition=%wide.region_2.3_spmd.clone, body=%wide.region_1.2_spmd.clone.sunk | while | flops 512539392 | bytes 5653123 | solution.py:116
  99.5 4.1 fusion.106
  105.4 3.0 fusion.107
  111.8 4.1 fusion.106
  117.6 3.0 fusion.107
  124.0 4.1 fusion.106
  129.9 3.0 fusion.107
  136.3 4.1 fusion.106
  142.1 3.0 fusion.107
  148.5 4.1 fusion.106
  154.4 3.0 fusion.107
  160.7 4.1 fusion.106
  166.6 3.0 fusion.107
  172.2 3.4 collective-permute-start.13
  175.8 13.9 %collective-permute-done.13 = f32[4,1,10,128]{3,0,2,1:T(4,128)S(1)} collective-permute-done((f32[4,1,10,128]{3,0,2,1:T(4,128)S(1)}, f32[4,1,10,128]{3,0,2,1:T(4,128)S(1)}, u32[]{:S(2)}, u32[]{:S(2)}) %collective-permute-start.13) | collective-permute-done | bytes 20512 | tf_op jit(solution)/shard_map/ppermute | solution.py:24
  189.7 3.3 collective-permute-start.14
  195.0 4.4 collective-permute-done.15
  203.4 16.3 %collective-permute-start.17 = (f32[1,8,128]{2,1,0:T(8,128)S(1)}, f32[1,8,128]{2,1,0:T(8,128)S(1)}, u32[]{:S(2)}, u32[]{:S(2)}) collective-permute-start(f32[1,8,128]{2,1,0:T(8,128)S(1)} %get-tuple-element.414), channel_id=1, source_target_pairs={{0,16},{16,32},{32,48},{48,64},{64,80},{80,96},{96,112},{112,128},... | collective-permute-start | bytes 12296 | tf_op jit(solution)/shard_map/ppermute | solution.py:21
  222.4 4.9 collective-permute-start.19
  230.2 16.6 %collective-permute-start.21 = (f32[1,8,128]{2,1,0:T(8,128)S(1)}, f32[1,8,128]{2,1,0:T(8,128)S(1)}, u32[]{:S(2)}, u32[]{:S(2)}) collective-permute-start(f32[1,8,128]{2,1,0:T(8,128)S(1)} %get-tuple-element.412), channel_id=1, source_target_pairs={{0,16},{16,32},{32,48},{48,64},{64,80},{80,96},{96,112},{112,128},... | collective-permute-start | bytes 12296 | tf_op jit(solution)/shard_map/ppermute | solution.py:21
  249.4 6.3 %collective-permute-start.23 = (f32[10,1,128]{2,1,0:T(1,128)S(1)}, f32[10,1,128]{2,1,0:T(1,128)S(1)}, u32[]{:S(2)}, u32[]{:S(2)}) collective-permute-start(f32[10,1,128]{2,1,0:T(1,128)S(1)} %get-tuple-element.404), channel_id=1, source_target_pairs={{0,1},{1,2},{2,3},{3,4},{4,5},{5,6},{6,7},{7,8},{8,9},{9,10},{10,1... | collective-permute-start | bytes 15368 | tf_op jit(solution)/shard_map/ppermute | solution.py:21
  258.6 16.8 %collective-permute-start.25 = (f32[1,8,128]{2,1,0:T(8,128)S(1)}, f32[1,8,128]{2,1,0:T(8,128)S(1)}, u32[]{:S(2)}, u32[]{:S(2)}) collective-permute-start(f32[1,8,128]{2,1,0:T(8,128)S(1)} %get-tuple-element.410), channel_id=1, source_target_pairs={{0,16},{16,32},{32,48},{48,64},{64,80},{80,96},{96,112},{112,128},... | collective-permute-start | bytes 12296 | tf_op jit(solution)/shard_map/ppermute | solution.py:21
  275.6 206.1 %while.33 = (s32[]{:T(128)}, f32[384,3,128]{2,1,0:T(4,128)S(1)}, s32[16,32,2]{1,0,2:T(8,128)S(1)}, f32[384,8,128]{2,0,1:T(8,128)S(1)}, f32[16,32]{1,0:T(8,128)S(1)}, /*index=5*/s32[]{:T(128)}) while((s32[]{:T(128)}, f32[384,3,128]{2,1,0:T(4,128)S(1)}, s32[16,32,2]{1,0,2:T(8,128)S(1)}, f32[384,8,128]{2,0,1:T(8,128)S(1)}, ...), condition=%wide.region_7.8_spmd, body=%wide.region_4.0_spmd.sunk | while | flops 34124096 | bytes 1313101 | solution.py:63
  277.0 3.3 fusion.96
  280.3 6.5 %fusion.97 = f32[32,3,128]{2,1,0:T(4,128)S(1)} fusion(f32[32]{0:T(128)S(1)} %dynamic-slice_bitcast_fusion.2, f32[32,128]{1,0:T(8,128)S(1)} %get-tuple-element.516, f32[32,128]{1,0:T(8,128)S(1)} %get-tuple-element.517, f32[32,128]{1,0:T(8,128)S(1)} %get-tuple-element.518, f32[32,128]{1,0:T(8,128)S(1)} %get-tuple-element.519, ...), kind=kOutput, calls=%fused_computation.7.clone.1 | convolution fusion | flops 26251264 | bytes 295040 | tf_op jit(solution)/shard_map/while/body/eval_jaxpr/tab,tcb->tca/dot_general | solution.py:58
  289.9 3.3 fusion.96
  293.2 6.5 %fusion.97 = f32[32,3,128]{2,1,0:T(4,128)S(1)} fusion(f32[32]{0:T(128)S(1)} %dynamic-slice_bitcast_fusion.2, f32[32,128]{1,0:T(8,128)S(1)} %get-tuple-element.516, f32[32,128]{1,0:T(8,128)S(1)} %get-tuple-element.517, f32[32,128]{1,0:T(8,128)S(1)} %get-tuple-element.518, f32[32,128]{1,0:T(8,128)S(1)} %get-tuple-element.519, ...), kind=kOutput, calls=%fused_computation.7.clone.1 | convolution fusion | flops 26251264 | bytes 295040 | tf_op jit(solution)/shard_map/while/body/eval_jaxpr/tab,tcb->tca/dot_general | solution.py:58
  302.8 3.3 fusion.96
  306.1 6.5 %fusion.97 = f32[32,3,128]{2,1,0:T(4,128)S(1)} fusion(f32[32]{0:T(128)S(1)} %dynamic-slice_bitcast_fusion.2, f32[32,128]{1,0:T(8,128)S(1)} %get-tuple-element.516, f32[32,128]{1,0:T(8,128)S(1)} %get-tuple-element.517, f32[32,128]{1,0:T(8,128)S(1)} %get-tuple-element.518, f32[32,128]{1,0:T(8,128)S(1)} %get-tuple-element.519, ...), kind=kOutput, calls=%fused_computation.7.clone.1 | convolution fusion | flops 26251264 | bytes 295040 | tf_op jit(solution)/shard_map/while/body/eval_jaxpr/tab,tcb->tca/dot_general | solution.py:58
  315.7 3.3 fusion.96
  319.0 6.5 %fusion.97 = f32[32,3,128]{2,1,0:T(4,128)S(1)} fusion(f32[32]{0:T(128)S(1)} %dynamic-slice_bitcast_fusion.2, f32[32,128]{1,0:T(8,128)S(1)} %get-tuple-element.516, f32[32,128]{1,0:T(8,128)S(1)} %get-tuple-element.517, f32[32,128]{1,0:T(8,128)S(1)} %get-tuple-element.518, f32[32,128]{1,0:T(8,128)S(1)} %get-tuple-element.519, ...), kind=kOutput, calls=%fused_computation.7.clone.1 | convolution fusion | flops 26251264 | bytes 295040 | tf_op jit(solution)/shard_map/while/body/eval_jaxpr/tab,tcb->tca/dot_general | solution.py:58
  328.6 3.3 fusion.96
  331.9 6.5 %fusion.97 = f32[32,3,128]{2,1,0:T(4,128)S(1)} fusion(f32[32]{0:T(128)S(1)} %dynamic-slice_bitcast_fusion.2, f32[32,128]{1,0:T(8,128)S(1)} %get-tuple-element.516, f32[32,128]{1,0:T(8,128)S(1)} %get-tuple-element.517, f32[32,128]{1,0:T(8,128)S(1)} %get-tuple-element.518, f32[32,128]{1,0:T(8,128)S(1)} %get-tuple-element.519, ...), kind=kOutput, calls=%fused_computation.7.clone.1 | convolution fusion | flops 26251264 | bytes 295040 | tf_op jit(solution)/shard_map/while/body/eval_jaxpr/tab,tcb->tca/dot_general | solution.py:58
  341.4 3.3 fusion.96
  344.7 6.5 %fusion.97 = f32[32,3,128]{2,1,0:T(4,128)S(1)} fusion(f32[32]{0:T(128)S(1)} %dynamic-slice_bitcast_fusion.2, f32[32,128]{1,0:T(8,128)S(1)} %get-tuple-element.516, f32[32,128]{1,0:T(8,128)S(1)} %get-tuple-element.517, f32[32,128]{1,0:T(8,128)S(1)} %get-tuple-element.518, f32[32,128]{1,0:T(8,128)S(1)} %get-tuple-element.519, ...), kind=kOutput, calls=%fused_computation.7.clone.1 | convolution fusion | flops 26251264 | bytes 295040 | tf_op jit(solution)/shard_map/while/body/eval_jaxpr/tab,tcb->tca/dot_general | solution.py:58
  354.3 3.3 fusion.96
  357.6 6.5 %fusion.97 = f32[32,3,128]{2,1,0:T(4,128)S(1)} fusion(f32[32]{0:T(128)S(1)} %dynamic-slice_bitcast_fusion.2, f32[32,128]{1,0:T(8,128)S(1)} %get-tuple-element.516, f32[32,128]{1,0:T(8,128)S(1)} %get-tuple-element.517, f32[32,128]{1,0:T(8,128)S(1)} %get-tuple-element.518, f32[32,128]{1,0:T(8,128)S(1)} %get-tuple-element.519, ...), kind=kOutput, calls=%fused_computation.7.clone.1 | convolution fusion | flops 26251264 | bytes 295040 | tf_op jit(solution)/shard_map/while/body/eval_jaxpr/tab,tcb->tca/dot_general | solution.py:58
  367.2 3.3 fusion.96
  370.5 6.5 %fusion.97 = f32[32,3,128]{2,1,0:T(4,128)S(1)} fusion(f32[32]{0:T(128)S(1)} %dynamic-slice_bitcast_fusion.2, f32[32,128]{1,0:T(8,128)S(1)} %get-tuple-element.516, f32[32,128]{1,0:T(8,128)S(1)} %get-tuple-element.517, f32[32,128]{1,0:T(8,128)S(1)} %get-tuple-element.518, f32[32,128]{1,0:T(8,128)S(1)} %get-tuple-element.519, ...), kind=kOutput, calls=%fused_computation.7.clone.1 | convolution fusion | flops 26251264 | bytes 295040 | tf_op jit(solution)/shard_map/while/body/eval_jaxpr/tab,tcb->tca/dot_general | solution.py:58
  380.1 3.3 fusion.96
  383.4 6.5 %fusion.97 = f32[32,3,128]{2,1,0:T(4,128)S(1)} fusion(f32[32]{0:T(128)S(1)} %dynamic-slice_bitcast_fusion.2, f32[32,128]{1,0:T(8,128)S(1)} %get-tuple-element.516, f32[32,128]{1,0:T(8,128)S(1)} %get-tuple-element.517, f32[32,128]{1,0:T(8,128)S(1)} %get-tuple-element.518, f32[32,128]{1,0:T(8,128)S(1)} %get-tuple-element.519, ...), kind=kOutput, calls=%fused_computation.7.clone.1 | convolution fusion | flops 26251264 | bytes 295040 | tf_op jit(solution)/shard_map/while/body/eval_jaxpr/tab,tcb->tca/dot_general | solution.py:58
  393.0 3.3 fusion.96
  396.3 6.5 %fusion.97 = f32[32,3,128]{2,1,0:T(4,128)S(1)} fusion(f32[32]{0:T(128)S(1)} %dynamic-slice_bitcast_fusion.2, f32[32,128]{1,0:T(8,128)S(1)} %get-tuple-element.516, f32[32,128]{1,0:T(8,128)S(1)} %get-tuple-element.517, f32[32,128]{1,0:T(8,128)S(1)} %get-tuple-element.518, f32[32,128]{1,0:T(8,128)S(1)} %get-tuple-element.519, ...), kind=kOutput, calls=%fused_computation.7.clone.1 | convolution fusion | flops 26251264 | bytes 295040 | tf_op jit(solution)/shard_map/while/body/eval_jaxpr/tab,tcb->tca/dot_general | solution.py:58
  405.8 3.3 fusion.96
  409.1 6.5 %fusion.97 = f32[32,3,128]{2,1,0:T(4,128)S(1)} fusion(f32[32]{0:T(128)S(1)} %dynamic-slice_bitcast_fusion.2, f32[32,128]{1,0:T(8,128)S(1)} %get-tuple-element.516, f32[32,128]{1,0:T(8,128)S(1)} %get-tuple-element.517, f32[32,128]{1,0:T(8,128)S(1)} %get-tuple-element.518, f32[32,128]{1,0:T(8,128)S(1)} %get-tuple-element.519, ...), kind=kOutput, calls=%fused_computation.7.clone.1 | convolution fusion | flops 26251264 | bytes 295040 | tf_op jit(solution)/shard_map/while/body/eval_jaxpr/tab,tcb->tca/dot_general | solution.py:58
  418.7 3.3 fusion.96
  422.0 6.5 %fusion.97 = f32[32,3,128]{2,1,0:T(4,128)S(1)} fusion(f32[32]{0:T(128)S(1)} %dynamic-slice_bitcast_fusion.2, f32[32,128]{1,0:T(8,128)S(1)} %get-tuple-element.516, f32[32,128]{1,0:T(8,128)S(1)} %get-tuple-element.517, f32[32,128]{1,0:T(8,128)S(1)} %get-tuple-element.518, f32[32,128]{1,0:T(8,128)S(1)} %get-tuple-element.519, ...), kind=kOutput, calls=%fused_computation.7.clone.1 | convolution fusion | flops 26251264 | bytes 295040 | tf_op jit(solution)/shard_map/while/body/eval_jaxpr/tab,tcb->tca/dot_general | solution.py:58
  431.6 3.3 fusion.96
  434.9 6.5 %fusion.97 = f32[32,3,128]{2,1,0:T(4,128)S(1)} fusion(f32[32]{0:T(128)S(1)} %dynamic-slice_bitcast_fusion.2, f32[32,128]{1,0:T(8,128)S(1)} %get-tuple-element.516, f32[32,128]{1,0:T(8,128)S(1)} %get-tuple-element.517, f32[32,128]{1,0:T(8,128)S(1)} %get-tuple-element.518, f32[32,128]{1,0:T(8,128)S(1)} %get-tuple-element.519, ...), kind=kOutput, calls=%fused_computation.7.clone.1 | convolution fusion | flops 26251264 | bytes 295040 | tf_op jit(solution)/shard_map/while/body/eval_jaxpr/tab,tcb->tca/dot_general | solution.py:58
  444.5 3.3 fusion.96
  447.8 6.5 %fusion.97 = f32[32,3,128]{2,1,0:T(4,128)S(1)} fusion(f32[32]{0:T(128)S(1)} %dynamic-slice_bitcast_fusion.2, f32[32,128]{1,0:T(8,128)S(1)} %get-tuple-element.516, f32[32,128]{1,0:T(8,128)S(1)} %get-tuple-element.517, f32[32,128]{1,0:T(8,128)S(1)} %get-tuple-element.518, f32[32,128]{1,0:T(8,128)S(1)} %get-tuple-element.519, ...), kind=kOutput, calls=%fused_computation.7.clone.1 | convolution fusion | flops 26251264 | bytes 295040 | tf_op jit(solution)/shard_map/while/body/eval_jaxpr/tab,tcb->tca/dot_general | solution.py:58
  457.3 3.3 fusion.96
  460.6 6.5 %fusion.97 = f32[32,3,128]{2,1,0:T(4,128)S(1)} fusion(f32[32]{0:T(128)S(1)} %dynamic-slice_bitcast_fusion.2, f32[32,128]{1,0:T(8,128)S(1)} %get-tuple-element.516, f32[32,128]{1,0:T(8,128)S(1)} %get-tuple-element.517, f32[32,128]{1,0:T(8,128)S(1)} %get-tuple-element.518, f32[32,128]{1,0:T(8,128)S(1)} %get-tuple-element.519, ...), kind=kOutput, calls=%fused_computation.7.clone.1 | convolution fusion | flops 26251264 | bytes 295040 | tf_op jit(solution)/shard_map/while/body/eval_jaxpr/tab,tcb->tca/dot_general | solution.py:58
  470.2 3.3 fusion.96
  473.5 6.5 %fusion.97 = f32[32,3,128]{2,1,0:T(4,128)S(1)} fusion(f32[32]{0:T(128)S(1)} %dynamic-slice_bitcast_fusion.2, f32[32,128]{1,0:T(8,128)S(1)} %get-tuple-element.516, f32[32,128]{1,0:T(8,128)S(1)} %get-tuple-element.517, f32[32,128]{1,0:T(8,128)S(1)} %get-tuple-element.518, f32[32,128]{1,0:T(8,128)S(1)} %get-tuple-element.519, ...), kind=kOutput, calls=%fused_computation.7.clone.1 | convolution fusion | flops 26251264 | bytes 295040 | tf_op jit(solution)/shard_map/while/body/eval_jaxpr/tab,tcb->tca/dot_general | solution.py:58
  483.6 5.7 %collective-permute-start.27 = (f32[10,1,128]{2,1,0:T(1,128)S(1)}, f32[10,1,128]{2,1,0:T(1,128)S(1)}, u32[]{:S(2)}, u32[]{:S(2)}) collective-permute-start(f32[10,1,128]{2,1,0:T(1,128)S(1)} %get-tuple-element.402), channel_id=1, source_target_pairs={{0,1},{1,2},{2,3},{3,4},{4,5},{5,6},{6,7},{7,8},{8,9},{9,10},{10,1... | collective-permute-start | bytes 15368 | tf_op jit(solution)/shard_map/ppermute | solution.py:21
  (374 shorter events, 123.0 us)
Async XLA Ops:
  3.2 18.7 %copy-start.3 = (f32[3,8,8,128]{3,2,1,0:T(8,128)S(1)}, f32[3,8,8,128]{3,2,1,0:T(8,128)}, u32[]{:S(2)}) copy-start(f32[3,8,8,128]{3,2,1,0:T(8,128)} %param.39) | copy-start | bytes 294916
  3.2 35.3 %copy-start.2 = (f32[8,8,128]{2,1,0:T(8,128)S(1)}, f32[8,8,128]{2,1,0:T(8,128)}, u32[]{:S(2)}) copy-start(f32[8,8,128]{2,1,0:T(8,128)} %param.40) | copy-start | bytes 98308
  3.2 37.2 %copy-start = (f32[1,1,128,8,128]{4,3,2,1,0:T(8,128)S(1)}, f32[1,1,128,8,128]{4,3,2,1,0:T(8,128)}, u32[]{:S(2)}) copy-start(f32[1,1,128,8,128]{4,3,2,1,0:T(8,128)} %param.32) | copy-start | bytes 1572868
  3.2 37.3 %copy-start.9 = (s32[1,1,2,4]{3,2,1,0:T(2,128)S(1)}, s32[1,1,2,4]{3,2,1,0:T(2,128)}, u32[]{:S(2)}) copy-start(s32[1,1,2,4]{3,2,1,0:T(2,128)} %param.34) | copy-start | bytes 100
  3.3 37.4 %copy-start.6 = (s32[1,1,4,64]{3,2,1,0:T(4,128)S(1)}, s32[1,1,4,64]{3,2,1,0:T(4,128)}, u32[]{:S(2)}) copy-start(s32[1,1,4,64]{3,2,1,0:T(4,128)} %param.33) | copy-start | bytes 3076
  3.3 38.3 %copy-start.10 = (s32[4]{0:T(128)S(1)}, s32[4]{0:T(128)}, u32[]{:S(2)}) copy-start(s32[4]{0:T(128)} %constant.324.clone.1) | copy-start | bytes 52
  3.3 39.7 %copy-start.7 = (s32[1,1,384,4]{2,3,1,0:T(4,128)S(1)}, s32[1,1,384,4]{2,3,1,0:T(4,128)}, u32[]{:S(2)}) copy-start(s32[1,1,384,4]{2,3,1,0:T(4,128)} %param.37) | copy-start | bytes 18436
  4.2 87.5 %collective-permute-start.4 = (f32[1,64,8,128]{3,2,1,0:T(8,128)}, f32[1,64,8,128]{3,2,1,0:T(8,128)S(1)}, u32[]{:S(2)}, u32[]{:S(2)}) collective-permute-start(f32[1,64,8,128]{3,2,1,0:T(8,128)} %get-tuple-element.393), channel_id=1, source_target_pairs={{0,16},{16,32},{32,48},{48,64},{64,80},{80,96},{96,112},{112,128},... | collective-permute-start | bytes 786440 | tf_op jit(solution)/shard_map/ppermute | solution.py:21
  16.5 80.1 %collective-permute-start.5 = (f32[1,64,8,128]{3,2,1,0:T(8,128)}, f32[1,64,8,128]{3,2,1,0:T(8,128)S(1)}, u32[]{:S(2)}, u32[]{:S(2)}) collective-permute-start(f32[1,64,8,128]{3,2,1,0:T(8,128)} %get-tuple-element.392), channel_id=1, source_target_pairs={{16,0},{32,16},{48,32},{64,48},{80,64},{96,80},{112,96},{128,112},... | collective-permute-start | bytes 786440 | tf_op jit(solution)/shard_map/ppermute | solution.py:24
  18.4 78.2 %collective-permute-start.6 = (f32[1,64,8,128]{3,2,1,0:T(8,128)S(1)}, f32[1,64,8,128]{3,2,1,0:T(8,128)S(1)}, u32[]{:S(2)}, u32[]{:S(2)}) collective-permute-start(f32[1,64,8,128]{3,2,1,0:T(8,128)S(1)} %get-tuple-element.391), channel_id=1, source_target_pairs={{0,1},{1,2},{2,3},{3,4},{4,5},{5,6},{6,7},{7,8},{8,9},{9,10},{10,1... | collective-permute-start | bytes 786440 | tf_op jit(solution)/shard_map/ppermute | solution.py:21
  21.9 40.4 %collective-permute-start.8 = (f32[3,1,8,128]{3,2,1,0:T(8,128)S(1)}, f32[3,1,8,128]{3,2,1,0:T(8,128)S(1)}, u32[]{:S(2)}, u32[]{:S(2)}) collective-permute-start(f32[3,1,8,128]{3,2,1,0:T(8,128)S(1)} %get-tuple-element.401), channel_id=1, source_target_pairs={{0,16},{16,32},{32,48},{48,64},{64,80},{80,96},{96,112},{112,128},... | collective-permute-start | bytes 36872 | tf_op jit(solution)/shard_map/ppermute | solution.py:21
  38.5 4.5 collective-permute-start.1
  43.1 17.3 %collective-permute-start = (f32[1,8,128]{2,1,0:T(8,128)S(1)}, f32[1,8,128]{2,1,0:T(8,128)S(1)}, u32[]{:S(2)}, u32[]{:S(2)}) collective-permute-start(f32[1,8,128]{2,1,0:T(8,128)S(1)} %get-tuple-element.416), channel_id=1, source_target_pairs={{16,0},{32,16},{48,32},{64,48},{80,64},{96,80},{112,96},{128,112},... | collective-permute-start | bytes 12296 | tf_op jit(solution)/shard_map/ppermute | solution.py:24
  60.4 17.4 %collective-permute-start.9 = (f32[3,1,8,128]{3,2,1,0:T(8,128)S(1)}, f32[3,1,8,128]{3,2,1,0:T(8,128)S(1)}, u32[]{:S(2)}, u32[]{:S(2)}) collective-permute-start(f32[3,1,8,128]{3,2,1,0:T(8,128)S(1)} %get-tuple-element.400), channel_id=1, source_target_pairs={{16,0},{32,16},{48,32},{64,48},{80,64},{96,80},{112,96},{128,112},... | collective-permute-start | bytes 36872 | tf_op jit(solution)/shard_map/ppermute | solution.py:24
  77.7 7.5 %collective-permute-start.10 = (f32[3,10,1,128]{3,2,1,0:T(1,128)S(1)}, f32[3,10,1,128]{3,2,1,0:T(1,128)S(1)}, u32[]{:S(2)}, u32[]{:S(2)}) collective-permute-start(f32[3,10,1,128]{3,2,1,0:T(1,128)S(1)} %get-tuple-element.398), channel_id=1, source_target_pairs={{0,1},{1,2},{2,3},{3,4},{4,5},{5,6},{6,7},{7,8},{8,9},{9,10},{10,1... | collective-permute-start | bytes 46088 | tf_op jit(solution)/shard_map/ppermute | solution.py:21
  83.3 6.3 %collective-permute-start.11 = (f32[3,10,1,128]{3,2,1,0:T(1,128)S(1)}, f32[3,10,1,128]{3,2,1,0:T(1,128)S(1)}, u32[]{:S(2)}, u32[]{:S(2)}) collective-permute-start(f32[3,10,1,128]{3,2,1,0:T(1,128)S(1)} %get-tuple-element.399), channel_id=1, source_target_pairs={{1,0},{2,1},{3,2},{4,3},{5,4},{6,5},{7,6},{8,7},{9,8},{10,9},{11,1... | collective-permute-start | bytes 46088 | tf_op jit(solution)/shard_map/ppermute | solution.py:24
  85.3 11.4 %collective-permute-start.7 = (f32[1,64,8,128]{3,2,1,0:T(8,128)S(1)}, f32[1,64,8,128]{3,2,1,0:T(8,128)S(1)}, u32[]{:S(2)}, u32[]{:S(2)}) collective-permute-start(f32[1,64,8,128]{3,2,1,0:T(8,128)S(1)} %get-tuple-element.390), channel_id=1, source_target_pairs={{1,0},{2,1},{3,2},{4,3},{5,4},{6,5},{7,6},{8,7},{9,8},{10,9},{11,1... | collective-permute-start | bytes 786440 | tf_op jit(solution)/shard_map/ppermute | solution.py:24
  89.6 86.0 %collective-permute-start.2 = (f32[10,1,128]{2,1,0:T(1,128)S(1)}, f32[10,1,128]{2,1,0:T(1,128)S(1)}, u32[]{:S(2)}, u32[]{:S(2)}) collective-permute-start(f32[10,1,128]{2,1,0:T(1,128)S(1)} %get-tuple-element.409), channel_id=1, source_target_pairs={{1,0},{2,1},{3,2},{4,3},{5,4},{6,5},{7,6},{8,7},{9,8},{10,9},{11,1... | collective-permute-start | bytes 15368 | tf_op jit(solution)/shard_map/ppermute | solution.py:24
  91.7 83.9 %collective-permute-start.3 = (f32[10,1,128]{2,1,0:T(1,128)S(1)}, f32[10,1,128]{2,1,0:T(1,128)S(1)}, u32[]{:S(2)}, u32[]{:S(2)}) collective-permute-start(f32[10,1,128]{2,1,0:T(1,128)S(1)} %get-tuple-element.408), channel_id=1, source_target_pairs={{0,1},{1,2},{2,3},{3,4},{4,5},{5,6},{6,7},{7,8},{8,9},{9,10},{10,1... | collective-permute-start | bytes 15368 | tf_op jit(solution)/shard_map/ppermute | solution.py:21
  170.1 31.3 %copy-start.1 = (f32[8,8,128]{2,1,0:T(8,128)S(1)}, f32[8,8,128]{2,1,0:T(8,128)}, u32[]{:S(2)}) copy-start(f32[8,8,128]{2,1,0:T(8,128)} %param.43) | copy-start | bytes 98308
  170.1 31.3 %copy-start.4 = (f32[8,8,128]{2,1,0:T(8,128)S(1)}, f32[8,8,128]{2,1,0:T(8,128)}, u32[]{:S(2)}) copy-start(f32[8,8,128]{2,1,0:T(8,128)} %param.41) | copy-start | bytes 98308
  170.2 31.3 %copy-start.5 = (f32[8,8,128]{2,1,0:T(8,128)S(1)}, f32[8,8,128]{2,1,0:T(8,128)}, u32[]{:S(2)}) copy-start(f32[8,8,128]{2,1,0:T(8,128)} %param.42) | copy-start | bytes 98308
  170.2 85.6 %copy-start.8 = (s32[1,1,512,2]{2,3,1,0:T(2,128)S(1)}, s32[1,1,512,2]{2,3,1,0:T(2,128)}, u32[]{:S(2)}) copy-start(s32[1,1,512,2]{2,3,1,0:T(2,128)} %param.35) | copy-start | bytes 12292
  170.3 5.5 %collective-permute-start.12 = (f32[4,1,10,128]{3,0,2,1:T(4,128)S(1)}, f32[4,1,10,128]{3,0,2,1:T(4,128)S(1)}, u32[]{:S(2)}, u32[]{:S(2)}) collective-permute-start(f32[4,1,10,128]{3,0,2,1:T(4,128)S(1)} %get-tuple-element.397), channel_id=1, source_target_pairs={{0,16},{16,32},{32,48},{48,64},{64,80},{80,96},{96,112},{112,128},... | collective-permute-start | bytes 61448 | tf_op jit(solution)/shard_map/ppermute | solution.py:21
  172.2 17.5 %collective-permute-start.13 = (f32[4,1,10,128]{3,0,2,1:T(4,128)S(1)}, f32[4,1,10,128]{3,0,2,1:T(4,128)S(1)}, u32[]{:S(2)}, u32[]{:S(2)}) collective-permute-start(f32[4,1,10,128]{3,0,2,1:T(4,128)S(1)} %get-tuple-element.396), channel_id=1, source_target_pairs={{16,0},{32,16},{48,32},{64,48},{80,64},{96,80},{112,96},{128,112},... | collective-permute-start | bytes 61448 | tf_op jit(solution)/shard_map/ppermute | solution.py:24
  189.7 5.3 %collective-permute-start.14 = (f32[4,12,1,128]{3,0,2,1:T(4,128)S(1)}, f32[4,12,1,128]{3,0,2,1:T(4,128)S(1)}, u32[]{:S(2)}, u32[]{:S(2)}) collective-permute-start(f32[4,12,1,128]{3,0,2,1:T(4,128)S(1)} %get-tuple-element.395), channel_id=1, source_target_pairs={{0,1},{1,2},{2,3},{3,4},{4,5},{5,6},{6,7},{7,8},{8,9},{9,10},{10,1... | collective-permute-start | bytes 73736 | tf_op jit(solution)/shard_map/ppermute | solution.py:21
  193.0 6.4 %collective-permute-start.15 = (f32[4,12,1,128]{3,0,2,1:T(4,128)S(1)}, f32[4,12,1,128]{3,0,2,1:T(4,128)S(1)}, u32[]{:S(2)}, u32[]{:S(2)}) collective-permute-start(f32[4,12,1,128]{3,0,2,1:T(4,128)S(1)} %get-tuple-element.394), channel_id=1, source_target_pairs={{1,0},{2,1},{3,2},{4,3},{5,4},{6,5},{7,6},{8,7},{9,8},{10,9},{11,1... | collective-permute-start | bytes 73736 | tf_op jit(solution)/shard_map/ppermute | solution.py:24
  201.5 18.2 %collective-permute-start.16 = (f32[1,8,128]{2,1,0:T(8,128)S(1)}, f32[1,8,128]{2,1,0:T(8,128)S(1)}, u32[]{:S(2)}, u32[]{:S(2)}) collective-permute-start(f32[1,8,128]{2,1,0:T(8,128)S(1)} %get-tuple-element.415), channel_id=1, source_target_pairs={{16,0},{32,16},{48,32},{64,48},{80,64},{96,80},{112,96},{128,112},... | collective-permute-start | bytes 12296 | tf_op jit(solution)/shard_map/ppermute | solution.py:24
  203.4 17.0 %collective-permute-start.17 = (f32[1,8,128]{2,1,0:T(8,128)S(1)}, f32[1,8,128]{2,1,0:T(8,128)S(1)}, u32[]{:S(2)}, u32[]{:S(2)}) collective-permute-start(f32[1,8,128]{2,1,0:T(8,128)S(1)} %get-tuple-element.414), channel_id=1, source_target_pairs={{0,16},{16,32},{32,48},{48,64},{64,80},{80,96},{96,112},{112,128},... | collective-permute-start | bytes 12296 | tf_op jit(solution)/shard_map/ppermute | solution.py:21
  220.5 6.8 %collective-permute-start.18 = (f32[10,1,128]{2,1,0:T(1,128)S(1)}, f32[10,1,128]{2,1,0:T(1,128)S(1)}, u32[]{:S(2)}, u32[]{:S(2)}) collective-permute-start(f32[10,1,128]{2,1,0:T(1,128)S(1)} %get-tuple-element.407), channel_id=1, source_target_pairs={{1,0},{2,1},{3,2},{4,3},{5,4},{6,5},{7,6},{8,7},{9,8},{10,9},{11,1... | collective-permute-start | bytes 15368 | tf_op jit(solution)/shard_map/ppermute | solution.py:24
  222.4 5.6 %collective-permute-start.19 = (f32[10,1,128]{2,1,0:T(1,128)S(1)}, f32[10,1,128]{2,1,0:T(1,128)S(1)}, u32[]{:S(2)}, u32[]{:S(2)}) collective-permute-start(f32[10,1,128]{2,1,0:T(1,128)S(1)} %get-tuple-element.406), channel_id=1, source_target_pairs={{0,1},{1,2},{2,3},{3,4},{4,5},{5,6},{6,7},{7,8},{8,9},{9,10},{10,1... | collective-permute-start | bytes 15368 | tf_op jit(solution)/shard_map/ppermute | solution.py:21
  228.3 19.1 %collective-permute-start.20 = (f32[1,8,128]{2,1,0:T(8,128)S(1)}, f32[1,8,128]{2,1,0:T(8,128)S(1)}, u32[]{:S(2)}, u32[]{:S(2)}) collective-permute-start(f32[1,8,128]{2,1,0:T(8,128)S(1)} %get-tuple-element.413), channel_id=1, source_target_pairs={{16,0},{32,16},{48,32},{64,48},{80,64},{96,80},{112,96},{128,112},... | collective-permute-start | bytes 12296 | tf_op jit(solution)/shard_map/ppermute | solution.py:24
  230.2 17.3 %collective-permute-start.21 = (f32[1,8,128]{2,1,0:T(8,128)S(1)}, f32[1,8,128]{2,1,0:T(8,128)S(1)}, u32[]{:S(2)}, u32[]{:S(2)}) collective-permute-start(f32[1,8,128]{2,1,0:T(8,128)S(1)} %get-tuple-element.412), channel_id=1, source_target_pairs={{0,16},{16,32},{32,48},{48,64},{64,80},{80,96},{96,112},{112,128},... | collective-permute-start | bytes 12296 | tf_op jit(solution)/shard_map/ppermute | solution.py:21
  247.5 8.6 %collective-permute-start.22 = (f32[10,1,128]{2,1,0:T(1,128)S(1)}, f32[10,1,128]{2,1,0:T(1,128)S(1)}, u32[]{:S(2)}, u32[]{:S(2)}) collective-permute-start(f32[10,1,128]{2,1,0:T(1,128)S(1)} %get-tuple-element.405), channel_id=1, source_target_pairs={{1,0},{2,1},{3,2},{4,3},{5,4},{6,5},{7,6},{8,7},{9,8},{10,9},{11,1... | collective-permute-start | bytes 15368 | tf_op jit(solution)/shard_map/ppermute | solution.py:24
  249.4 7.0 %collective-permute-start.23 = (f32[10,1,128]{2,1,0:T(1,128)S(1)}, f32[10,1,128]{2,1,0:T(1,128)S(1)}, u32[]{:S(2)}, u32[]{:S(2)}) collective-permute-start(f32[10,1,128]{2,1,0:T(1,128)S(1)} %get-tuple-element.404), channel_id=1, source_target_pairs={{0,1},{1,2},{2,3},{3,4},{4,5},{5,6},{6,7},{7,8},{8,9},{9,10},{10,1... | collective-permute-start | bytes 15368 | tf_op jit(solution)/shard_map/ppermute | solution.py:21
  256.7 225.0 %collective-permute-start.24 = (f32[1,8,128]{2,1,0:T(8,128)S(1)}, f32[1,8,128]{2,1,0:T(8,128)S(1)}, u32[]{:S(2)}, u32[]{:S(2)}) collective-permute-start(f32[1,8,128]{2,1,0:T(8,128)S(1)} %get-tuple-element.411), channel_id=1, source_target_pairs={{16,0},{32,16},{48,32},{64,48},{80,64},{96,80},{112,96},{128,112},... | collective-permute-start | bytes 12296 | tf_op jit(solution)/shard_map/ppermute | solution.py:24
  258.6 223.0 %collective-permute-start.25 = (f32[1,8,128]{2,1,0:T(8,128)S(1)}, f32[1,8,128]{2,1,0:T(8,128)S(1)}, u32[]{:S(2)}, u32[]{:S(2)}) collective-permute-start(f32[1,8,128]{2,1,0:T(8,128)S(1)} %get-tuple-element.410), channel_id=1, source_target_pairs={{0,16},{16,32},{32,48},{48,64},{64,80},{80,96},{96,112},{112,128},... | collective-permute-start | bytes 12296 | tf_op jit(solution)/shard_map/ppermute | solution.py:21
  481.7 10.2 %collective-permute-start.26 = (f32[10,1,128]{2,1,0:T(1,128)S(1)}, f32[10,1,128]{2,1,0:T(1,128)S(1)}, u32[]{:S(2)}, u32[]{:S(2)}) collective-permute-start(f32[10,1,128]{2,1,0:T(1,128)S(1)} %get-tuple-element.403), channel_id=1, source_target_pairs={{1,0},{2,1},{3,2},{4,3},{5,4},{6,5},{7,6},{8,7},{9,8},{10,9},{11,1... | collective-permute-start | bytes 15368 | tf_op jit(solution)/shard_map/ppermute | solution.py:24
  483.6 8.3 %collective-permute-start.27 = (f32[10,1,128]{2,1,0:T(1,128)S(1)}, f32[10,1,128]{2,1,0:T(1,128)S(1)}, u32[]{:S(2)}, u32[]{:S(2)}) collective-permute-start(f32[10,1,128]{2,1,0:T(1,128)S(1)} %get-tuple-element.402), channel_id=1, source_target_pairs={{0,1},{1,2},{2,3},{3,4},{4,5},{5,6},{6,7},{7,8},{8,9},{9,10},{10,1... | collective-permute-start | bytes 15368 | tf_op jit(solution)/shard_map/ppermute | solution.py:21
where the time goes:
time: 495 us; the launch traced here: 493 us
  matrix products  150 us (30%)
  starting transfers between devices  147 us (30%)
  other arithmetic  101 us (20%)
  waiting for transfers between devices  50.8 us (10%)
  local copies, waits for them, and re-layouts  40.4 us (8%)
    ppermute x14, starting transfers between devices, extended_2(): lax.ppermute(lax.slice_in_dim(block, block.shape[dim] - width, None, axis...  116 us
    dot_general x16, matrix products, tile_step(): jnp.einsum('tab,tcb->tca', weight, second_side[:, 0:3, :], precision=topm...  104 us
    reduce_sum x16, other arithmetic, tile_step(): pushed = first_side[:, 0:3, :] * jnp.sum(weight, axis=2)[:, None, :]  52.2 us
    ppermute x14, waiting for transfers between devices, extended_2(): lax.ppermute(lax.slice_in_dim(block, 0, width, axis=dim), axis, backward)  48.9 us
    ppermute x14, starting transfers between devices, extended_2(): lax.ppermute(lax.slice_in_dim(block, 0, width, axis=dim), axis, backward)  30.7 us
    scatter-add x16, other arithmetic, tile_step(): force_total.at[pair_group[:, 0]].add(stiffness * (pushed - pulled))  26.4 us
    dot_general x6, matrix products, group_advance(): jnp.einsum('gkcz,gpz->gkcp', local_flow, depth_pick, precision=topmost_va...  24.8 us
    dot_general x6, matrix products, group_advance(): jnp.einsum('gkcp,gpz->gkcz', slot_breakdown, depth_pick, precision=topmos...  18 us
  transfers between devices with their start and end apart: 28, of which 9 were waited for; matrix products, arithmetic and copies ran while one was open for 58% of the time, Pallas kernels for 0%

commit v1 on v0

v1 whole, which is shorter than its diff:
```python
import functools

import jax
import jax.numpy as jnp
from jax import lax
from jax.experimental import pallas as pl
from jax.experimental.pallas import tpu as pltpu
from jax.sharding import PartitionSpec as P

F32 = jnp.float32
BF16 = jnp.bfloat16
NB = 128
SLOTS = 64
MOVERS = 16
PAIRS = (SLOTS - MOVERS) // 2
GROUP = MOVERS + PAIRS
OWNABLE = NB + 4 * MOVERS
POOL_TILES = NB + 4 * GROUP
ITERS = 4

VM = pl.BlockSpec(memory_space=pltpu.VMEM)
SM = pl.BlockSpec(memory_space=pltpu.SMEM)
PARAMS = pltpu.CompilerParams(vmem_limit_bytes=32 * 2**20)


def shape(*dims):
    return jax.ShapeDtypeStruct(dims, F32)


def call(kernel, outs, in_specs, scratch=(), flops=10**6, moved=10**6):
    return pl.pallas_call(
        kernel,
        out_shape=outs,
        in_specs=in_specs,
        out_specs=jax.tree.map(lambda _: VM, outs),
        scratch_shapes=list(scratch),
        compiler_params=PARAMS,
        cost_estimate=pl.CostEstimate(flops=flops, bytes_accessed=moved, transcendentals=0),
    )


def put_blocks(parts, sends, direction, out):
    for s in range(MOVERS):
        out[s] = parts[sends[direction, s]]
    for k in range(PAIRS):
        out[MOVERS + k, 0:4, :] = parts[sends[direction, MOVERS + k], 0:4, :]
        out[MOVERS + k, 4:8, :] = parts[sends[direction, MOVERS + PAIRS + k], 0:4, :]


def pack_y(parts, sends, flow, pres, screen, source, solid, out_e, out_o, gain_ref, rest_ref):
    parity = lax.axis_index("gy") % 2
    gain_ref[...] = 1.0 / (6.0 + screen[...])
    rest_ref[...] = source[...] - 2.0 * solid[...]
    for out, up in ((out_e, parity == 0), (out_o, parity == 1)):
        put_blocks(parts, sends, jnp.where(up, 2, 3), out)
        for c in range(3):
            out[GROUP + c] = jnp.where(up, flow[c, :, 7, :], flow[c, :, 0, :])
        at = GROUP + 3
        for ref in (pres, gain_ref, rest_ref):
            for x in range(8):
                row = 4 * (x % 2)
                out[at + x // 2, row : row + 4, :] = jnp.where(up, ref[x, 4:8, :], ref[x, 0:4, :])
            at += 4


Y_TILES = GROUP + 3 + 12
X_TILES = GROUP + 6 + 8 + 6 + 6


def pack_x(
    parts, sends, flow, pres, gain, rest, in_e, in_o, out_e, out_o, flow_x, pres_x, gain_x, rest_x
):
    parity = lax.axis_index("gy") % 2
    even = parity == 0
    for c in range(3):
        flow_x[c, :, 4:12, :] = flow[c]
        a = in_e[GROUP + c]
        b = in_o[GROUP + c]
        flow_x[c, :, 12, :] = jnp.where(even, a, b)
        flow_x[c, :, 3, :] = jnp.where(even, b, a)
    at = GROUP + 3
    for wide, ref in ((pres_x, pres), (gain_x, gain), (rest_x, rest)):
        wide[:, 4:12, :] = ref[...]
        for x in range(8):
            row = 4 * (x % 2)
            a = in_e[at + x // 2, row : row + 4, :]
            b = in_o[at + x // 2, row : row + 4, :]
            wide[x, 12:16, :] = jnp.where(even, a, b)
            wide[x, 0:4, :] = jnp.where(even, b, a)
        at += 4
    parity = lax.axis_index("gx") % 2
    for out, up in ((out_e, parity == 0), (out_o, parity == 1)):
        put_blocks(parts, sends, jnp.where(up, 0, 1), out)
        at = GROUP
        for c in range(3):
            edge = jnp.where(up, 7, 0)
            out[at] = flow_x[c, edge, 0:8, :]
            out[at + 1] = flow_x[c, edge, 8:16, :]
            at += 2
        for wide, count in ((pres_x, 4), (gain_x, 3), (rest_x, 3)):
            first = jnp.where(up, 8 - count, 0)
            for r in range(count):
                out[at] = wide[first + r, 0:8, :]
                out[at + 1] = wide[first + r, 8:16, :]
                at += 2


def couple(
    parts, sends, moves, tiles, slots, flow_x, in_xe, in_xo, in_ye, in_yo,
    drag, dep, out_e, out_o,
    pool, table, sums, owned,
):
    x_even = lax.axis_index("gx") % 2 == 0
    y_even = lax.axis_index("gy") % 2 == 0
    pool[0:NB] = parts[...]
    for d, (up, even, a, b) in enumerate(
        ((0, x_even, in_xe, in_xo), (1, x_even, in_xe, in_xo), (0, y_even, in_ye, in_yo), (1, y_even, in_ye, in_yo))
    ):
        first, second = (b, a) if up == 0 else (a, b)
        pool[NB + d * MOVERS : NB + (d + 1) * MOVERS] = jnp.where(even, first[0:MOVERS], second[0:MOVERS])

    def stay(k, carry):
        owned[k] = 1.0
        return carry

    lax.fori_loop(0, NB, stay, 0)
    for d in range(4):

        def leave(s, carry, d=d):
            owned[sends[d, s]] = 0.0
            return carry

        lax.fori_loop(0, moves[0, d], leave, 0)
        for s in range(MOVERS):
            owned[NB + d * MOVERS + s] = jnp.where(s < moves[1, d], 1.0, 0.0)
    for c in range(3):
        high = jnp.where(x_even, in_xe[GROUP + 2 * c], in_xo[GROUP + 2 * c])
        high2 = jnp.where(x_even, in_xe[GROUP + 2 * c + 1], in_xo[GROUP + 2 * c + 1])
        low = jnp.where(x_even, in_xo[GROUP + 2 * c], in_xe[GROUP + 2 * c])
        low2 = jnp.where(x_even, in_xo[GROUP + 2 * c + 1], in_xe[GROUP + 2 * c + 1])
        for x in range(10):
            if x == 0:
                one, two = low, low2
            elif x == 9:
                one, two = high, high2
            else:
                one, two = flow_x[c, x - 1, 0:8, :], flow_x[c, x - 1, 8:16, :]
            table[x * 10 : x * 10 + 5, 4 + c, :] = one[3:8]
            table[x * 10 + 5 : x * 10 + 10, 4 + c, :] = two[0:5]
    sums[...] = jnp.zeros_like(sums)
    drag[...] = jnp.zeros_like(drag)

    row = lax.broadcasted_iota(jnp.int32, (8, NB), 0)
    low_rows = row < 4
    last_row = row == 7
    half = jnp.where(low_rows, 0, 1)
    depth_rows = lax.broadcasted_iota(jnp.int32, (128, NB), 0)

    def one_block(m, at):
        own = owned[m]
        state = pool[m]
        code = jnp.broadcast_to(slots[pl.ds(at, 1), :], (8, NB))
        depth = code & 127
        slot = code >> 7
        columns = [tiles[k, at] for k in range(4)]
        seen = [jnp.take_along_axis(table[n], depth, axis=1, mode="promise_in_bounds") for n in columns]
        at_particle = jnp.where(
            slot < 2, jnp.where(slot == 0, seen[0], seen[1]), jnp.where(slot == 2, seen[2], seen[3])
        )
        coeff = jnp.broadcast_to(state[7:8], (8, NB))
        radius = jnp.broadcast_to(state[3:4], (8, NB))
        values = jnp.where(last_row, radius * radius * radius, coeff * (at_particle - state)) * own
        both = jnp.where(low_rows, pltpu.roll(values, 4, 0), values)
        for c in range(3):
            drag[c, pl.ds(at, 1), :] = both[c : c + 1]
        first = jnp.where(slot == half, both, 0.0)
        second = jnp.where(slot == half + 2, both, 0.0)
        sixteen = jnp.concatenate([first, second], axis=0)
        upper = sixteen.astype(BF16)
        lower = (sixteen - upper.astype(F32)).astype(BF16)
        pick = (depth_rows == jnp.broadcast_to(depth[0:1], (128, NB))).astype(BF16)
        spread = lax.dot_general(
            jnp.concatenate([upper, lower], axis=0), pick, (((1,), (1,)), ((), ())),
            preferred_element_type=F32,
        )
        spread = spread[0:16] + spread[16:32]
        parts_ = (
            jnp.where(low_rows, spread[0:8], 0.0), jnp.where(low_rows, 0.0, spread[0:8]),
            jnp.where(low_rows, spread[8:16], 0.0), jnp.where(low_rows, 0.0, spread[8:16]),
        )
        return columns, parts_

    def add(columns, pieces):
        olds = [sums[n] for n in columns]
        for n, old, piece in zip(columns, olds, pieces, strict=True):
            sums[n] = old + piece

    def blocks(g, carry):
        made = []
        for u in range(4):
            m = g * 4 + u
            at = jnp.where(m < NB, m, NB + ((m - NB) // MOVERS) * SLOTS + (m - NB) % MOVERS)
            made.append(one_block(m, at))
        for columns, pieces in made:
            add(columns, pieces)
        return carry

    lax.fori_loop(0, OWNABLE // 4, blocks, 0)
    dep[...] = jnp.zeros_like(dep)
    for n in range(100):
        total = sums[n]
        total = total[0:4] + total[4:8]
        for f in range(4):
            dep[f, n // 10, n % 10 + 3, :] = total[f]
    for out, up in ((out_e, y_even), (out_o, jnp.logical_not(y_even))):
        for f in range(4):
            for x in range(10):
                i = f * 10 + x
                r = 4 * (i % 2)
                out[i // 2, r : r + 4, :] = jnp.where(up, dep[f, x, 9:13, :], dep[f, x, 3:7, :])


def fold_y(dep, in_e, in_o, dep_x, out_e, out_o):
    even = lax.axis_index("gy") % 2 == 0
    dep_x[...] = dep[...]
    for f in range(4):
        for x in range(10):
            i = f * 10 + x
            r = 4 * (i % 2)
            a = in_e[i // 2, r : r + 4, :]
            b = in_o[i // 2, r : r + 4, :]
            dep_x[f, x, 11:15, :] += jnp.where(even, a, b)
            dep_x[f, x, 1:5, :] += jnp.where(even, b, a)
    parity = lax.axis_index("gx") % 2
    for out, up in ((out_e, parity == 0), (out_o, parity == 1)):
        first = jnp.where(up, 6, 0)
        rim = jnp.where(up, 9, 0)
        for r in range(4):
            out[2 * r] = dep_x[3, first + r, 0:8, :]
            out[2 * r + 1] = dep_x[3, first + r, 8:16, :]
        for c in range(3):
            out[8 + 2 * c] = dep_x[c, rim, 0:8, :]
            out[9 + 2 * c] = dep_x[c, rim, 8:16, :]


D_TILES = 14


def tiles16(ref, at):
    return jnp.concatenate([ref[at], ref[at + 1]], axis=0)


def finish(dep_x, in_e, in_o, near_e, near_o, pres_x, gain_x, rest_x, pressure, drag_sum, now, new, gain, off):
    even = lax.axis_index("gx") % 2 == 0

    def from_up(a, b, at):
        return jnp.where(even, tiles16(a, at), tiles16(b, at))

    def from_down(a, b, at):
        return jnp.where(even, tiles16(b, at), tiles16(a, at))

    for c in range(3):
        drag_sum[c] = dep_x[c, 1:9, 4:12, :]
        drag_sum[c, 0] += from_down(in_e, in_o, 8 + 2 * c)[4:12]
        drag_sum[c, 7] += from_up(in_e, in_o, 8 + 2 * c)[4:12]
    p_at = GROUP + 6
    g_at = p_at + 8
    s_at = g_at + 6
    for x in range(16):
        if x < 4:
            now[x] = from_down(near_e, near_o, p_at + 2 * x)
        elif x < 12:
            now[x] = pres_x[x - 4]
        else:
            now[x] = from_up(near_e, near_o, p_at + 2 * (x - 12))
    for x in range(1, 15):
        if x < 4:
            g = from_down(near_e, near_o, g_at + 2 * (x - 1))
            s = from_down(near_e, near_o, s_at + 2 * (x - 1))
        elif x < 12:
            g = gain_x[x - 4]
            s = rest_x[x - 4]
        else:
            g = from_up(near_e, near_o, g_at + 2 * (x - 12))
            s = from_up(near_e, near_o, s_at + 2 * (x - 12))
        load = jnp.zeros((16, 128), F32)
        if 3 <= x <= 12:
            load = load + dep_x[3, x - 3]
        if x <= 4:
            load = load + from_down(in_e, in_o, 2 * (x - 1))
        if x >= 11:
            load = load + from_up(in_e, in_o, 2 * (x - 11))
        gain[x] = g
        off[x] = g * (s + 2.0 * load)
    lane = lax.broadcasted_iota(jnp.int32, (16, 128), 1)
    inner_low = lane > 0
    inner_high = lane < 127
    source, target = now, new
    for sweep in range(ITERS):
        for x in range(sweep + 1, 15 - sweep):
            p = source[x]
            near = source[x - 1] + source[x + 1]
            near = near + pltpu.roll(p, 1, 0) + pltpu.roll(p, 15, 0)
            near = near + jnp.where(inner_low, pltpu.roll(p, 1, 1), 0.0)
            near = near + jnp.where(inner_high, pltpu.roll(p, 127, 1), 0.0)
            target[x] = gain[x] * near + off[x]
        source, target = target, source
    pressure[...] = source[4:12, 4:12, :]


def contact(pairs, count, parts, in_xe, in_xo, in_ye, in_yo, drag, after, force, pool):
    x_even = lax.axis_index("gx") % 2 == 0
    y_even = lax.axis_index("gy") % 2 == 0
    pool[0 : NB * 8] = parts[...].reshape(NB * 8, 128)
    for d, (up, even, a, b) in enumerate(
        ((0, x_even, in_xe, in_xo), (1, x_even, in_xe, in_xo), (0, y_even, in_ye, in_yo), (1, y_even, in_ye, in_yo))
    ):
        first, second = (b, a) if up == 0 else (a, b)
        at = (NB + d * GROUP) * 8
        pool[at : at + GROUP * 8] = jnp.where(even, first[0:GROUP], second[0:GROUP]).reshape(GROUP * 8, 128)
    force[...] = drag[...]
    total = count[0, 0]

    def row_of(m):
        q = m - NB
        d = q // SLOTS
        s = q % SLOTS
        base = (NB + d * GROUP) * 8
        tail = jnp.where(
            s < MOVERS + PAIRS, 8 * s, 8 * (s - PAIRS) + 4
        )
        return jnp.where(m < NB, 8 * m, base + tail)

    def tile(t):
        i = pairs[0, t]
        j = pairs[1, t]
        x = pool[pl.ds(pl.multiple_of(row_of(i), 4), 4), :]
        y = pool[pl.ds(pl.multiple_of(row_of(j), 4), 4), :]
        xs = [jnp.broadcast_to(x[c : c + 1], (8, 128)) for c in range(4)]
        ys = [
            pltpu.roll(jnp.broadcast_to(y[c : c + 1], (8, 128)), 0, 1, stride=1, stride_axis=0)
            for c in range(4)
        ]
        sums = [jnp.zeros((8, 128), F32) for _ in range(3)]
        for step in range(16):
            turned = ys if step == 0 else [pltpu.roll(v, 8 * step, 1) for v in ys]
            apart = [xs[c] - turned[c] for c in range(3)]
            distance = apart[0] * apart[0] + apart[1] * apart[1] + apart[2] * apart[2]
            reach = xs[3] + turned[3]
            reach = reach * reach
            guess = pl.reciprocal(reach, approx=True)
            inverse = guess * (2.0 - reach * guess)
            weight = jnp.maximum(1.0 - distance * inverse, 0.0)
            sums = [s + weight * a for s, a in zip(sums, apart, strict=True)]
        scale = jnp.where(t < total, 0.5, 0.0)
        return i, [jnp.sum(s, axis=0, keepdims=True) * scale for s in sums]

    unroll = 4

    def step(g, carry):
        made = [tile(g * unroll + u) for u in range(unroll)]
        for i, sums in made:
            for c in range(3):
                force[c, pl.ds(i, 1), :] += sums[c]
        return carry

    lax.fori_loop(0, (total + unroll - 1) // unroll, step, 0)


def pairs_of(first, count, last):
    up = [(i, i + 1) for i in range(first, last, 2)]
    return up + [(b, a) for a, b in up]


def swap(array, axis, first):
    count = lax.axis_size(axis)
    return lax.ppermute(array, axis, pairs_of(first, count, count - 1))


def body(
    particles,
    send_list,
    move_count,
    tile_pairs,
    tile_count,
    drag_tiles,
    cell_slot,
    fluid_velocity,
    pressure_init,
    source,
    solid_old,
    screening,
):
    parts = particles[0, 0]
    sends = send_list[0, 0]
    moves = move_count[0, 0]
    tiles = drag_tiles[0, 0].T
    pairs = tile_pairs[0, 0].T
    slots = cell_slot[0, 0]
    cells = (8, 8, 128)
    wide = (8, 16, 128)
    ye, yo, gain, rest = call(
        pack_y, (shape(Y_TILES, 8, 128), shape(Y_TILES, 8, 128), shape(*cells), shape(*cells)), [VM, SM] + [VM] * 5
    )(parts, sends, fluid_velocity, pressure_init, screening, source, solid_old)
    got_ye = swap(ye, "gy", 0)
    got_yo = swap(yo, "gy", 1)
    xe, xo, flow_x, pres_x, gain_x, rest_x = call(
        pack_x,
        (shape(X_TILES, 8, 128), shape(X_TILES, 8, 128), shape(3, *wide), shape(*wide), shape(*wide), shape(*wide)),
        [VM, SM] + [VM] * 6,
    )(parts, sends, fluid_velocity, pressure_init, gain, rest, got_ye, got_yo)
    got_xo = swap(xo, "gx", 1)
    got_xe = swap(xe, "gx", 0)
    drag, dep, de, do = call(
        couple,
        (shape(3, 384, 128), shape(4, 10, 16, 128), shape(20, 8, 128), shape(20, 8, 128)),
        [VM, SM, SM, SM] + [VM] * 6,
        [
            pltpu.VMEM((OWNABLE, 8, 128), F32),
            pltpu.VMEM((100, 8, 128), F32),
            pltpu.VMEM((100, 8, 128), F32),
            pltpu.SMEM((OWNABLE,), F32),
        ],
    )(parts, sends, moves, tiles, slots, flow_x, got_xe, got_xo, got_ye, got_yo)
    got_de = swap(de, "gy", 0)
    got_do = swap(do, "gy", 1)
    dep_x, fe, fo = call(
        fold_y, (shape(4, 10, 16, 128), shape(D_TILES, 8, 128), shape(D_TILES, 8, 128)), [VM] * 3
    )(dep, got_de, got_do)
    got_fo = swap(fo, "gx", 1)
    got_fe = swap(fe, "gx", 0)
    force = call(
        contact,
        shape(3, 384, 128),
        [SM, SM] + [VM] * 7,
        [pltpu.VMEM((POOL_TILES * 8, 128), F32)],
        flops=10**9,
    )(pairs, tile_count, parts, got_xe, got_xo, got_ye, got_yo, drag, fo)
    pressure, drag_sum = call(
        finish,
        (shape(*cells), shape(3, *cells)),
        [VM] * 8,
        [pltpu.VMEM((16, 16, 128), F32)] * 4,
    )(dep_x, got_fe, got_fo, got_xe, got_xo, pres_x, gain_x, rest_x)
    return (pressure, drag_sum, force.transpose(1, 0, 2)[None, None])


def solution(mesh):
    in_specs = (
        P("gx", "gy", None, None, None),
        P("gx", "gy", None, None),
        P("gx", "gy", None, None),
        P("gx", "gy", None, None),
        P("gx", "gy"),
        P("gx", "gy", None, None),
        P("gx", "gy", None, None),
        P(None, "gx", "gy", None),
        P("gx", "gy", None),
        P("gx", "gy", None),
        P("gx", "gy", None),
        P("gx", "gy", None),
    )
    out_specs = (P("gx", "gy", None), P(None, "gx", "gy", None), P("gx", "gy", None, None, None))
    return jax.shard_map(body, mesh=mesh, in_specs=in_specs, out_specs=out_specs, check_vma=False)
```

time: 495 us -> 147 us (0.30)
  the two profiles are of different devices: /device:TPU:127 before, /device:TPU:30 now
where the time goes in v1:
time: 147 us; the launch traced here: 146 us
  Pallas kernels  84.5 us (57%)
  starting transfers between devices  47.6 us (32%)
  local copies, waits for them, and re-layouts  6.33 us (4%)
  waiting for transfers between devices  5.92 us (4%)
    pallas_call x1, Pallas kernels, body(): call(contact, shape(3, 384, 128), [SM, SM] + [VM] * 7, [pltpu.VMEM((POOL_...  67.8 us
    ppermute x8, starting transfers between devices, swap(): return lax.ppermute(array, axis, pairs_of(first, count, count - 1))  47.6 us
    pallas_call x1, Pallas kernels, body(): call(couple, (shape(3, 384, 128), shape(4, 10, 16, 128), shape(20, 8, 128...  14.1 us
    unnamed x24, local copies, waits for them, and re-layouts  6.33 us
    ppermute x8, waiting for transfers between devices, swap(): return lax.ppermute(array, axis, pairs_of(first, count, count - 1))  5.92 us
  transfers between devices with their start and end apart: 8, of which 2 were waited for; matrix products, arithmetic and copies ran while one was open for 0% of the time, Pallas kernels for 46%

profile of v1, /device:TPU:30, one launch (start us, length us, event | category | flops | bytes accessed | tf_op | source)
XLA Modules:
  0.0 145.8 jit_solution(16113284933995821645)
XLA Ops:
  0.6 0.0 copy-start.8
  0.6 0.7 copy-done.8
  1.3 0.0 copy-start
  1.3 1.0 copy-done
  2.4 0.0 copy-start.2
  2.4 0.9 copy-done.2
  3.3 0.0 copy-start.4
  3.3 0.8 copy-done.4
  4.0 0.0 copy-start.5
  4.0 0.8 copy-done.5
  4.8 0.0 copy-start.6
  4.8 0.8 copy-done.6
  5.5 0.0 copy-start.7
  5.5 0.8 copy-done.7
  6.3 0.7 shard_map.139
  7.0 1.9 %collective-permute-start = (f32[55,8,128]{2,1,0:T(8,128)S(1)}, f32[55,8,128]{2,1,0:T(8,128)S(1)}, u32[]{:S(2)}, u32[]{:S(2)}) collective-permute-start(f32[55,8,128]{2,1,0:T(8,128)S(1)} %get-tuple-element.24), channel_id=1, source_target_pairs={{0,1},{2,3},{4,5},{6,7},{8,9},{10,11},{12,13},{14,15},{1,0},{3,2},... | collective-permute-start | bytes 675848 | tf_op jit(solution)/shard_map/ppermute | solution.py:377
  9.0 0.7 collective-permute-start.1
  9.6 0.8 collective-permute-done.in_e.in_ye
  10.4 0.0 collective-permute-done.1.in_o.in_yo
  10.4 0.0 copy-start.3
  10.4 0.8 shard_map.140
  11.2 0.0 copy-start.9
  11.2 2.7 %collective-permute-start.2 = (f32[66,8,128]{2,1,0:T(8,128)S(1)}, f32[66,8,128]{2,1,0:T(8,128)S(1)}, u32[]{:S(2)}, u32[]{:S(2)}) collective-permute-start(f32[66,8,128]{2,1,0:T(8,128)S(1)} %get-tuple-element.27), channel_id=1, source_target_pairs={{0,16},{32,48},{64,80},{96,112},{128,144},{160,176},{192,208},{224... | collective-permute-start | bytes 811016 | tf_op jit(solution)/shard_map/ppermute | solution.py:377
  13.9 16.1 %collective-permute-start.3 = (f32[66,8,128]{2,1,0:T(8,128)S(1)}, f32[66,8,128]{2,1,0:T(8,128)S(1)}, u32[]{:S(2)}, u32[]{:S(2)}) collective-permute-start(f32[66,8,128]{2,1,0:T(8,128)S(1)} %get-tuple-element.28), channel_id=1, source_target_pairs={{16,32},{48,64},{80,96},{112,128},{144,160},{176,192},{208,224},{2... | collective-permute-start | bytes 811016 | tf_op jit(solution)/shard_map/ppermute | solution.py:377
  30.0 0.0 collective-permute-done.2.in_xe.near_e
  30.0 5.1 %collective-permute-done.3.in_xo.near_o = f32[66,8,128]{2,1,0:T(8,128)S(1)} collective-permute-done((f32[66,8,128]{2,1,0:T(8,128)S(1)}, f32[66,8,128]{2,1,0:T(8,128)S(1)}, u32[]{:S(2)}, u32[]{:S(2)}) %collective-permute-start.3) | collective-permute-done | bytes 270368 | tf_op jit(solution)/shard_map/ppermute | solution.py:377
  35.1 0.0 copy-start.10
  35.1 0.0 copy-done.3
  35.1 0.0 copy-done.9
  35.1 0.7 copy-done.10
  35.8 0.0 copy-start.1
  35.8 14.1 %shard_map.141 = (f32[3,384,128]{2,1,0:T(8,128)S(1)}, f32[4,10,16,128]{3,2,1,0:T(8,128)S(1)}, f32[20,8,128]{2,1,0:T(8,128)S(1)}, f32[20,8,128]{2,1,0:T(8,128)S(1)}) custom-call(f32[128,8,128]{2,1,0:T(8,128)S(1)} %bitcast.15, s32[4,64]{1,0:T(4,128)S(1)} %bitcast.20, s32[2,4]{1,0:T(2,128)S(1)} %bitcast.22, s32[4,384]{1,0:T(4,128)S(1)} %bitcast.21, ...), custom_call_target="tpu_custom_call" | custom-call | flops 1000000 | bytes 1000000 | tf_op jit(solution)/shard_map/pallas_call | solution.py:414
  50.0 7.5 %collective-permute-start.4 = (f32[20,8,128]{2,1,0:T(8,128)S(1)}, f32[20,8,128]{2,1,0:T(8,128)S(1)}, u32[]{:S(2)}, u32[]{:S(2)}) collective-permute-start(f32[20,8,128]{2,1,0:T(8,128)S(1)} %get-tuple-element.30), channel_id=1, source_target_pairs={{0,1},{2,3},{4,5},{6,7},{8,9},{10,11},{12,13},{14,15},{1,0},{3,2},... | collective-permute-start | bytes 245768 | tf_op jit(solution)/shard_map/ppermute | solution.py:377
  57.5 0.7 collective-permute-start.5
  58.8 0.0 collective-permute-done.4.in_e
  58.8 0.0 collective-permute-done.5.in_o
  58.8 0.1 shard_map.142
  58.9 0.0 copy-start.11
  58.9 1.9 %collective-permute-start.6 = (f32[14,8,128]{2,1,0:T(8,128)S(1)}, f32[14,8,128]{2,1,0:T(8,128)S(1)}, u32[]{:S(2)}, u32[]{:S(2)}) collective-permute-start(f32[14,8,128]{2,1,0:T(8,128)S(1)} %get-tuple-element.33), channel_id=1, source_target_pairs={{0,16},{32,48},{64,80},{96,112},{128,144},{160,176},{192,208},{224... | collective-permute-start | bytes 172040 | tf_op jit(solution)/shard_map/ppermute | solution.py:377
  60.8 16.2 %collective-permute-start.7 = (f32[14,8,128]{2,1,0:T(8,128)S(1)}, f32[14,8,128]{2,1,0:T(8,128)S(1)}, u32[]{:S(2)}, u32[]{:S(2)}) collective-permute-start(f32[14,8,128]{2,1,0:T(8,128)S(1)} %get-tuple-element.34.after), channel_id=1, source_target_pairs={{16,32},{48,64},{80,96},{112,128},{144,160},{176,192},{208,224},{2... | collective-permute-start | bytes 172040 | tf_op jit(solution)/shard_map/ppermute | solution.py:377
  77.0 0.0 copy-done.1
  77.0 0.0 copy-done.11
  77.0 67.8 %shard_map.144 = f32[3,384,128]{2,1,0:T(8,128)} custom-call(s32[2,512]{1,0:T(2,128)S(1)} %bitcast.23, s32[1,1]{1,0:T(1,128)S(6)} %copy.15.count, f32[128,8,128]{2,1,0:T(8,128)S(1)} %bitcast.16, f32[66,8,128]{2,1,0:T(8,128)S(1)} %collective-permute-done.2.in_xe.near_e, f32[66,8,128]{2,1,0:T(8,128)S(1)} %collective-permute-done.3.in_xo.near_o, ...), custom_call_target="tpu_custom_call" | custom-call | flops 1000000000 | bytes 1000000 | tf_op jit(solution)/shard_map/pallas_call | solution.py:432
  144.8 0.0 collective-permute-done.6.in_e
  144.8 0.0 collective-permute-done.7.in_o
  144.8 1.0 shard_map.143
Async XLA Ops:
  0.6 0.7 copy-start.8
  1.3 1.0 copy-start
  2.4 0.9 copy-start.2
  3.3 0.8 copy-start.4
  4.0 0.8 copy-start.5
  4.8 0.8 copy-start.6
  5.5 0.8 copy-start.7
  7.0 3.4 %collective-permute-start = (f32[55,8,128]{2,1,0:T(8,128)S(1)}, f32[55,8,128]{2,1,0:T(8,128)S(1)}, u32[]{:S(2)}, u32[]{:S(2)}) collective-permute-start(f32[55,8,128]{2,1,0:T(8,128)S(1)} %get-tuple-element.24), channel_id=1, source_target_pairs={{0,1},{2,3},{4,5},{6,7},{8,9},{10,11},{12,13},{14,15},{1,0},{3,2},... | collective-permute-start | bytes 675848 | tf_op jit(solution)/shard_map/ppermute | solution.py:377
  9.0 1.5 collective-permute-start.1
  10.4 24.7 %copy-start.3 = (s32[1,1,384,128]{3,2,1,0:T(8,128)S(1)}, s32[1,1,384,128]{3,2,1,0:T(8,128)}, u32[]{:S(2)}) copy-start(s32[1,1,384,128]{3,2,1,0:T(8,128)} %param.18) | copy-start | bytes 589828
  11.2 24.0 %copy-start.9 = (s32[1,1,384,4]{2,3,1,0:T(4,128)S(1)}, s32[1,1,384,4]{2,3,1,0:T(4,128)}, u32[]{:S(2)}) copy-start(s32[1,1,384,4]{2,3,1,0:T(4,128)} %param.17) | copy-start | bytes 18436
  11.2 18.8 %collective-permute-start.2 = (f32[66,8,128]{2,1,0:T(8,128)S(1)}, f32[66,8,128]{2,1,0:T(8,128)S(1)}, u32[]{:S(2)}, u32[]{:S(2)}) collective-permute-start(f32[66,8,128]{2,1,0:T(8,128)S(1)} %get-tuple-element.27), channel_id=1, source_target_pairs={{0,16},{32,48},{64,80},{96,112},{128,144},{160,176},{192,208},{224... | collective-permute-start | bytes 811016 | tf_op jit(solution)/shard_map/ppermute | solution.py:377
  13.9 21.3 %collective-permute-start.3 = (f32[66,8,128]{2,1,0:T(8,128)S(1)}, f32[66,8,128]{2,1,0:T(8,128)S(1)}, u32[]{:S(2)}, u32[]{:S(2)}) collective-permute-start(f32[66,8,128]{2,1,0:T(8,128)S(1)} %get-tuple-element.28), channel_id=1, source_target_pairs={{16,32},{48,64},{80,96},{112,128},{144,160},{176,192},{208,224},{2... | collective-permute-start | bytes 811016 | tf_op jit(solution)/shard_map/ppermute | solution.py:377
  35.1 0.7 copy-start.10
  35.8 41.2 %copy-start.1 = (f32[1,1,128,8,128]{4,3,2,1,0:T(8,128)S(1)}, f32[1,1,128,8,128]{4,3,2,1,0:T(8,128)}, u32[]{:S(2)}) copy-start(f32[1,1,128,8,128]{4,3,2,1,0:T(8,128)} %param.12) | copy-start | bytes 1572868
  50.0 8.8 %collective-permute-start.4 = (f32[20,8,128]{2,1,0:T(8,128)S(1)}, f32[20,8,128]{2,1,0:T(8,128)S(1)}, u32[]{:S(2)}, u32[]{:S(2)}) collective-permute-start(f32[20,8,128]{2,1,0:T(8,128)S(1)} %get-tuple-element.30), channel_id=1, source_target_pairs={{0,1},{2,3},{4,5},{6,7},{8,9},{10,11},{12,13},{14,15},{1,0},{3,2},... | collective-permute-start | bytes 245768 | tf_op jit(solution)/shard_map/ppermute | solution.py:377
  57.5 1.3 collective-permute-start.5
  58.9 18.1 %copy-start.11 = (s32[1,1,512,2]{2,3,1,0:T(2,128)S(1)}, s32[1,1,512,2]{2,3,1,0:T(2,128)}, u32[]{:S(2)}) copy-start(s32[1,1,512,2]{2,3,1,0:T(2,128)} %param.15) | copy-start | bytes 12292
  58.9 85.9 %collective-permute-start.6 = (f32[14,8,128]{2,1,0:T(8,128)S(1)}, f32[14,8,128]{2,1,0:T(8,128)S(1)}, u32[]{:S(2)}, u32[]{:S(2)}) collective-permute-start(f32[14,8,128]{2,1,0:T(8,128)S(1)} %get-tuple-element.33), channel_id=1, source_target_pairs={{0,16},{32,48},{64,80},{96,112},{128,144},{160,176},{192,208},{224... | collective-permute-start | bytes 172040 | tf_op jit(solution)/shard_map/ppermute | solution.py:377
  60.8 84.0 %collective-permute-start.7 = (f32[14,8,128]{2,1,0:T(8,128)S(1)}, f32[14,8,128]{2,1,0:T(8,128)S(1)}, u32[]{:S(2)}, u32[]{:S(2)}) collective-permute-start(f32[14,8,128]{2,1,0:T(8,128)S(1)} %get-tuple-element.34.after), channel_id=1, source_target_pairs={{16,32},{48,64},{80,96},{112,128},{144,160},{176,192},{208,224},{2... | collective-permute-start | bytes 172040 | tf_op jit(solution)/shard_map/ppermute | solution.py:377

commit v2 on v1

--- a/solution.py
+++ b/solution.py
@@ -15,11 +15,16 @@
 PAIRS = (SLOTS - MOVERS) // 2
 GROUP = MOVERS + PAIRS
 OWNABLE = NB + 4 * MOVERS
-POOL_TILES = NB + 4 * GROUP
+POOL = 384
+MAXT = 512
 ITERS = 4
+CONTACT_UNROLL = 32
+PREPARE = 4
+COUPLE_UNROLL = 32
 
 VM = pl.BlockSpec(memory_space=pltpu.VMEM)
 SM = pl.BlockSpec(memory_space=pltpu.SMEM)
+HB = pl.BlockSpec(memory_space=pltpu.HBM)
 PARAMS = pltpu.CompilerParams(vmem_limit_bytes=32 * 2**20)
 
 
@@ -27,13 +32,14 @@
     return jax.ShapeDtypeStruct(dims, F32)
 
 
-def call(kernel, outs, in_specs, scratch=(), flops=10**6, moved=10**6):
+def call(kernel, outs, in_specs, scratch=(), flops=10**6, moved=10**6, aliases=None):
     return pl.pallas_call(
         kernel,
         out_shape=outs,
         in_specs=in_specs,
         out_specs=jax.tree.map(lambda _: VM, outs),
         scratch_shapes=list(scratch),
+        input_output_aliases=aliases or {},
         compiler_params=PARAMS,
         cost_estimate=pl.CostEstimate(flops=flops, bytes_accessed=moved, transcendentals=0),
     )
@@ -47,8 +53,25 @@
         out[MOVERS + k, 4:8, :] = parts[sends[direction, MOVERS + PAIRS + k], 0:4, :]
 
 
-def pack_y(parts, sends, flow, pres, screen, source, solid, out_e, out_o, gain_ref, rest_ref):
+def fetch(sources, targets, sems):
+    copies = [pltpu.make_async_copy(a, b, sems.at[n]) for n, (a, b) in enumerate(zip(sources, targets, strict=True))]
+    for copy in copies:
+        copy.start()
+    return copies
+
+
+def pack_y(
+    parts_in, sends_in, flow_in, pres_in, screen_in, source_in, solid_in, slots_in,
+    out_e, out_o, gain_ref, rest_ref, parts, flow, pres, slots,
+    sends, screen, source, solid, sems,
+):
     parity = lax.axis_index("gy") % 2
+    for copy in fetch(
+        (sends_in, parts_in, flow_in, pres_in, screen_in, source_in, solid_in, slots_in),
+        (sends, parts, flow, pres, screen, source, solid, slots),
+        sems,
+    ):
+        copy.wait()
     gain_ref[...] = 1.0 / (6.0 + screen[...])
     rest_ref[...] = source[...] - 2.0 * solid[...]
     for out, up in ((out_e, parity == 0), (out_o, parity == 1)):
@@ -68,7 +91,7 @@
 
 
 def pack_x(
-    parts, sends, flow, pres, gain, rest, in_e, in_o, out_e, out_o, flow_x, pres_x, gain_x, rest_x
+    parts, sends, flow, pres, gain, rest, in_e, in_o, out_o, out_e, flow_x, pres_x, gain_x, rest_x
 ):
     parity = lax.axis_index("gy") % 2
     even = parity == 0
@@ -106,10 +129,11 @@
 
 
 def couple(
-    parts, sends, moves, tiles, slots, flow_x, in_xe, in_xo, in_ye, in_yo,
+    parts, sends_in, moves_in, tiles_in, slots, flow_x, in_xe, in_xo, in_ye, in_yo, after,
     drag, dep, out_e, out_o,
-    pool, table, sums, owned,
+    pool, table, sums, owned, sends, moves, tiles, sems,
 ):
+    copies = fetch((sends_in, moves_in, tiles_in), (sends, moves, tiles), sems)
     x_even = lax.axis_index("gx") % 2 == 0
     y_even = lax.axis_index("gy") % 2 == 0
     pool[0:NB] = parts[...]
@@ -119,20 +143,6 @@
         first, second = (b, a) if up == 0 else (a, b)
         pool[NB + d * MOVERS : NB + (d + 1) * MOVERS] = jnp.where(even, first[0:MOVERS], second[0:MOVERS])
 
-    def stay(k, carry):
-        owned[k] = 1.0
-        return carry
-
-    lax.fori_loop(0, NB, stay, 0)
-    for d in range(4):
-
-        def leave(s, carry, d=d):
-            owned[sends[d, s]] = 0.0
-            return carry
-
-        lax.fori_loop(0, moves[0, d], leave, 0)
-        for s in range(MOVERS):
-            owned[NB + d * MOVERS + s] = jnp.where(s < moves[1, d], 1.0, 0.0)
     for c in range(3):
         high = jnp.where(x_even, in_xe[GROUP + 2 * c], in_xo[GROUP + 2 * c])
         high2 = jnp.where(x_even, in_xe[GROUP + 2 * c + 1], in_xo[GROUP + 2 * c + 1])
@@ -149,6 +159,23 @@
             table[x * 10 + 5 : x * 10 + 10, 4 + c, :] = two[0:5]
     sums[...] = jnp.zeros_like(sums)
     drag[...] = jnp.zeros_like(drag)
+    for copy in copies:
+        copy.wait()
+
+    def stay(k, carry):
+        owned[k] = 1.0
+        return carry
+
+    lax.fori_loop(0, NB, stay, 0)
+    for d in range(4):
+
+        def leave(s, carry, d=d):
+            owned[sends[d, s]] = 0.0
+            return carry
+
+        lax.fori_loop(0, moves[0, d], leave, 0)
+        for s in range(MOVERS):
+            owned[NB + d * MOVERS + s] = jnp.where(s < moves[1, d], 1.0, 0.0)
 
     row = lax.broadcasted_iota(jnp.int32, (8, NB), 0)
     low_rows = row < 4
@@ -197,15 +224,15 @@
 
     def blocks(g, carry):
         made = []
-        for u in range(4):
-            m = g * 4 + u
+        for u in range(COUPLE_UNROLL):
+            m = g * COUPLE_UNROLL + u
             at = jnp.where(m < NB, m, NB + ((m - NB) // MOVERS) * SLOTS + (m - NB) % MOVERS)
             made.append(one_block(m, at))
         for columns, pieces in made:
             add(columns, pieces)
         return carry
 
-    lax.fori_loop(0, OWNABLE // 4, blocks, 0)
+    lax.fori_loop(0, OWNABLE // COUPLE_UNROLL, blocks, 0)
     dep[...] = jnp.zeros_like(dep)
     for n in range(100):
         total = sums[n]
@@ -220,7 +247,7 @@
                 out[i // 2, r : r + 4, :] = jnp.where(up, dep[f, x, 9:13, :], dep[f, x, 3:7, :])
 
 
-def fold_y(dep, in_e, in_o, dep_x, out_e, out_o):
+def fold_y(dep, in_e, in_o, dep_x, out_o, out_e):
     even = lax.axis_index("gy") % 2 == 0
     dep_x[...] = dep[...]
     for f in range(4):
@@ -308,63 +335,182 @@
     pressure[...] = source[4:12, 4:12, :]
 
 
-def contact(pairs, count, parts, in_xe, in_xo, in_ye, in_yo, drag, after, force, pool):
+def head(v):
+    return v.astype(BF16).astype(F32)
+
+def preparers(left, near, right):
+    row = lax.broadcasted_iota(jnp.int32, (8, 128), 0)
+    first_four = row < 4
+    space = row < 3
+    bias = jnp.where(space, 1.5, 0.0)
+    sign = jnp.where(row == 7, 1.0, jnp.where(first_four, 0.0, -1.0))
+    turned_sign = jnp.where(space, -1.0, jnp.where(row == 3, 1.0, 0.0))
+    last = jnp.where(row == 7, 1.0, 0.0)
+
+    def left_of(tile, m):
+        centred = tile - bias
+        v = jnp.where(first_four, centred, pltpu.roll(centred * centred, 4, 0))
+        h = head(v)
+        rest = v - h
+        mid = head(rest)
+        low = rest - mid
+        extra = jnp.where(space, 1.0, jnp.where(first_four, 0.0, low))
+        shifted = jnp.where(first_four, 1.0, jnp.where(row == 7, 0.0, pltpu.roll(mid, 4, 0)))
+        near[m] = jnp.concatenate([jnp.where(space, h, shifted), jnp.where(space, low, 0.0)], axis=0).astype(BF16)
+        return [h, h, mid, extra]
+
+    def right_of(tile, n):
+        centred = tile - bias
+        square = jnp.where(first_four, centred * centred, 0.0)
+        t = jnp.broadcast_to(jnp.sum(square * turned_sign, axis=0, keepdims=True), (8, 128))
+        r2 = jnp.broadcast_to(square[3:4], (8, 128))
+        d = jnp.where(first_four, 2.0 * centred, sign)
+        h = head(d)
+        mid = head(d - h)
+
+        def terms(v):
+            a = head(v)
+            b = head(v - a)
+            return a, b, v - a - b
+
+        ta, tb, tc = terms(t)
+        ra, rb, rc = terms(r2)
+        fourth = jnp.where(row == 0, ta, jnp.where(row == 1, tb, jnp.where(row == 2, tc, sign)))
+        reach = jnp.where(row == 3, h, last)
+        reach_mid = jnp.where(row == 3, mid, 0.0)
+        fourth_reach = jnp.where(row == 0, ra, jnp.where(row == 1, rb, jnp.where(row == 2, rc, last)))
+        right[n, :, 0:128] = jnp.concatenate([h, mid, h, fourth], axis=0).astype(BF16)
+        right[n, :, 128:256] = jnp.concatenate([reach, reach_mid, reach, fourth_reach], axis=0).astype(BF16)
+
+    def four(tiles, m):
+        rows = []
+        for b, tile in enumerate(tiles):
+            rows += left_of(tile, m + b)
+        left[m // 4] = jnp.concatenate(rows, axis=0).astype(BF16).T
+
+    return four, right_of
+
+
+def lister(pairs, total, chosen, wanted_own):
+    def look(first, count, size):
+        for v in range(size):
+            t = first + v
+            own = jnp.maximum(pairs[0, t], pairs[1, t]) < NB
+            wanted = own if wanted_own else jnp.logical_not(own)
+            chosen[count] = t
+            count = count + jnp.where(wanted & (t < total), 1, 0)
+        return count
+
+    return look
+
+
+def run_tiles(pairs, chosen, count, left, near, right, sums):
+    def tile(n):
+        t = chosen[jnp.minimum(n, count - 1)]
+        i = pairs[0, t]
+        j = pairs[1, t]
+        q = i - NB
+        i = jnp.where(i < NB, i, NB + (q // SLOTS) * MOVERS + q % SLOTS)
+        mine = right[i]
+        place = j % 4
+        none = jnp.zeros_like(mine)
+        weights = jnp.concatenate([jnp.where(place == k, mine, none) for k in range(4)], axis=0)
+        both = jnp.dot(left[j // 4], weights, preferred_element_type=F32)
+        overlap = jnp.maximum(both[:, :128], 0.0)
+        reach = both[:, 128:]
+        guess = pl.reciprocal(reach, approx=True)
+        weight = overlap * (guess * (2.0 - reach * guess))
+        upper = weight.astype(BF16)
+        lower = (weight - upper.astype(F32)).astype(BF16)
+        a = near[j]
+        got = jnp.dot(a, upper, preferred_element_type=F32) + jnp.dot(a, lower, preferred_element_type=F32)
+        got = got[0:8] + pltpu.roll(got[0:8], 4, 0) + got[8:16]
+        return i, got * jnp.where(n < count, 1.0, 0.0)
+
+    def step(g, carry):
+        made = [tile(g * CONTACT_UNROLL + u) for u in range(CONTACT_UNROLL)]
+        for i, got in made:
+            sums[i] += got
+        return carry
+
+    lax.fori_loop(0, (count + CONTACT_UNROLL - 1) // CONTACT_UNROLL, step, 0)
+
+
+def contact_own(pairs, total_ref, parts, after, left, near, right, sums, chosen):
+    total = total_ref[0, 0]
+    sums[...] = jnp.zeros_like(sums)
+    four, right_of = preparers(left, near, right)
+    look = lister(pairs, total, chosen, True)
+    groups = NB // 4 // PREPARE
+
+    def own(k, count):
+        for u in range(PREPARE):
+            m = 4 * (k * PREPARE + u)
+            tiles = [parts[m + b] for b in range(4)]
+            four(tiles, m)
+            for b in range(4):
+                right_of(tiles[b], m + b)
+        return look(k * (MAXT // groups), count, MAXT // groups)
+
+    count = lax.fori_loop(0, groups, own, 0)
+    run_tiles(pairs, chosen, count, left, near, right, sums)
+
+
+def contact_rest(
+    pairs, total_ref, parts, in_xe, in_xo, in_ye, in_yo, drag, after, left_in, near_in, right_in, sums_in,
+    force, left, near, right, sums, chosen,
+):
     x_even = lax.axis_index("gx") % 2 == 0
     y_even = lax.axis_index("gy") % 2 == 0
-    pool[0 : NB * 8] = parts[...].reshape(NB * 8, 128)
-    for d, (up, even, a, b) in enumerate(
-        ((0, x_even, in_xe, in_xo), (1, x_even, in_xe, in_xo), (0, y_even, in_ye, in_yo), (1, y_even, in_ye, in_yo))
-    ):
+    total = total_ref[0, 0]
+    four, right_of = preparers(left, near, right)
+    look = lister(pairs, total, chosen, False)
+    groups = (
+        (0, x_even, in_xe, in_xo), (1, x_even, in_xe, in_xo), (0, y_even, in_ye, in_yo), (1, y_even, in_ye, in_yo)
+    )
+    count = jnp.int32(0)
+    part = MAXT // 16
+    for d, (up, even, a, b) in enumerate(groups):
         first, second = (b, a) if up == 0 else (a, b)
-        at = (NB + d * GROUP) * 8
-        pool[at : at + GROUP * 8] = jnp.where(even, first[0:GROUP], second[0:GROUP]).reshape(GROUP * 8, 128)
-    force[...] = drag[...]
-    total = count[0, 0]
-
-    def row_of(m):
-        q = m - NB
-        d = q // SLOTS
-        s = q % SLOTS
-        base = (NB + d * GROUP) * 8
-        tail = jnp.where(
-            s < MOVERS + PAIRS, 8 * s, 8 * (s - PAIRS) + 4
-        )
-        return jnp.where(m < NB, 8 * m, base + tail)
-
-    def tile(t):
-        i = pairs[0, t]
-        j = pairs[1, t]
-        x = pool[pl.ds(pl.multiple_of(row_of(i), 4), 4), :]
-        y = pool[pl.ds(pl.multiple_of(row_of(j), 4), 4), :]
-        xs = [jnp.broadcast_to(x[c : c + 1], (8, 128)) for c in range(4)]
-        ys = [
-            pltpu.roll(jnp.broadcast_to(y[c : c + 1], (8, 128)), 0, 1, stride=1, stride_axis=0)
-            for c in range(4)
-        ]
-        sums = [jnp.zeros((8, 128), F32) for _ in range(3)]
-        for step in range(16):
-            turned = ys if step == 0 else [pltpu.roll(v, 8 * step, 1) for v in ys]
-            apart = [xs[c] - turned[c] for c in range(3)]
-            distance = apart[0] * apart[0] + apart[1] * apart[1] + apart[2] * apart[2]
-            reach = xs[3] + turned[3]
-            reach = reach * reach
-            guess = pl.reciprocal(reach, approx=True)
-            inverse = guess * (2.0 - reach * guess)
-            weight = jnp.maximum(1.0 - distance * inverse, 0.0)
-            sums = [s + weight * a for s, a in zip(sums, apart, strict=True)]
-        scale = jnp.where(t < total, 0.5, 0.0)
-        return i, [jnp.sum(s, axis=0, keepdims=True) * scale for s in sums]
-
-    unroll = 4
-
-    def step(g, carry):
-        made = [tile(g * unroll + u) for u in range(unroll)]
-        for i, sums in made:
-            for c in range(3):
-                force[c, pl.ds(i, 1), :] += sums[c]
-        return carry
-
-    lax.fori_loop(0, (total + unroll - 1) // unroll, step, 0)
+        for u in range(MOVERS // 4):
+            tiles = [jnp.where(even, first[4 * u + b], second[4 * u + b]) for b in range(4)]
+            four(tiles, NB + d * SLOTS + 4 * u)
+            for b in range(4):
+                right_of(tiles[b], NB + d * MOVERS + 4 * u + b)
+        count = look(d * 4 * part, count, part)
+
+        def others(k, count, d=d, even=even, first=first, second=second):
+            for u in range(2):
+                s = MOVERS + 8 * k + 4 * u
+                tiles = [jnp.where(even, first[s + b], second[s + b]) for b in range(4)]
+                four(tiles, NB + d * SLOTS + s)
+                four([pltpu.roll(tile, 4, 0) for tile in tiles], NB + d * SLOTS + s + PAIRS)
+            return look((d * 4 + 1 + k) * part, count, part)
+
+        count = lax.fori_loop(0, PAIRS // 8, others, count)
+    run_tiles(pairs, chosen, count, left, near, right, sums)
+
+    def put(n, at, position):
+        for c in range(3):
+            x = position(c) - 1.5
+            w = sums[8 * n : 8 * n + 8, 3, :]
+            y = sums[8 * n : 8 * n + 8, c, :]
+            force[c, at : at + 8, :] = drag[c, at : at + 8, :] + 0.5 * (x * w - y)
+
+    for n in range(NB // 8):
+        put(n, 8 * n, lambda c, n=n: parts[8 * n : 8 * n + 8, c, :])
+    for d, (up, even, a, b) in enumerate(groups):
+        first, second = (b, a) if up == 0 else (a, b)
+        for k in range(2):
+            put(
+                NB // 8 + 2 * d + k,
+                NB + d * SLOTS + 8 * k,
+                lambda c, k=k, even=even, first=first, second=second: jnp.where(
+                    even, first[8 * k : 8 * k + 8, c, :], second[8 * k : 8 * k + 8, c, :]
+                ),
+            )
+        for c in range(3):
+            force[c, NB + d * SLOTS + MOVERS : NB + (d + 1) * SLOTS, :] = jnp.zeros((SLOTS - MOVERS, 128), F32)
 
 
 def pairs_of(first, count, last):
@@ -391,51 +537,75 @@
     solid_old,
     screening,
 ):
-    parts = particles[0, 0]
     sends = send_list[0, 0]
     moves = move_count[0, 0]
     tiles = drag_tiles[0, 0].T
     pairs = tile_pairs[0, 0].T
-    slots = cell_slot[0, 0]
     cells = (8, 8, 128)
     wide = (8, 16, 128)
-    ye, yo, gain, rest = call(
-        pack_y, (shape(Y_TILES, 8, 128), shape(Y_TILES, 8, 128), shape(*cells), shape(*cells)), [VM, SM] + [VM] * 5
-    )(parts, sends, fluid_velocity, pressure_init, screening, source, solid_old)
+    ye, yo, gain, rest, parts, flow, pres, slots = call(
+        pack_y,
+        (
+            shape(Y_TILES, 8, 128), shape(Y_TILES, 8, 128), shape(*cells), shape(*cells),
+            shape(NB, 8, 128), shape(3, *cells), shape(*cells), jax.ShapeDtypeStruct((384, 128), jnp.int32),
+        ),
+        [HB] * 8,
+        [
+            pltpu.SMEM((4, SLOTS), jnp.int32),
+            pltpu.VMEM(cells, F32),
+            pltpu.VMEM(cells, F32),
+            pltpu.VMEM(cells, F32),
+            pltpu.SemaphoreType.DMA((8,)),
+        ],
+    )(particles[0, 0], sends, fluid_velocity, pressure_init, screening, source, solid_old, cell_slot[0, 0])
     got_ye = swap(ye, "gy", 0)
     got_yo = swap(yo, "gy", 1)
-    xe, xo, flow_x, pres_x, gain_x, rest_x = call(
+    xo, xe, flow_x, pres_x, gain_x, rest_x = call(
         pack_x,
         (shape(X_TILES, 8, 128), shape(X_TILES, 8, 128), shape(3, *wide), shape(*wide), shape(*wide), shape(*wide)),
         [VM, SM] + [VM] * 6,
-    )(parts, sends, fluid_velocity, pressure_init, gain, rest, got_ye, got_yo)
+    )(parts, sends, flow, pres, gain, rest, got_ye, got_yo)
+    got_xe = swap(xe, "gx", 0)
     got_xo = swap(xo, "gx", 1)
-    got_xe = swap(xe, "gx", 0)
+    operands = (
+        jax.ShapeDtypeStruct((POOL // 4, 128, 128), BF16),
+        jax.ShapeDtypeStruct((POOL, 16, 128), BF16),
+        jax.ShapeDtypeStruct((OWNABLE, 32, 256), BF16),
+        shape(OWNABLE, 8, 128),
+    )
+    prepared = call(
+        contact_own, operands, [SM, SM, VM, VM], [pltpu.SMEM((MAXT + 1,), jnp.int32)], flops=10**8
+    )(pairs, tile_count, parts, xo)
     drag, dep, de, do = call(
         couple,
         (shape(3, 384, 128), shape(4, 10, 16, 128), shape(20, 8, 128), shape(20, 8, 128)),
-        [VM, SM, SM, SM] + [VM] * 6,
+        [VM, HB, HB, HB] + [VM] * 7,
         [
             pltpu.VMEM((OWNABLE, 8, 128), F32),
             pltpu.VMEM((100, 8, 128), F32),
             pltpu.VMEM((100, 8, 128), F32),
             pltpu.SMEM((OWNABLE,), F32),
+            pltpu.SMEM((4, SLOTS), jnp.int32),
+            pltpu.SMEM((2, 4), jnp.int32),
+            pltpu.SMEM((4, 384), jnp.int32),
+            pltpu.SemaphoreType.DMA((3,)),
         ],
-    )(parts, sends, moves, tiles, slots, flow_x, got_xe, got_xo, got_ye, got_yo)
+    )(parts, sends, moves, tiles, slots, flow_x, got_xe, got_xo, got_ye, got_yo, prepared[3])
     got_de = swap(de, "gy", 0)
     got_do = swap(do, "gy", 1)
-    dep_x, fe, fo = call(
+    dep_x, fo, fe = call(
         fold_y, (shape(4, 10, 16, 128), shape(D_TILES, 8, 128), shape(D_TILES, 8, 128)), [VM] * 3
     )(dep, got_de, got_do)
+    got_fe = swap(fe, "gx", 0)
     got_fo = swap(fo, "gx", 1)
-    got_fe = swap(fe, "gx", 0)
     force = call(
-        contact,
-        shape(3, 384, 128),
-        [SM, SM] + [VM] * 7,
-        [pltpu.VMEM((POOL_TILES * 8, 128), F32)],
+        contact_rest,
+        (shape(3, 384, 128), *operands),
+        [SM, SM] + [VM] * 11,
+        [pltpu.SMEM((MAXT + 1,), jnp.int32)],
         flops=10**9,
-    )(pairs, tile_count, parts, got_xe, got_xo, got_ye, got_yo, drag, fo)
+        aliases={9: 1, 10: 2, 11: 3, 12: 4},
+    )(pairs, tile_count, parts, got_xe, got_xo, got_ye, got_yo, drag, fo, *prepared)[0]
     pressure, drag_sum = call(
         finish,
         (shape(*cells), shape(3, *cells)),

time: 147 us -> 108 us (0.73)
  the two profiles are of different devices: /device:TPU:30 before, /device:TPU:31 now
where the time goes in v2:
time: 108 us; the launch traced here: 107 us
  starting transfers between devices  60.2 us (56%)
  Pallas kernels  30.4 us (28%)
  local copies, waits for them, and re-layouts  8.62 us (8%)
  waiting for transfers between devices  6.26 us (6%)
  between operations  1.46 us (1%)
    ppermute x8, starting transfers between devices, swap(): return lax.ppermute(array, axis, pairs_of(first, count, count - 1))  60.2 us
    pallas_call x1, Pallas kernels, body(): call(contact_rest, (shape(3, 384, 128), *operands), [SM, SM] + [VM] * 11,...  14 us
    unnamed x24, local copies, waits for them, and re-layouts  8.62 us
    pallas_call x1, Pallas kernels, body(): call(contact_own, operands, [SM, SM, VM, VM], [pltpu.SMEM((MAXT + 1,), jn...  7.12 us
    pallas_call x1, Pallas kernels, body(): call(couple, (shape(3, 384, 128), shape(4, 10, 16, 128), shape(20, 8, 128...  6.57 us
    ppermute x8, waiting for transfers between devices, swap(): return lax.ppermute(array, axis, pairs_of(first, count, count - 1))  6.26 us
  transfers between devices with their start and end apart: 8, of which 2 were waited for; matrix products, arithmetic and copies ran while one was open for 0% of the time, Pallas kernels for 20%

profile of v2, /device:TPU:31, one launch (start us, length us, event | category | flops | bytes accessed | tf_op | source)
XLA Modules:
  0.0 107.0 jit_solution(6039005845176067253)
XLA Ops:
  0.6 0.0 copy-start.9
  0.6 0.0 copy-start
  0.7 1.0 copy-done
  1.7 0.0 copy-start.1
  1.7 0.9 copy-done.1
  2.6 0.0 copy-start.2
  2.6 0.9 copy-done.2
  3.5 0.0 copy-start.3
  3.5 0.8 copy-done.3
  4.3 0.0 copy-start.4
  4.3 0.8 copy-done.4
  5.0 0.0 copy-start.5
  5.0 0.8 copy-done.5
  5.8 0.0 copy-start.6
  5.8 0.8 copy-done.6
  6.5 0.0 copy-start.7
  6.5 0.7 copy-done.7
  7.2 0.8 shard_map.139
  8.1 2.6 %collective-permute-start = (f32[55,8,128]{2,1,0:T(8,128)S(1)}, f32[55,8,128]{2,1,0:T(8,128)S(1)}, u32[]{:S(2)}, u32[]{:S(2)}) collective-permute-start(f32[55,8,128]{2,1,0:T(8,128)S(1)} %get-tuple-element.37), channel_id=1, source_target_pairs={{0,1},{2,3},{4,5},{6,7},{8,9},{10,11},{12,13},{14,15},{1,0},{3,2},... | collective-permute-start | bytes 675848 | tf_op jit(solution)/shard_map/ppermute | solution.py:523
  10.7 3.4 %collective-permute-start.1 = (f32[55,8,128]{2,1,0:T(8,128)S(1)}, f32[55,8,128]{2,1,0:T(8,128)S(1)}, u32[]{:S(2)}, u32[]{:S(2)}) collective-permute-start(f32[55,8,128]{2,1,0:T(8,128)S(1)} %get-tuple-element.38), channel_id=1, source_target_pairs={{1,2},{3,4},{5,6},{7,8},{9,10},{11,12},{13,14},{2,1},{4,3},{6,5},{... | collective-permute-start | bytes 675848 | tf_op jit(solution)/shard_map/ppermute | solution.py:523
  14.1 0.0 collective-permute-done.in_e.in_ye
  14.1 4.1 %collective-permute-done.1.in_o.in_yo = f32[55,8,128]{2,1,0:T(8,128)S(1)} collective-permute-done((f32[55,8,128]{2,1,0:T(8,128)S(1)}, f32[55,8,128]{2,1,0:T(8,128)S(1)}, u32[]{:S(2)}, u32[]{:S(2)}) %collective-permute-start.1) | collective-permute-done | bytes 225312 | tf_op jit(solution)/shard_map/ppermute | solution.py:523
  18.3 0.8 shard_map.140
  19.0 2.4 %collective-permute-start.2 = (f32[66,8,128]{2,1,0:T(8,128)S(1)}, f32[66,8,128]{2,1,0:T(8,128)S(1)}, u32[]{:S(2)}, u32[]{:S(2)}) collective-permute-start(f32[66,8,128]{2,1,0:T(8,128)S(1)} %get-tuple-element.40), channel_id=1, source_target_pairs={{0,16},{32,48},{64,80},{96,112},{128,144},{160,176},{192,208},{224... | collective-permute-start | bytes 811016 | tf_op jit(solution)/shard_map/ppermute | solution.py:523
  21.4 15.8 %collective-permute-start.3 = (f32[66,8,128]{2,1,0:T(8,128)S(1)}, f32[66,8,128]{2,1,0:T(8,128)S(1)}, u32[]{:S(2)}, u32[]{:S(2)}) collective-permute-start(f32[66,8,128]{2,1,0:T(8,128)S(1)} %get-tuple-element.41.after), channel_id=1, source_target_pairs={{16,32},{48,64},{80,96},{112,128},{144,160},{176,192},{208,224},{2... | collective-permute-start | bytes 811016 | tf_op jit(solution)/shard_map/ppermute | solution.py:523
  37.9 0.0 copy-start.8
  37.9 0.7 copy-done.8
  38.6 7.1 %shard_map.141 = (bf16[96,128,128]{2,1,0:T(8,128)(2,1)S(1)}, bf16[384,16,128]{2,1,0:T(8,128)(2,1)S(1)}, bf16[192,32,256]{2,1,0:T(8,128)(2,1)S(1)}, f32[192,8,128]{2,1,0:T(8,128)S(1)}) custom-call(s32[2,512]{1,0:T(2,128)S(1)} %bitcast.18, s32[1,1]{1,0:T(1,128)S(6)} %copy.23.total_ref, f32[128,8,128]{2,1,0:T(8,128)S(1)} %get-tuple-element.31.parts, ...), custom_call_target="tpu_custom_call" | custom-call | flops 100000000 | bytes 1000000 | tf_op jit(solution)/shard_map/pallas_call | solution.py:576
  45.7 0.0 collective-permute-done.2.in_xe.near_e
  45.7 0.0 collective-permute-done.3.in_xo.near_o
  45.7 0.0 copy-start.10
  45.8 0.7 copy-done.10
  46.4 0.0 copy-start.11
  46.4 0.7 copy-done.11
  47.1 6.6 %shard_map.142 = (f32[3,384,128]{2,1,0:T(8,128)S(1)}, f32[4,10,16,128]{3,2,1,0:T(8,128)S(1)}, f32[20,8,128]{2,1,0:T(8,128)S(1)}, f32[20,8,128]{2,1,0:T(8,128)S(1)}) custom-call(f32[128,8,128]{2,1,0:T(8,128)S(1)} %get-tuple-element.31.parts, s32[4,64]{1,0:T(4,128)S(1)} %bitcast.17, s32[2,4]{1,0:T(2,128)S(1)} %bitcast.21, s32[4,384]{1,0:T(4,128)S(1)} %bitcast.20, ...), custom_call_target="tpu_custom_call" | custom-call | flops 1000000 | bytes 1000000 | tf_op jit(solution)/shard_map/pallas_call | solution.py:579
  53.7 1.9 %collective-permute-start.4 = (f32[20,8,128]{2,1,0:T(8,128)S(1)}, f32[20,8,128]{2,1,0:T(8,128)S(1)}, u32[]{:S(2)}, u32[]{:S(2)}) collective-permute-start(f32[20,8,128]{2,1,0:T(8,128)S(1)} %get-tuple-element.44), channel_id=1, source_target_pairs={{0,1},{2,3},{4,5},{6,7},{8,9},{10,11},{12,13},{14,15},{1,0},{3,2},... | collective-permute-start | bytes 245768 | tf_op jit(solution)/shard_map/ppermute | solution.py:523
  55.6 20.1 %collective-permute-start.5 = (f32[20,8,128]{2,1,0:T(8,128)S(1)}, f32[20,8,128]{2,1,0:T(8,128)S(1)}, u32[]{:S(2)}, u32[]{:S(2)}) collective-permute-start(f32[20,8,128]{2,1,0:T(8,128)S(1)} %get-tuple-element.45), channel_id=1, source_target_pairs={{1,2},{3,4},{5,6},{7,8},{9,10},{11,12},{13,14},{2,1},{4,3},{6,5},{... | collective-permute-start | bytes 245768 | tf_op jit(solution)/shard_map/ppermute | solution.py:523
  75.7 0.0 collective-permute-done.4.in_e
  75.7 2.1 %collective-permute-done.5.in_o = f32[20,8,128]{2,1,0:T(8,128)S(1)} collective-permute-done((f32[20,8,128]{2,1,0:T(8,128)S(1)}, f32[20,8,128]{2,1,0:T(8,128)S(1)}, u32[]{:S(2)}, u32[]{:S(2)}) %collective-permute-start.5) | collective-permute-done | bytes 81952 | tf_op jit(solution)/shard_map/ppermute | solution.py:523
  77.8 0.1 shard_map.143
  77.9 1.9 %collective-permute-start.6 = (f32[14,8,128]{2,1,0:T(8,128)S(1)}, f32[14,8,128]{2,1,0:T(8,128)S(1)}, u32[]{:S(2)}, u32[]{:S(2)}) collective-permute-start(f32[14,8,128]{2,1,0:T(8,128)S(1)} %get-tuple-element.47), channel_id=1, source_target_pairs={{0,16},{32,48},{64,80},{96,112},{128,144},{160,176},{192,208},{224... | collective-permute-start | bytes 172040 | tf_op jit(solution)/shard_map/ppermute | solution.py:523
  79.8 12.1 %collective-permute-start.7 = (f32[14,8,128]{2,1,0:T(8,128)S(1)}, f32[14,8,128]{2,1,0:T(8,128)S(1)}, u32[]{:S(2)}, u32[]{:S(2)}) collective-permute-start(f32[14,8,128]{2,1,0:T(8,128)S(1)} %get-tuple-element.48.after), channel_id=1, source_target_pairs={{16,32},{48,64},{80,96},{112,128},{144,160},{176,192},{208,224},{2... | collective-permute-start | bytes 172040 | tf_op jit(solution)/shard_map/ppermute | solution.py:523
  91.9 0.0 copy-done.9
  91.9 14.0 %shard_map.145 = (f32[3,384,128]{2,1,0:T(8,128)}, bf16[96,128,128]{2,1,0:T(8,128)(2,1)S(1)}, bf16[384,16,128]{2,1,0:T(8,128)(2,1)S(1)}, bf16[192,32,256]{2,1,0:T(8,128)(2,1)S(1)}, f32[192,8,128]{2,1,0:T(8,128)S(1)}) custom-call(s32[2,512]{1,0:T(2,128)S(1)} %bitcast.19, ...), custom_call_target="tpu_custom_call", output_to_operand_aliasing={{1}: (9, {}), {2}: (10, {}), {3}: (11, {}), {4}: (12, {})} | custom-call | flops 1000000000 | bytes 1000000 | tf_op jit(solution)/shard_map/pallas_call | solution.py:601
  105.9 0.0 collective-permute-done.6.in_e
  105.9 0.0 collective-permute-done.7.in_o
  105.9 1.0 shard_map.144
Async XLA Ops:
  0.6 91.3 %copy-start.9 = (s32[1,1,512,2]{2,3,1,0:T(2,128)S(1)}, s32[1,1,512,2]{2,3,1,0:T(2,128)}, u32[]{:S(2)}) copy-start(s32[1,1,512,2]{2,3,1,0:T(2,128)} %param.15) | copy-start | bytes 12292
  0.6 1.0 copy-start
  1.7 0.9 copy-start.1
  2.6 0.9 copy-start.2
  3.5 0.8 copy-start.3
  4.3 0.8 copy-start.4
  5.0 0.8 copy-start.5
  5.8 0.8 copy-start.6
  6.5 0.7 copy-start.7
  8.1 6.0 %collective-permute-start = (f32[55,8,128]{2,1,0:T(8,128)S(1)}, f32[55,8,128]{2,1,0:T(8,128)S(1)}, u32[]{:S(2)}, u32[]{:S(2)}) collective-permute-start(f32[55,8,128]{2,1,0:T(8,128)S(1)} %get-tuple-element.37), channel_id=1, source_target_pairs={{0,1},{2,3},{4,5},{6,7},{8,9},{10,11},{12,13},{14,15},{1,0},{3,2},... | collective-permute-start | bytes 675848 | tf_op jit(solution)/shard_map/ppermute | solution.py:523
  10.7 7.6 %collective-permute-start.1 = (f32[55,8,128]{2,1,0:T(8,128)S(1)}, f32[55,8,128]{2,1,0:T(8,128)S(1)}, u32[]{:S(2)}, u32[]{:S(2)}) collective-permute-start(f32[55,8,128]{2,1,0:T(8,128)S(1)} %get-tuple-element.38), channel_id=1, source_target_pairs={{1,2},{3,4},{5,6},{7,8},{9,10},{11,12},{13,14},{2,1},{4,3},{6,5},{... | collective-permute-start | bytes 675848 | tf_op jit(solution)/shard_map/ppermute | solution.py:523
  19.0 26.7 %collective-permute-start.2 = (f32[66,8,128]{2,1,0:T(8,128)S(1)}, f32[66,8,128]{2,1,0:T(8,128)S(1)}, u32[]{:S(2)}, u32[]{:S(2)}) collective-permute-start(f32[66,8,128]{2,1,0:T(8,128)S(1)} %get-tuple-element.40), channel_id=1, source_target_pairs={{0,16},{32,48},{64,80},{96,112},{128,144},{160,176},{192,208},{224... | collective-permute-start | bytes 811016 | tf_op jit(solution)/shard_map/ppermute | solution.py:523
  21.4 24.3 %collective-permute-start.3 = (f32[66,8,128]{2,1,0:T(8,128)S(1)}, f32[66,8,128]{2,1,0:T(8,128)S(1)}, u32[]{:S(2)}, u32[]{:S(2)}) collective-permute-start(f32[66,8,128]{2,1,0:T(8,128)S(1)} %get-tuple-element.41.after), channel_id=1, source_target_pairs={{16,32},{48,64},{80,96},{112,128},{144,160},{176,192},{208,224},{2... | collective-permute-start | bytes 811016 | tf_op jit(solution)/shard_map/ppermute | solution.py:523
  37.9 0.7 copy-start.8
  45.7 0.7 copy-start.10
  46.4 0.7 copy-start.11
  53.7 22.0 %collective-permute-start.4 = (f32[20,8,128]{2,1,0:T(8,128)S(1)}, f32[20,8,128]{2,1,0:T(8,128)S(1)}, u32[]{:S(2)}, u32[]{:S(2)}) collective-permute-start(f32[20,8,128]{2,1,0:T(8,128)S(1)} %get-tuple-element.44), channel_id=1, source_target_pairs={{0,1},{2,3},{4,5},{6,7},{8,9},{10,11},{12,13},{14,15},{1,0},{3,2},... | collective-permute-start | bytes 245768 | tf_op jit(solution)/shard_map/ppermute | solution.py:523
  55.6 22.2 %collective-permute-start.5 = (f32[20,8,128]{2,1,0:T(8,128)S(1)}, f32[20,8,128]{2,1,0:T(8,128)S(1)}, u32[]{:S(2)}, u32[]{:S(2)}) collective-permute-start(f32[20,8,128]{2,1,0:T(8,128)S(1)} %get-tuple-element.45), channel_id=1, source_target_pairs={{1,2},{3,4},{5,6},{7,8},{9,10},{11,12},{13,14},{2,1},{4,3},{6,5},{... | collective-permute-start | bytes 245768 | tf_op jit(solution)/shard_map/ppermute | solution.py:523
  77.9 28.0 %collective-permute-start.6 = (f32[14,8,128]{2,1,0:T(8,128)S(1)}, f32[14,8,128]{2,1,0:T(8,128)S(1)}, u32[]{:S(2)}, u32[]{:S(2)}) collective-permute-start(f32[14,8,128]{2,1,0:T(8,128)S(1)} %get-tuple-element.47), channel_id=1, source_target_pairs={{0,16},{32,48},{64,80},{96,112},{128,144},{160,176},{192,208},{224... | collective-permute-start | bytes 172040 | tf_op jit(solution)/shard_map/ppermute | solution.py:523
  79.8 26.1 %collective-permute-start.7 = (f32[14,8,128]{2,1,0:T(8,128)S(1)}, f32[14,8,128]{2,1,0:T(8,128)S(1)}, u32[]{:S(2)}, u32[]{:S(2)}) collective-permute-start(f32[14,8,128]{2,1,0:T(8,128)S(1)} %get-tuple-element.48.after), channel_id=1, source_target_pairs={{16,32},{48,64},{80,96},{112,128},{144,160},{176,192},{208,224},{2... | collective-permute-start | bytes 172040 | tf_op jit(solution)/shard_map/ppermute | solution.py:523

commit v3 on v2

--- a/solution.py
+++ b/solution.py
@@ -19,6 +19,9 @@
 MAXT = 512
 ITERS = 4
 CONTACT_UNROLL = 32
+EARLY = 96
+LIST = 640
+LAST = LIST - 1
 PREPARE = 4
 COUPLE_UNROLL = 32
 
@@ -37,7 +40,7 @@
         kernel,
         out_shape=outs,
         in_specs=in_specs,
-        out_specs=jax.tree.map(lambda _: VM, outs),
+        out_specs=jax.tree.map(lambda o: SM if len(o.shape) == 1 else VM, outs),
         scratch_shapes=list(scratch),
         input_output_aliases=aliases or {},
         compiler_params=PARAMS,
@@ -60,77 +63,48 @@
     return copies
 
 
-def pack_y(
-    parts_in, sends_in, flow_in, pres_in, screen_in, source_in, solid_in, slots_in,
-    out_e, out_o, gain_ref, rest_ref, parts, flow, pres, slots,
-    sends, screen, source, solid, sems,
-):
+Y_TILES = GROUP + 3
+X_TILES = GROUP + 6
+
+
+def pack_y(parts, sends, flow, out_e, out_o):
     parity = lax.axis_index("gy") % 2
-    for copy in fetch(
-        (sends_in, parts_in, flow_in, pres_in, screen_in, source_in, solid_in, slots_in),
-        (sends, parts, flow, pres, screen, source, solid, slots),
-        sems,
-    ):
-        copy.wait()
-    gain_ref[...] = 1.0 / (6.0 + screen[...])
-    rest_ref[...] = source[...] - 2.0 * solid[...]
     for out, up in ((out_e, parity == 0), (out_o, parity == 1)):
         put_blocks(parts, sends, jnp.where(up, 2, 3), out)
         for c in range(3):
             out[GROUP + c] = jnp.where(up, flow[c, :, 7, :], flow[c, :, 0, :])
-        at = GROUP + 3
-        for ref in (pres, gain_ref, rest_ref):
-            for x in range(8):
-                row = 4 * (x % 2)
-                out[at + x // 2, row : row + 4, :] = jnp.where(up, ref[x, 4:8, :], ref[x, 0:4, :])
-            at += 4
-
-
-Y_TILES = GROUP + 3 + 12
-X_TILES = GROUP + 6 + 8 + 6 + 6
-
-
-def pack_x(
-    parts, sends, flow, pres, gain, rest, in_e, in_o, out_o, out_e, flow_x, pres_x, gain_x, rest_x
-):
-    parity = lax.axis_index("gy") % 2
-    even = parity == 0
+
+
+def put_flow(flow_x, up, out):
+    edge = jnp.where(up, 7, 0)
+    for c in range(3):
+        out[GROUP + 2 * c] = flow_x[c, edge, 0:8, :]
+        out[GROUP + 2 * c + 1] = flow_x[c, edge, 8:16, :]
+
+
+def pack_first(parts, sends, flow, in_e, in_o, out, flow_x):
+    even = lax.axis_index("gy") % 2 == 0
     for c in range(3):
         flow_x[c, :, 4:12, :] = flow[c]
         a = in_e[GROUP + c]
         b = in_o[GROUP + c]
         flow_x[c, :, 12, :] = jnp.where(even, a, b)
         flow_x[c, :, 3, :] = jnp.where(even, b, a)
-    at = GROUP + 3
-    for wide, ref in ((pres_x, pres), (gain_x, gain), (rest_x, rest)):
-        wide[:, 4:12, :] = ref[...]
-        for x in range(8):
-            row = 4 * (x % 2)
-            a = in_e[at + x // 2, row : row + 4, :]
-            b = in_o[at + x // 2, row : row + 4, :]
-            wide[x, 12:16, :] = jnp.where(even, a, b)
-            wide[x, 0:4, :] = jnp.where(even, b, a)
-        at += 4
-    parity = lax.axis_index("gx") % 2
-    for out, up in ((out_e, parity == 0), (out_o, parity == 1)):
-        put_blocks(parts, sends, jnp.where(up, 0, 1), out)
-        at = GROUP
-        for c in range(3):
-            edge = jnp.where(up, 7, 0)
-            out[at] = flow_x[c, edge, 0:8, :]
-            out[at + 1] = flow_x[c, edge, 8:16, :]
-            at += 2
-        for wide, count in ((pres_x, 4), (gain_x, 3), (rest_x, 3)):
-            first = jnp.where(up, 8 - count, 0)
-            for r in range(count):
-                out[at] = wide[first + r, 0:8, :]
-                out[at + 1] = wide[first + r, 8:16, :]
-                at += 2
+    up = lax.axis_index("gx") % 2 == 0
+    put_blocks(parts, sends, jnp.where(up, 0, 1), out)
+    put_flow(flow_x, up, out)
+
+
+def pack_second(parts, sends, flow_x, out):
+    up = lax.axis_index("gx") % 2 == 1
+    put_blocks(parts, sends, jnp.where(up, 0, 1), out)
+    put_flow(flow_x, up, out)
 
 
 def couple(
-    parts, sends_in, moves_in, tiles_in, slots, flow_x, in_xe, in_xo, in_ye, in_yo, after,
-    drag, dep, out_e, out_o,
+    parts, sends_in, moves_in, tiles_in, slots, flow_x, in_xo, in_xe, in_ye, in_yo, after,
+    pres, screen, source, solid,
+    drag, dep, out_e, gain, rest,
     pool, table, sums, owned, sends, moves, tiles, sems,
 ):
     copies = fetch((sends_in, moves_in, tiles_in), (sends, moves, tiles), sems)
@@ -239,86 +213,118 @@
         total = total[0:4] + total[4:8]
         for f in range(4):
             dep[f, n // 10, n % 10 + 3, :] = total[f]
-    for out, up in ((out_e, y_even), (out_o, jnp.logical_not(y_even))):
-        for f in range(4):
-            for x in range(10):
-                i = f * 10 + x
-                r = 4 * (i % 2)
-                out[i // 2, r : r + 4, :] = jnp.where(up, dep[f, x, 9:13, :], dep[f, x, 3:7, :])
-
-
-def fold_y(dep, in_e, in_o, dep_x, out_o, out_e):
+    gain[...] = 1.0 / (6.0 + screen[...])
+    rest[...] = source[...] - 2.0 * solid[...]
+    put_rims(dep, pres, gain, rest, x_even, out_e)
+
+
+P_AT = 14
+G_AT = P_AT + 4
+S_AT = G_AT + 3
+D_TILES = S_AT + 3
+
+
+def put_rims(dep, pres, gain, rest, up, out):
+    first = jnp.where(up, 6, 0)
+    rim = jnp.where(up, 9, 0)
+    for r in range(4):
+        out[2 * r] = dep[3, first + r, 0:8, :]
+        out[2 * r + 1] = dep[3, first + r, 8:16, :]
+    for c in range(3):
+        out[8 + 2 * c] = dep[c, rim, 0:8, :]
+        out[9 + 2 * c] = dep[c, rim, 8:16, :]
+    for at, ref, count in ((P_AT, pres, 4), (G_AT, gain, 3), (S_AT, rest, 3)):
+        start = jnp.where(up, 8 - count, 0)
+        for r in range(count):
+            out[at + r] = ref[start + r]
+
+
+def pack_fo(dep, pres, gain, rest, out):
+    put_rims(dep, pres, gain, rest, lax.axis_index("gx") % 2 == 1, out)
+
+
+H_DRAG = 7
+H_FIELDS = H_DRAG + 3
+H_TILES = H_FIELDS + 24
+
+
+def fold_x(dep, pres, gain, rest, in_o, in_e, after, load, drag, pres_w, gain_w, rest_w, out_e, out_o):
+    even = lax.axis_index("gx") % 2 == 0
+
+    def from_up(at):
+        return jnp.where(even, in_e[at], in_o[at])
+
+    def from_down(at):
+        return jnp.where(even, in_o[at], in_e[at])
+
+    def two(side, at):
+        return jnp.concatenate([side(at), side(at + 1)], axis=0)
+
+    for x in range(16):
+        total = jnp.zeros((16, 128), F32)
+        if 3 <= x <= 12:
+            total = total + dep[3, x - 3]
+        if 1 <= x <= 4:
+            total = total + two(from_down, 2 * (x - 1))
+        if 11 <= x <= 14:
+            total = total + two(from_up, 2 * (x - 11))
+        load[x] = total
+    for c in range(3):
+        drag[c] = dep[c, 1:9]
+        drag[c, 0] += two(from_down, 8 + 2 * c)
+        drag[c, 7] += two(from_up, 8 + 2 * c)
+    for wide, ref, at, count in ((pres_w, pres, P_AT, 4), (gain_w, gain, G_AT, 3), (rest_w, rest, S_AT, 3)):
+        wide[4:12] = ref[...]
+        if count == 3:
+            wide[0] = jnp.zeros((8, 128), F32)
+            wide[15] = jnp.zeros((8, 128), F32)
+        for r in range(count):
+            wide[4 - count + r] = from_down(at + r)
+            wide[12 + r] = from_up(at + r)
+    parity = lax.axis_index("gy") % 2
+    for out, up in ((out_e, parity == 0), (out_o, parity == 1)):
+        for x in range(14):
+            row = 4 * (x % 2)
+            out[x // 2, row : row + 4, :] = jnp.where(up, load[x + 1, 9:13, :], load[x + 1, 3:7, :])
+        for c in range(3):
+            out[H_DRAG + c] = jnp.where(up, drag[c, :, 12, :], drag[c, :, 3, :])
+        at = H_FIELDS
+        for wide in (pres_w, gain_w, rest_w):
+            for x in range(16):
+                row = 4 * (x % 2)
+                out[at + x // 2, row : row + 4, :] = jnp.where(up, wide[x, 4:8, :], wide[x, 0:4, :])
+            at += 8
+
+
+def finish(load, drag, pres_w, gain_w, rest_w, in_e, in_o, pressure, drag_sum, now, new, gain, off):
     even = lax.axis_index("gy") % 2 == 0
-    dep_x[...] = dep[...]
-    for f in range(4):
-        for x in range(10):
-            i = f * 10 + x
-            r = 4 * (i % 2)
-            a = in_e[i // 2, r : r + 4, :]
-            b = in_o[i // 2, r : r + 4, :]
-            dep_x[f, x, 11:15, :] += jnp.where(even, a, b)
-            dep_x[f, x, 1:5, :] += jnp.where(even, b, a)
-    parity = lax.axis_index("gx") % 2
-    for out, up in ((out_e, parity == 0), (out_o, parity == 1)):
-        first = jnp.where(up, 6, 0)
-        rim = jnp.where(up, 9, 0)
-        for r in range(4):
-            out[2 * r] = dep_x[3, first + r, 0:8, :]
-            out[2 * r + 1] = dep_x[3, first + r, 8:16, :]
-        for c in range(3):
-            out[8 + 2 * c] = dep_x[c, rim, 0:8, :]
-            out[9 + 2 * c] = dep_x[c, rim, 8:16, :]
-
-
-D_TILES = 14
-
-
-def tiles16(ref, at):
-    return jnp.concatenate([ref[at], ref[at + 1]], axis=0)
-
-
-def finish(dep_x, in_e, in_o, near_e, near_o, pres_x, gain_x, rest_x, pressure, drag_sum, now, new, gain, off):
-    even = lax.axis_index("gx") % 2 == 0
-
-    def from_up(a, b, at):
-        return jnp.where(even, tiles16(a, at), tiles16(b, at))
-
-    def from_down(a, b, at):
-        return jnp.where(even, tiles16(b, at), tiles16(a, at))
+
+    def half(side_up, at, x):
+        row = 4 * (x % 2)
+        a = in_e[at + x // 2, row : row + 4, :]
+        b = in_o[at + x // 2, row : row + 4, :]
+        return jnp.where(even, a, b) if side_up else jnp.where(even, b, a)
 
     for c in range(3):
-        drag_sum[c] = dep_x[c, 1:9, 4:12, :]
-        drag_sum[c, 0] += from_down(in_e, in_o, 8 + 2 * c)[4:12]
-        drag_sum[c, 7] += from_up(in_e, in_o, 8 + 2 * c)[4:12]
-    p_at = GROUP + 6
-    g_at = p_at + 8
-    s_at = g_at + 6
+        drag_sum[c] = drag[c, :, 4:12, :]
+        a = in_e[H_DRAG + c]
+        b = in_o[H_DRAG + c]
+        drag_sum[c, :, 0, :] += jnp.where(even, b, a)
+        drag_sum[c, :, 7, :] += jnp.where(even, a, b)
+
+    def rows(wide, n, x):
+        at = H_FIELDS + 8 * n
+        return jnp.concatenate([half(False, at, x), wide[x], half(True, at, x)], axis=0)
+
     for x in range(16):
-        if x < 4:
-            now[x] = from_down(near_e, near_o, p_at + 2 * x)
-        elif x < 12:
-            now[x] = pres_x[x - 4]
-        else:
-            now[x] = from_up(near_e, near_o, p_at + 2 * (x - 12))
+        now[x] = rows(pres_w, 0, x)
     for x in range(1, 15):
-        if x < 4:
-            g = from_down(near_e, near_o, g_at + 2 * (x - 1))
-            s = from_down(near_e, near_o, s_at + 2 * (x - 1))
-        elif x < 12:
-            g = gain_x[x - 4]
-            s = rest_x[x - 4]
-        else:
-            g = from_up(near_e, near_o, g_at + 2 * (x - 12))
-            s = from_up(near_e, near_o, s_at + 2 * (x - 12))
-        load = jnp.zeros((16, 128), F32)
-        if 3 <= x <= 12:
-            load = load + dep_x[3, x - 3]
-        if x <= 4:
-            load = load + from_down(in_e, in_o, 2 * (x - 1))
-        if x >= 11:
-            load = load + from_up(in_e, in_o, 2 * (x - 11))
+        off[x] = load[x]
+        off[x, 1:5, :] += half(False, 0, x - 1)
+        off[x, 11:15, :] += half(True, 0, x - 1)
+        g = rows(gain_w, 1, x)
         gain[x] = g
-        off[x] = g * (s + 2.0 * load)
+        off[x] = g * (rows(rest_w, 2, x) + 2.0 * off[x])
     lane = lax.broadcasted_iota(jnp.int32, (16, 128), 1)
     inner_low = lane > 0
     inner_high = lane < 127
@@ -404,7 +410,7 @@
     return look
 
 
-def run_tiles(pairs, chosen, count, left, near, right, sums):
+def run_tiles(pairs, chosen, count, left, near, right, sums, begin, end):
     def tile(n):
         t = chosen[jnp.minimum(n, count - 1)]
         i = pairs[0, t]
@@ -428,12 +434,12 @@
         return i, got * jnp.where(n < count, 1.0, 0.0)
 
     def step(g, carry):
-        made = [tile(g * CONTACT_UNROLL + u) for u in range(CONTACT_UNROLL)]
+        made = [tile(begin + g * CONTACT_UNROLL + u) for u in range(CONTACT_UNROLL)]
         for i, got in made:
             sums[i] += got
         return carry
 
-    lax.fori_loop(0, (count + CONTACT_UNROLL - 1) // CONTACT_UNROLL, step, 0)
+    lax.fori_loop(0, jnp.maximum(end - begin + CONTACT_UNROLL - 1, 0) // CONTACT_UNROLL, step, 0)
 
 
 def contact_own(pairs, total_ref, parts, after, left, near, right, sums, chosen):
@@ -453,25 +459,25 @@
         return look(k * (MAXT // groups), count, MAXT // groups)
 
     count = lax.fori_loop(0, groups, own, 0)
-    run_tiles(pairs, chosen, count, left, near, right, sums)
-
-
-def contact_rest(
-    pairs, total_ref, parts, in_xe, in_xo, in_ye, in_yo, drag, after, left_in, near_in, right_in, sums_in,
-    force, left, near, right, sums, chosen,
-):
+    run_tiles(pairs, chosen, count, left, near, right, sums, 0, count)
+
+
+def received(in_xe, in_xo, in_ye, in_yo):
     x_even = lax.axis_index("gx") % 2 == 0
     y_even = lax.axis_index("gy") % 2 == 0
+    return ((x_even, in_xo, in_xe), (x_even, in_xe, in_xo), (y_even, in_yo, in_ye), (y_even, in_ye, in_yo))
+
+
+def contact_more(
+    pairs, total_ref, in_xo, in_xe, in_ye, in_yo, after, left_in, near_in, right_in, sums_in,
+    left, near, right, sums, chosen,
+):
     total = total_ref[0, 0]
     four, right_of = preparers(left, near, right)
     look = lister(pairs, total, chosen, False)
-    groups = (
-        (0, x_even, in_xe, in_xo), (1, x_even, in_xe, in_xo), (0, y_even, in_ye, in_yo), (1, y_even, in_ye, in_yo)
-    )
     count = jnp.int32(0)
     part = MAXT // 16
-    for d, (up, even, a, b) in enumerate(groups):
-        first, second = (b, a) if up == 0 else (a, b)
+    for d, (even, first, second) in enumerate(received(in_xe, in_xo, in_ye, in_yo)):
         for u in range(MOVERS // 4):
             tiles = [jnp.where(even, first[4 * u + b], second[4 * u + b]) for b in range(4)]
             four(tiles, NB + d * SLOTS + 4 * u)
@@ -488,7 +494,15 @@
             return look((d * 4 + 1 + k) * part, count, part)
 
         count = lax.fori_loop(0, PAIRS // 8, others, count)
-    run_tiles(pairs, chosen, count, left, near, right, sums)
+    chosen[LAST] = count
+    run_tiles(pairs, chosen, count, left, near, right, sums, 0, jnp.minimum(EARLY, count))
+
+
+def contact_end(
+    pairs, parts, in_xo, in_xe, in_ye, in_yo, drag, after, left, near, right, chosen, sums_in, force, sums
+):
+    count = chosen[LAST]
+    run_tiles(pairs, chosen, count, left, near, right, sums, EARLY, count)
 
     def put(n, at, position):
         for c in range(3):
@@ -499,8 +513,7 @@
 
     for n in range(NB // 8):
         put(n, 8 * n, lambda c, n=n: parts[8 * n : 8 * n + 8, c, :])
-    for d, (up, even, a, b) in enumerate(groups):
-        first, second = (b, a) if up == 0 else (a, b)
+    for d, (even, first, second) in enumerate(received(in_xe, in_xo, in_ye, in_yo)):
         for k in range(2):
             put(
                 NB // 8 + 2 * d + k,
@@ -537,35 +550,21 @@
     solid_old,
     screening,
 ):
+    parts = particles[0, 0]
     sends = send_list[0, 0]
     moves = move_count[0, 0]
     tiles = drag_tiles[0, 0].T
     pairs = tile_pairs[0, 0].T
+    slots = cell_slot[0, 0]
     cells = (8, 8, 128)
-    wide = (8, 16, 128)
-    ye, yo, gain, rest, parts, flow, pres, slots = call(
-        pack_y,
-        (
-            shape(Y_TILES, 8, 128), shape(Y_TILES, 8, 128), shape(*cells), shape(*cells),
-            shape(NB, 8, 128), shape(3, *cells), shape(*cells), jax.ShapeDtypeStruct((384, 128), jnp.int32),
-        ),
-        [HB] * 8,
-        [
-            pltpu.SMEM((4, SLOTS), jnp.int32),
-            pltpu.VMEM(cells, F32),
-            pltpu.VMEM(cells, F32),
-            pltpu.VMEM(cells, F32),
-            pltpu.SemaphoreType.DMA((8,)),
-        ],
-    )(particles[0, 0], sends, fluid_velocity, pressure_init, screening, source, solid_old, cell_slot[0, 0])
+    ye, yo = call(pack_y, (shape(Y_TILES, 8, 128), shape(Y_TILES, 8, 128)), [VM, SM, VM])(parts, sends, fluid_velocity)
     got_ye = swap(ye, "gy", 0)
     got_yo = swap(yo, "gy", 1)
-    xo, xe, flow_x, pres_x, gain_x, rest_x = call(
-        pack_x,
-        (shape(X_TILES, 8, 128), shape(X_TILES, 8, 128), shape(3, *wide), shape(*wide), shape(*wide), shape(*wide)),
-        [VM, SM] + [VM] * 6,
-    )(parts, sends, flow, pres, gain, rest, got_ye, got_yo)
+    xe, flow_x = call(pack_first, (shape(X_TILES, 8, 128), shape(3, 8, 16, 128)), [VM, SM, VM, VM, VM])(
+        parts, sends, fluid_velocity, got_ye, got_yo
+    )
     got_xe = swap(xe, "gx", 0)
+    xo = call(pack_second, shape(X_TILES, 8, 128), [VM, SM, VM])(parts, sends, flow_x)
     got_xo = swap(xo, "gx", 1)
     operands = (
         jax.ShapeDtypeStruct((POOL // 4, 128, 128), BF16),
@@ -574,12 +573,12 @@
         shape(OWNABLE, 8, 128),
     )
     prepared = call(
-        contact_own, operands, [SM, SM, VM, VM], [pltpu.SMEM((MAXT + 1,), jnp.int32)], flops=10**8
+        contact_own, operands, [SM, SM, VM, VM], [pltpu.SMEM((LIST,), jnp.int32)], flops=10**8
     )(pairs, tile_count, parts, xo)
-    drag, dep, de, do = call(
+    drag, dep, fe, gain, rest = call(
         couple,
-        (shape(3, 384, 128), shape(4, 10, 16, 128), shape(20, 8, 128), shape(20, 8, 128)),
-        [VM, HB, HB, HB] + [VM] * 7,
+        (shape(3, 384, 128), shape(4, 10, 16, 128), shape(D_TILES, 8, 128), shape(*cells), shape(*cells)),
+        [VM, HB, HB, HB] + [VM] * 11,
         [
             pltpu.VMEM((OWNABLE, 8, 128), F32),
             pltpu.VMEM((100, 8, 128), F32),
@@ -590,28 +589,43 @@
             pltpu.SMEM((4, 384), jnp.int32),
             pltpu.SemaphoreType.DMA((3,)),
         ],
-    )(parts, sends, moves, tiles, slots, flow_x, got_xe, got_xo, got_ye, got_yo, prepared[3])
-    got_de = swap(de, "gy", 0)
-    got_do = swap(do, "gy", 1)
-    dep_x, fo, fe = call(
-        fold_y, (shape(4, 10, 16, 128), shape(D_TILES, 8, 128), shape(D_TILES, 8, 128)), [VM] * 3
-    )(dep, got_de, got_do)
+    )(
+        parts, sends, moves, tiles, slots, flow_x, got_xo, got_xe, got_ye, got_yo, prepared[3],
+        pressure_init, screening, source, solid_old,
+    )
     got_fe = swap(fe, "gx", 0)
+    fo = call(pack_fo, shape(D_TILES, 8, 128), [VM] * 4)(dep, pressure_init, gain, rest)
     got_fo = swap(fo, "gx", 1)
-    force = call(
-        contact_rest,
-        (shape(3, 384, 128), *operands),
-        [SM, SM] + [VM] * 11,
-        [pltpu.SMEM((MAXT + 1,), jnp.int32)],
+    *more, chosen = call(
+        contact_more,
+        (*operands, jax.ShapeDtypeStruct((LIST,), jnp.int32)),
+        [SM, SM] + [VM] * 9,
+        flops=10**8,
+        aliases={7: 0, 8: 1, 9: 2, 10: 3},
+    )(pairs, tile_count, got_xo, got_xe, got_ye, got_yo, fo, *prepared)
+    load, drag_x, pres_w, gain_w, rest_w, he, ho = call(
+        fold_x,
+        (
+            shape(16, 16, 128), shape(3, 8, 16, 128), shape(16, 8, 128), shape(16, 8, 128), shape(16, 8, 128),
+            shape(H_TILES, 8, 128), shape(H_TILES, 8, 128),
+        ),
+        [VM] * 7,
+    )(dep, pressure_init, gain, rest, got_fo, got_fe, more[3])
+    got_he = swap(he, "gy", 0)
+    got_ho = swap(ho, "gy", 1)
+    force, unused = call(
+        contact_end,
+        (shape(3, 384, 128), operands[3]),
+        [SM] + [VM] * 10 + [SM, VM],
         flops=10**9,
-        aliases={9: 1, 10: 2, 11: 3, 12: 4},
-    )(pairs, tile_count, parts, got_xe, got_xo, got_ye, got_yo, drag, fo, *prepared)[0]
+        aliases={12: 1},
+    )(pairs, parts, got_xo, got_xe, got_ye, got_yo, drag, ho, *more[:3], chosen, more[3])
     pressure, drag_sum = call(
         finish,
         (shape(*cells), shape(3, *cells)),
-        [VM] * 8,
+        [VM] * 7,
         [pltpu.VMEM((16, 16, 128), F32)] * 4,
-    )(dep_x, got_fe, got_fo, got_xe, got_xo, pres_x, gain_x, rest_x)
+    )(load, drag_x, pres_w, gain_w, rest_w, got_he, got_ho)
     return (pressure, drag_sum, force.transpose(1, 0, 2)[None, None])
 
 

time: 108 us -> 92.5 us (0.86)
  the two profiles are of different devices: /device:TPU:31 before, /device:TPU:54 now
where the time goes in v3:
time: 92.5 us; the launch traced here: 92.1 us
  starting transfers between devices  48.9 us (53%)
  Pallas kernels  33.7 us (36%)
  waiting for transfers between devices  4.66 us (5%)
  local copies, waits for them, and re-layouts  3.33 us (4%)
  between operations  1.56 us (2%)
    ppermute x8, starting transfers between devices, swap(): return lax.ppermute(array, axis, pairs_of(first, count, count - 1))  48.9 us
    pallas_call x1, Pallas kernels, body(): call(contact_more, (*operands, jax.ShapeDtypeStruct((LIST,), jnp.int32)),...  9.16 us
    pallas_call x1, Pallas kernels, body(): call(contact_end, (shape(3, 384, 128), operands[3]), [SM] + [VM] * 10 + [...  7.54 us
    pallas_call x1, Pallas kernels, body(): call(contact_own, operands, [SM, SM, VM, VM], [pltpu.SMEM((LIST,), jnp.in...  7.12 us
    pallas_call x1, Pallas kernels, body(): call(couple, (shape(3, 384, 128), shape(4, 10, 16, 128), shape(D_TILES, 8...  6.63 us
    ppermute x8, waiting for transfers between devices, swap(): return lax.ppermute(array, axis, pairs_of(first, count, count - 1))  4.66 us
    unnamed x24, local copies, waits for them, and re-layouts  3.33 us
  transfers between devices with their start and end apart: 8, of which 1 were waited for; matrix products, arithmetic and copies ran while one was open for 0% of the time, Pallas kernels for 26%

profile of v3, /device:TPU:54, one launch (start us, length us, event | category | flops | bytes accessed | tf_op | source)
XLA Modules:
  0.0 92.1 jit_solution(1662796069821950302)
XLA Ops:
  0.6 0.0 copy-start.11
  0.6 0.0 copy-start
  0.7 1.0 %copy-done = f32[1,1,128,8,128]{4,3,2,1,0:T(8,128)S(1)} copy-done((f32[1,1,128,8,128]{4,3,2,1,0:T(8,128)S(1)}, f32[1,1,128,8,128]{4,3,2,1,0:T(8,128)}, u32[]{:S(2)}) %copy-start) | copy-done | bytes 524312
  1.7 0.0 copy-start.2
  1.7 0.9 copy-done.2
  2.6 0.0 copy-start.9
  2.6 0.7 copy-done.9
  3.3 0.0 copy-start.3
  3.3 0.0 copy-start.4
  3.3 0.0 copy-start.6
  3.3 0.0 copy-start.7
  3.3 0.0 copy-start.8
  3.3 0.0 copy-start.10
  3.3 0.7 shard_map.139
  4.0 1.9 %collective-permute-start = (f32[43,8,128]{2,1,0:T(8,128)S(1)}, f32[43,8,128]{2,1,0:T(8,128)S(1)}, u32[]{:S(2)}, u32[]{:S(2)}) collective-permute-start(f32[43,8,128]{2,1,0:T(8,128)S(1)} %get-tuple-element.31), channel_id=1, source_target_pairs={{0,1},{2,3},{4,5},{6,7},{8,9},{10,11},{12,13},{14,15},{1,0},{3,2},... | collective-permute-start | bytes 528392 | tf_op jit(solution)/shard_map/ppermute | solution.py:536
  6.0 2.1 %collective-permute-start.1 = (f32[43,8,128]{2,1,0:T(8,128)S(1)}, f32[43,8,128]{2,1,0:T(8,128)S(1)}, u32[]{:S(2)}, u32[]{:S(2)}) collective-permute-start(f32[43,8,128]{2,1,0:T(8,128)S(1)} %get-tuple-element.32), channel_id=1, source_target_pairs={{1,2},{3,4},{5,6},{7,8},{9,10},{11,12},{13,14},{2,1},{4,3},{6,5},{... | collective-permute-start | bytes 528392 | tf_op jit(solution)/shard_map/ppermute | solution.py:536
  8.1 0.0 collective-permute-done.in_e.in_ye
  8.1 4.6 %collective-permute-done.1.in_o.in_yo = f32[43,8,128]{2,1,0:T(8,128)S(1)} collective-permute-done((f32[43,8,128]{2,1,0:T(8,128)S(1)}, f32[43,8,128]{2,1,0:T(8,128)S(1)}, u32[]{:S(2)}, u32[]{:S(2)}) %collective-permute-start.1) | collective-permute-done | bytes 176160 | tf_op jit(solution)/shard_map/ppermute | solution.py:536
  12.7 0.7 shard_map.140
  13.4 0.7 shard_map.141.after
  14.1 2.4 %collective-permute-start.2 = (f32[46,8,128]{2,1,0:T(8,128)S(1)}, f32[46,8,128]{2,1,0:T(8,128)S(1)}, u32[]{:S(2)}, u32[]{:S(2)}) collective-permute-start(f32[46,8,128]{2,1,0:T(8,128)S(1)} %shard_map.141.after), channel_id=1, source_target_pairs={{16,32},{48,64},{80,96},{112,128},{144,160},{176,192},{208,224},{2... | collective-permute-start | bytes 565256 | tf_op jit(solution)/shard_map/ppermute | solution.py:536
  16.4 15.2 %collective-permute-start.3 = (f32[46,8,128]{2,1,0:T(8,128)S(1)}, f32[46,8,128]{2,1,0:T(8,128)S(1)}, u32[]{:S(2)}, u32[]{:S(2)}) collective-permute-start(f32[46,8,128]{2,1,0:T(8,128)S(1)} %get-tuple-element.34), channel_id=1, source_target_pairs={{0,16},{32,48},{64,80},{96,112},{128,144},{160,176},{192,208},{224... | collective-permute-start | bytes 565256 | tf_op jit(solution)/shard_map/ppermute | solution.py:536
  32.3 0.0 copy-start.5
  32.3 0.7 copy-done.5
  33.0 7.1 %shard_map.142 = (bf16[96,128,128]{2,1,0:T(8,128)(2,1)S(1)}, bf16[384,16,128]{2,1,0:T(8,128)(2,1)S(1)}, bf16[192,32,256]{2,1,0:T(8,128)(2,1)S(1)}, f32[192,8,128]{2,1,0:T(8,128)S(1)}) custom-call(s32[2,512]{1,0:T(2,128)S(1)} %bitcast.20, s32[1,1]{1,0:T(1,128)S(6)} %copy.25.total_ref, f32[128,8,128]{2,1,0:T(8,128)S(1)} %bitcast.16, ...), custom_call_target="tpu_custom_call" | custom-call | flops 100000000 | bytes 1000000 | tf_op jit(solution)/shard_map/pallas_call | solution.py:575
  40.1 0.0 collective-permute-done.2.in_xo
  40.1 0.0 collective-permute-done.3.in_xe
  40.2 0.0 copy-done.11
  40.2 0.0 copy-done.3
  40.2 0.0 copy-done.4
  40.2 0.0 copy-done.6
  40.2 0.0 copy-done.7
  40.2 0.0 copy-done.8
  40.2 0.0 copy-done.10
  40.2 6.6 %shard_map.143 = (f32[3,384,128]{2,1,0:T(8,128)S(1)}, f32[4,10,16,128]{3,2,1,0:T(8,128)S(1)}, f32[24,8,128]{2,1,0:T(8,128)S(1)}, f32[8,8,128]{2,1,0:T(8,128)S(1)}, f32[8,8,128]{2,1,0:T(8,128)S(1)}) custom-call(f32[128,8,128]{2,1,0:T(8,128)S(1)} %bitcast.17, s32[4,64]{1,0:T(4,128)S(1)} %bitcast.26, s32[2,4]{1,0:T(2,128)S(1)} %bitcast.28, ...), custom_call_target="tpu_custom_call" | custom-call | flops 1000000 | bytes 1000000 | tf_op jit(solution)/shard_map/pallas_call | solution.py:578
  46.9 1.9 %collective-permute-start.4 = (f32[24,8,128]{2,1,0:T(8,128)S(1)}, f32[24,8,128]{2,1,0:T(8,128)S(1)}, u32[]{:S(2)}, u32[]{:S(2)}) collective-permute-start(f32[24,8,128]{2,1,0:T(8,128)S(1)} %shard_map.144.after), channel_id=1, source_target_pairs={{16,32},{48,64},{80,96},{112,128},{144,160},{176,192},{208,224},{2... | collective-permute-start | bytes 294920 | tf_op jit(solution)/shard_map/ppermute | solution.py:536
  48.8 21.5 %collective-permute-start.5 = (f32[24,8,128]{2,1,0:T(8,128)S(1)}, f32[24,8,128]{2,1,0:T(8,128)S(1)}, u32[]{:S(2)}, u32[]{:S(2)}) collective-permute-start(f32[24,8,128]{2,1,0:T(8,128)S(1)} %get-tuple-element.39), channel_id=1, source_target_pairs={{0,16},{32,48},{64,80},{96,112},{128,144},{160,176},{192,208},{224... | collective-permute-start | bytes 294920 | tf_op jit(solution)/shard_map/ppermute | solution.py:536
  70.4 0.0 copy-start.1
  70.4 9.2 %shard_map.145 = (bf16[96,128,128]{2,1,0:T(8,128)(2,1)S(1)}, bf16[384,16,128]{2,1,0:T(8,128)(2,1)S(1)}, bf16[192,32,256]{2,1,0:T(8,128)(2,1)S(1)}, f32[192,8,128]{2,1,0:T(8,128)S(1)}, s32[640]{0:T(1024)S(1)}) custom-call(s32[2,512]{1,0:T(2,128)S(1)} %bitcast.21, ...), custom_call_target="tpu_custom_call", output_to_operand_aliasing={{0}: (7, {}), {1}: (8, {}), {2}: (9, {}), {3}: (10, {})} | custom-call | flops 100000000 | bytes 1000000 | tf_op jit(solution)/shard_map/pallas_call | solution.py:599
  79.5 0.0 collective-permute-done.4.in_o
  79.5 0.0 collective-permute-done.5.in_e
  79.5 0.1 shard_map.146
  79.7 1.9 %collective-permute-start.6 = (f32[34,8,128]{2,1,0:T(8,128)S(1)}, f32[34,8,128]{2,1,0:T(8,128)S(1)}, u32[]{:S(2)}, u32[]{:S(2)}) collective-permute-start(f32[34,8,128]{2,1,0:T(8,128)S(1)} %get-tuple-element.49), channel_id=1, source_target_pairs={{0,1},{2,3},{4,5},{6,7},{8,9},{10,11},{12,13},{14,15},{1,0},{3,2},... | collective-permute-start | bytes 417800 | tf_op jit(solution)/shard_map/ppermute | solution.py:536
  81.6 1.9 %collective-permute-start.7 = (f32[34,8,128]{2,1,0:T(8,128)S(1)}, f32[34,8,128]{2,1,0:T(8,128)S(1)}, u32[]{:S(2)}, u32[]{:S(2)}) collective-permute-start(f32[34,8,128]{2,1,0:T(8,128)S(1)} %get-tuple-element.50.after), channel_id=1, source_target_pairs={{1,2},{3,4},{5,6},{7,8},{9,10},{11,12},{13,14},{2,1},{4,3},{6,5},{... | collective-permute-start | bytes 417800 | tf_op jit(solution)/shard_map/ppermute | solution.py:536
  83.5 0.0 copy-done.1
  83.5 7.5 %shard_map.148 = (f32[3,384,128]{2,1,0:T(8,128)}, f32[192,8,128]{2,1,0:T(8,128)S(1)}) custom-call(s32[2,512]{1,0:T(2,128)S(1)} %bitcast.22, f32[128,8,128]{2,1,0:T(8,128)S(1)} %bitcast.18, f32[46,8,128]{2,1,0:T(8,128)S(1)} %collective-permute-done.2.in_xo, f32[46,8,128]{2,1,0:T(8,128)S(1)} %collective-permute-done.3.in_xe, ...), custom_call_target="tpu_custom_call", output_to_operand_aliasing={{1}: (12, {})} | custom-call | flops 1000000000 | bytes 1000000 | tf_op jit(solution)/shard_map/pallas_call | solution.py:616
  91.1 0.0 collective-permute-done.6.in_e
  91.1 0.0 collective-permute-done.7.in_o
  91.1 1.0 %shard_map.147 = (f32[8,8,128]{2,1,0:T(8,128)}, f32[3,8,8,128]{3,2,1,0:T(8,128)}) custom-call(f32[16,16,128]{2,1,0:T(8,128)S(1)} %get-tuple-element.44.load, f32[3,8,16,128]{3,2,1,0:T(8,128)S(1)} %get-tuple-element.45.drag, f32[16,8,128]{2,1,0:T(8,128)S(1)} %get-tuple-element.46.pres_w, f32[16,8,128]{2,1,0:T(8,128)S(1)} %get-tuple-element.47.gain_w, ...), custom_call_target="tpu_custom_call" | custom-call | flops 1000000 | bytes 1000000 | tf_op jit(solution)/shard_map/pallas_call | solution.py:623
  (1 shorter events, 0.0 us)
Async XLA Ops:
  0.6 39.5 %copy-start.11 = (s32[1,1,2,4]{3,2,1,0:T(2,128)S(1)}, s32[1,1,2,4]{3,2,1,0:T(2,128)}, u32[]{:S(2)}) copy-start(s32[1,1,2,4]{3,2,1,0:T(2,128)} %param.14) | copy-start | bytes 100
  0.6 1.0 %copy-start = (f32[1,1,128,8,128]{4,3,2,1,0:T(8,128)S(1)}, f32[1,1,128,8,128]{4,3,2,1,0:T(8,128)}, u32[]{:S(2)}) copy-start(f32[1,1,128,8,128]{4,3,2,1,0:T(8,128)} %param.12) | copy-start | bytes 1572868
  1.7 0.9 copy-start.2
  2.6 0.7 copy-start.9
  3.3 36.9 %copy-start.3 = (f32[8,8,128]{2,1,0:T(8,128)S(1)}, f32[8,8,128]{2,1,0:T(8,128)}, u32[]{:S(2)}) copy-start(f32[8,8,128]{2,1,0:T(8,128)} %pres.5) | copy-start | bytes 98308
  3.3 36.9 %copy-start.4 = (s32[1,1,384,128]{3,2,1,0:T(8,128)S(1)}, s32[1,1,384,128]{3,2,1,0:T(8,128)}, u32[]{:S(2)}) copy-start(s32[1,1,384,128]{3,2,1,0:T(8,128)} %param.18) | copy-start | bytes 589828
  3.3 36.9 %copy-start.6 = (f32[8,8,128]{2,1,0:T(8,128)S(1)}, f32[8,8,128]{2,1,0:T(8,128)}, u32[]{:S(2)}) copy-start(f32[8,8,128]{2,1,0:T(8,128)} %screen.1) | copy-start | bytes 98308
  3.3 36.9 %copy-start.7 = (f32[8,8,128]{2,1,0:T(8,128)S(1)}, f32[8,8,128]{2,1,0:T(8,128)}, u32[]{:S(2)}) copy-start(f32[8,8,128]{2,1,0:T(8,128)} %source.1) | copy-start | bytes 98308
  3.3 36.9 %copy-start.8 = (f32[8,8,128]{2,1,0:T(8,128)S(1)}, f32[8,8,128]{2,1,0:T(8,128)}, u32[]{:S(2)}) copy-start(f32[8,8,128]{2,1,0:T(8,128)} %solid.1) | copy-start | bytes 98308
  3.3 36.9 %copy-start.10 = (s32[1,1,384,4]{2,3,1,0:T(4,128)S(1)}, s32[1,1,384,4]{2,3,1,0:T(4,128)}, u32[]{:S(2)}) copy-start(s32[1,1,384,4]{2,3,1,0:T(4,128)} %param.17) | copy-start | bytes 18436
  4.0 4.1 %collective-permute-start = (f32[43,8,128]{2,1,0:T(8,128)S(1)}, f32[43,8,128]{2,1,0:T(8,128)S(1)}, u32[]{:S(2)}, u32[]{:S(2)}) collective-permute-start(f32[43,8,128]{2,1,0:T(8,128)S(1)} %get-tuple-element.31), channel_id=1, source_target_pairs={{0,1},{2,3},{4,5},{6,7},{8,9},{10,11},{12,13},{14,15},{1,0},{3,2},... | collective-permute-start | bytes 528392 | tf_op jit(solution)/shard_map/ppermute | solution.py:536
  6.0 6.8 %collective-permute-start.1 = (f32[43,8,128]{2,1,0:T(8,128)S(1)}, f32[43,8,128]{2,1,0:T(8,128)S(1)}, u32[]{:S(2)}, u32[]{:S(2)}) collective-permute-start(f32[43,8,128]{2,1,0:T(8,128)S(1)} %get-tuple-element.32), channel_id=1, source_target_pairs={{1,2},{3,4},{5,6},{7,8},{9,10},{11,12},{13,14},{2,1},{4,3},{6,5},{... | collective-permute-start | bytes 528392 | tf_op jit(solution)/shard_map/ppermute | solution.py:536
  14.1 26.1 %collective-permute-start.2 = (f32[46,8,128]{2,1,0:T(8,128)S(1)}, f32[46,8,128]{2,1,0:T(8,128)S(1)}, u32[]{:S(2)}, u32[]{:S(2)}) collective-permute-start(f32[46,8,128]{2,1,0:T(8,128)S(1)} %shard_map.141.after), channel_id=1, source_target_pairs={{16,32},{48,64},{80,96},{112,128},{144,160},{176,192},{208,224},{2... | collective-permute-start | bytes 565256 | tf_op jit(solution)/shard_map/ppermute | solution.py:536
  16.4 23.7 %collective-permute-start.3 = (f32[46,8,128]{2,1,0:T(8,128)S(1)}, f32[46,8,128]{2,1,0:T(8,128)S(1)}, u32[]{:S(2)}, u32[]{:S(2)}) collective-permute-start(f32[46,8,128]{2,1,0:T(8,128)S(1)} %get-tuple-element.34), channel_id=1, source_target_pairs={{0,16},{32,48},{64,80},{96,112},{128,144},{160,176},{192,208},{224... | collective-permute-start | bytes 565256 | tf_op jit(solution)/shard_map/ppermute | solution.py:536
  32.3 0.7 copy-start.5
  46.9 32.6 %collective-permute-start.4 = (f32[24,8,128]{2,1,0:T(8,128)S(1)}, f32[24,8,128]{2,1,0:T(8,128)S(1)}, u32[]{:S(2)}, u32[]{:S(2)}) collective-permute-start(f32[24,8,128]{2,1,0:T(8,128)S(1)} %shard_map.144.after), channel_id=1, source_target_pairs={{16,32},{48,64},{80,96},{112,128},{144,160},{176,192},{208,224},{2... | collective-permute-start | bytes 294920 | tf_op jit(solution)/shard_map/ppermute | solution.py:536
  48.8 30.7 %collective-permute-start.5 = (f32[24,8,128]{2,1,0:T(8,128)S(1)}, f32[24,8,128]{2,1,0:T(8,128)S(1)}, u32[]{:S(2)}, u32[]{:S(2)}) collective-permute-start(f32[24,8,128]{2,1,0:T(8,128)S(1)} %get-tuple-element.39), channel_id=1, source_target_pairs={{0,16},{32,48},{64,80},{96,112},{128,144},{160,176},{192,208},{224... | collective-permute-start | bytes 294920 | tf_op jit(solution)/shard_map/ppermute | solution.py:536
  70.4 13.2 %copy-start.1 = (f32[1,1,128,8,128]{4,3,2,1,0:T(8,128)S(1)}, f32[1,1,128,8,128]{4,3,2,1,0:T(8,128)}, u32[]{:S(2)}) copy-start(f32[1,1,128,8,128]{4,3,2,1,0:T(8,128)} %param.12) | copy-start | bytes 1572868
  79.7 11.4 %collective-permute-start.6 = (f32[34,8,128]{2,1,0:T(8,128)S(1)}, f32[34,8,128]{2,1,0:T(8,128)S(1)}, u32[]{:S(2)}, u32[]{:S(2)}) collective-permute-start(f32[34,8,128]{2,1,0:T(8,128)S(1)} %get-tuple-element.49), channel_id=1, source_target_pairs={{0,1},{2,3},{4,5},{6,7},{8,9},{10,11},{12,13},{14,15},{1,0},{3,2},... | collective-permute-start | bytes 417800 | tf_op jit(solution)/shard_map/ppermute | solution.py:536
  81.6 9.5 %collective-permute-start.7 = (f32[34,8,128]{2,1,0:T(8,128)S(1)}, f32[34,8,128]{2,1,0:T(8,128)S(1)}, u32[]{:S(2)}, u32[]{:S(2)}) collective-permute-start(f32[34,8,128]{2,1,0:T(8,128)S(1)} %get-tuple-element.50.after), channel_id=1, source_target_pairs={{1,2},{3,4},{5,6},{7,8},{9,10},{11,12},{13,14},{2,1},{4,3},{6,5},{... | collective-permute-start | bytes 417800 | tf_op jit(solution)/shard_map/ppermute | solution.py:536

commit v4 on v3

--- a/solution.py
+++ b/solution.py
@@ -397,12 +397,15 @@
     return four, right_of
 
 
-def lister(pairs, total, chosen, wanted_own):
+def lister(pairs, total, chosen, from_x):
+    def along_x(m):
+        return (m >= NB) & (m < NB + 2 * SLOTS)
+
     def look(first, count, size):
         for v in range(size):
             t = first + v
-            own = jnp.maximum(pairs[0, t], pairs[1, t]) < NB
-            wanted = own if wanted_own else jnp.logical_not(own)
+            needs = along_x(pairs[0, t]) | along_x(pairs[1, t])
+            wanted = needs if from_x else jnp.logical_not(needs)
             chosen[count] = t
             count = count + jnp.where(wanted & (t < total), 1, 0)
         return count
@@ -442,12 +445,32 @@
     lax.fori_loop(0, jnp.maximum(end - begin + CONTACT_UNROLL - 1, 0) // CONTACT_UNROLL, step, 0)
 
 
-def contact_own(pairs, total_ref, parts, after, left, near, right, sums, chosen):
+def prepare_received(four, right_of, d, even, first, second, look, at, part, count):
+    for u in range(MOVERS // 4):
+        tiles = [jnp.where(even, first[4 * u + b], second[4 * u + b]) for b in range(4)]
+        four(tiles, NB + d * SLOTS + 4 * u)
+        for b in range(4):
+            right_of(tiles[b], NB + d * MOVERS + 4 * u + b)
+    count = look(at, count, part)
+
+    def others(k, count):
+        for u in range(2):
+            s = MOVERS + 8 * k + 4 * u
+            tiles = [jnp.where(even, first[s + b], second[s + b]) for b in range(4)]
+            four(tiles, NB + d * SLOTS + s)
+            four([pltpu.roll(tile, 4, 0) for tile in tiles], NB + d * SLOTS + s + PAIRS)
+        return look(at + (1 + k) * part, count, part)
+
+    return lax.fori_loop(0, PAIRS // 8, others, count)
+
+
+def contact_near(pairs, total_ref, parts, in_ye, in_yo, after, left, near, right, sums, chosen):
     total = total_ref[0, 0]
     sums[...] = jnp.zeros_like(sums)
     four, right_of = preparers(left, near, right)
-    look = lister(pairs, total, chosen, True)
+    look = lister(pairs, total, chosen, False)
     groups = NB // 4 // PREPARE
+    part = MAXT // 2 // groups
 
     def own(k, count):
         for u in range(PREPARE):
@@ -456,9 +479,13 @@
             four(tiles, m)
             for b in range(4):
                 right_of(tiles[b], m + b)
-        return look(k * (MAXT // groups), count, MAXT // groups)
-
-    count = lax.fori_loop(0, groups, own, 0)
+        return look(k * part, count, part)
+
+    count = lax.fori_loop(0, groups, own, jnp.int32(0))
+    y_even = lax.axis_index("gy") % 2 == 0
+    for d, first, second in ((2, in_yo, in_ye), (3, in_ye, in_yo)):
+        at = MAXT // 2 + (d - 2) * (MAXT // 4)
+        count = prepare_received(four, right_of, d, y_even, first, second, look, at, MAXT // 16, count)
     run_tiles(pairs, chosen, count, left, near, right, sums, 0, count)
 
 
@@ -469,31 +496,18 @@
 
 
 def contact_more(
-    pairs, total_ref, in_xo, in_xe, in_ye, in_yo, after, left_in, near_in, right_in, sums_in,
+    pairs, total_ref, in_xo, in_xe, after, left_in, near_in, right_in, sums_in,
     left, near, right, sums, chosen,
 ):
     total = total_ref[0, 0]
     four, right_of = preparers(left, near, right)
-    look = lister(pairs, total, chosen, False)
+    look = lister(pairs, total, chosen, True)
+    x_even = lax.axis_index("gx") % 2 == 0
     count = jnp.int32(0)
-    part = MAXT // 16
-    for d, (even, first, second) in enumerate(received(in_xe, in_xo, in_ye, in_yo)):
-        for u in range(MOVERS // 4):
-            tiles = [jnp.where(even, first[4 * u + b], second[4 * u + b]) for b in range(4)]
-            four(tiles, NB + d * SLOTS + 4 * u)
-            for b in range(4):
-                right_of(tiles[b], NB + d * MOVERS + 4 * u + b)
-        count = look(d * 4 * part, count, part)
-
-        def others(k, count, d=d, even=even, first=first, second=second):
-            for u in range(2):
-                s = MOVERS + 8 * k + 4 * u
-                tiles = [jnp.where(even, first[s + b], second[s + b]) for b in range(4)]
-                four(tiles, NB + d * SLOTS + s)
-                four([pltpu.roll(tile, 4, 0) for tile in tiles], NB + d * SLOTS + s + PAIRS)
-            return look((d * 4 + 1 + k) * part, count, part)
-
-        count = lax.fori_loop(0, PAIRS // 8, others, count)
+    for d, first, second in ((0, in_xo, in_xe), (1, in_xe, in_xo)):
+        count = prepare_received(
+            four, right_of, d, x_even, first, second, look, d * (MAXT // 2), MAXT // 8, count
+        )
     chosen[LAST] = count
     run_tiles(pairs, chosen, count, left, near, right, sums, 0, jnp.minimum(EARLY, count))
 
@@ -573,8 +587,8 @@
         shape(OWNABLE, 8, 128),
     )
     prepared = call(
-        contact_own, operands, [SM, SM, VM, VM], [pltpu.SMEM((LIST,), jnp.int32)], flops=10**8
-    )(pairs, tile_count, parts, xo)
+        contact_near, operands, [SM, SM] + [VM] * 4, [pltpu.SMEM((LIST,), jnp.int32)], flops=10**8
+    )(pairs, tile_count, parts, got_ye, got_yo, xo)
     drag, dep, fe, gain, rest = call(
         couple,
         (shape(3, 384, 128), shape(4, 10, 16, 128), shape(D_TILES, 8, 128), shape(*cells), shape(*cells)),
@@ -599,10 +613,10 @@
     *more, chosen = call(
         contact_more,
         (*operands, jax.ShapeDtypeStruct((LIST,), jnp.int32)),
-        [SM, SM] + [VM] * 9,
+        [SM, SM] + [VM] * 7,
         flops=10**8,
-        aliases={7: 0, 8: 1, 9: 2, 10: 3},
-    )(pairs, tile_count, got_xo, got_xe, got_ye, got_yo, fo, *prepared)
+        aliases={5: 0, 6: 1, 7: 2, 8: 3},
+    )(pairs, tile_count, got_xo, got_xe, fo, *prepared)
     load, drag_x, pres_w, gain_w, rest_w, he, ho = call(
         fold_x,
         (

time: 92.5 us -> 90.6 us (0.979)
  the two profiles are of different devices: /device:TPU:54 before, /device:TPU:55 now
where the time goes in v4:
time: 90.6 us; the launch traced here: 90.2 us
  starting transfers between devices  47.3 us (52%)
  Pallas kernels  32.2 us (36%)
  waiting for transfers between devices  5.78 us (6%)
  local copies, waits for them, and re-layouts  3.35 us (4%)
  between operations  1.59 us (2%)
    ppermute x8, starting transfers between devices, swap(): return lax.ppermute(array, axis, pairs_of(first, count, count - 1))  47.3 us
    pallas_call x1, Pallas kernels, body(): call(contact_near, operands, [SM, SM] + [VM] * 4, [pltpu.SMEM((LIST,), jn...  10.9 us
    pallas_call x1, Pallas kernels, body(): call(contact_more, (*operands, jax.ShapeDtypeStruct((LIST,), jnp.int32)),...  9.54 us
    pallas_call x1, Pallas kernels, body(): call(couple, (shape(3, 384, 128), shape(4, 10, 16, 128), shape(D_TILES, 8...  6.48 us
    ppermute x8, waiting for transfers between devices, swap(): return lax.ppermute(array, axis, pairs_of(first, count, count - 1))  5.78 us
    unnamed x28, local copies, waits for them, and re-layouts  3.35 us
    pallas_call x1, Pallas kernels, body(): call(contact_end, (shape(3, 384, 128), operands[3]), [SM] + [VM] * 10 + [...  1.98 us
  transfers between devices with their start and end apart: 8, of which 2 were waited for; matrix products, arithmetic and copies ran while one was open for 0% of the time, Pallas kernels for 25%

profile of v4, /device:TPU:55, one launch (start us, length us, event | category | flops | bytes accessed | tf_op | source)
XLA Modules:
  0.0 90.2 jit_solution(9311016690358326709)
XLA Ops:
  0.6 0.0 copy-start.11
  0.6 0.0 copy-start.13
  0.7 0.0 copy-start
  0.7 1.0 %copy-done = f32[1,1,128,8,128]{4,3,2,1,0:T(8,128)S(1)} copy-done((f32[1,1,128,8,128]{4,3,2,1,0:T(8,128)S(1)}, f32[1,1,128,8,128]{4,3,2,1,0:T(8,128)}, u32[]{:S(2)}) %copy-start) | copy-done | bytes 524312
  1.7 0.0 copy-start.2
  1.7 0.9 copy-done.2
  2.6 0.0 copy-start.10
  2.6 0.7 copy-done.10
  3.3 0.0 copy-start.3
  3.3 0.0 copy-start.4
  3.3 0.0 copy-start.7
  3.3 0.0 copy-start.8
  3.3 0.0 copy-start.9
  3.3 0.0 copy-start.12
  3.3 0.7 shard_map.139
  4.1 0.0 copy-start.6
  4.1 2.6 %collective-permute-start = (f32[43,8,128]{2,1,0:T(8,128)S(1)}, f32[43,8,128]{2,1,0:T(8,128)S(1)}, u32[]{:S(2)}, u32[]{:S(2)}) collective-permute-start(f32[43,8,128]{2,1,0:T(8,128)S(1)} %get-tuple-element.31), channel_id=1, source_target_pairs={{0,1},{2,3},{4,5},{6,7},{8,9},{10,11},{12,13},{14,15},{1,0},{3,2},... | collective-permute-start | bytes 528392 | tf_op jit(solution)/shard_map/ppermute | solution.py:550
  6.7 3.4 %collective-permute-start.1 = (f32[43,8,128]{2,1,0:T(8,128)S(1)}, f32[43,8,128]{2,1,0:T(8,128)S(1)}, u32[]{:S(2)}, u32[]{:S(2)}) collective-permute-start(f32[43,8,128]{2,1,0:T(8,128)S(1)} %get-tuple-element.32), channel_id=1, source_target_pairs={{1,2},{3,4},{5,6},{7,8},{9,10},{11,12},{13,14},{2,1},{4,3},{6,5},{... | collective-permute-start | bytes 528392 | tf_op jit(solution)/shard_map/ppermute | solution.py:550
  10.1 0.0 collective-permute-done.in_e.in_ye
  10.1 3.3 %collective-permute-done.1.in_o.in_yo = f32[43,8,128]{2,1,0:T(8,128)S(1)} collective-permute-done((f32[43,8,128]{2,1,0:T(8,128)S(1)}, f32[43,8,128]{2,1,0:T(8,128)S(1)}, u32[]{:S(2)}, u32[]{:S(2)}) %collective-permute-start.1) | collective-permute-done | bytes 176160 | tf_op jit(solution)/shard_map/ppermute | solution.py:550
  13.4 0.7 shard_map.140
  14.1 0.7 shard_map.141.after
  14.8 2.1 %collective-permute-start.2 = (f32[46,8,128]{2,1,0:T(8,128)S(1)}, f32[46,8,128]{2,1,0:T(8,128)S(1)}, u32[]{:S(2)}, u32[]{:S(2)}) collective-permute-start(f32[46,8,128]{2,1,0:T(8,128)S(1)} %shard_map.141.after), channel_id=1, source_target_pairs={{16,32},{48,64},{80,96},{112,128},{144,160},{176,192},{208,224},{2... | collective-permute-start | bytes 565256 | tf_op jit(solution)/shard_map/ppermute | solution.py:550
  16.8 15.0 %collective-permute-start.3 = (f32[46,8,128]{2,1,0:T(8,128)S(1)}, f32[46,8,128]{2,1,0:T(8,128)S(1)}, u32[]{:S(2)}, u32[]{:S(2)}) collective-permute-start(f32[46,8,128]{2,1,0:T(8,128)S(1)} %get-tuple-element.34), channel_id=1, source_target_pairs={{0,16},{32,48},{64,80},{96,112},{128,144},{160,176},{192,208},{224... | collective-permute-start | bytes 565256 | tf_op jit(solution)/shard_map/ppermute | solution.py:550
  32.5 0.0 copy-start.5
  32.5 0.7 copy-done.5
  33.1 10.9 %shard_map.142 = (bf16[96,128,128]{2,1,0:T(8,128)(2,1)S(1)}, bf16[384,16,128]{2,1,0:T(8,128)(2,1)S(1)}, bf16[192,32,256]{2,1,0:T(8,128)(2,1)S(1)}, f32[192,8,128]{2,1,0:T(8,128)S(1)}) custom-call(s32[2,512]{1,0:T(2,128)S(1)} %bitcast.20, s32[1,1]{1,0:T(1,128)S(6)} %copy.25.total_ref, f32[128,8,128]{2,1,0:T(8,128)S(1)} %bitcast.16, ...), custom_call_target="tpu_custom_call" | custom-call | flops 100000000 | bytes 1000000 | tf_op jit(solution)/shard_map/pallas_call | solution.py:589
  44.1 0.0 collective-permute-done.2.in_xo
  44.1 0.0 collective-permute-done.3.in_xe
  44.1 0.0 copy-done.11
  44.1 0.0 copy-done.13
  44.1 0.0 copy-done.3
  44.1 0.0 copy-done.4
  44.1 0.0 copy-done.7
  44.1 0.0 copy-done.8
  44.2 0.0 copy-done.9
  44.2 0.0 copy-done.12
  44.2 6.5 %shard_map.143 = (f32[3,384,128]{2,1,0:T(8,128)S(1)}, f32[4,10,16,128]{3,2,1,0:T(8,128)S(1)}, f32[24,8,128]{2,1,0:T(8,128)S(1)}, f32[8,8,128]{2,1,0:T(8,128)S(1)}, f32[8,8,128]{2,1,0:T(8,128)S(1)}) custom-call(f32[128,8,128]{2,1,0:T(8,128)S(1)} %bitcast.17, s32[4,64]{1,0:T(4,128)S(1)} %bitcast.26, s32[2,4]{1,0:T(2,128)S(1)} %bitcast.28, ...), custom_call_target="tpu_custom_call" | custom-call | flops 1000000 | bytes 1000000 | tf_op jit(solution)/shard_map/pallas_call | solution.py:592
  50.7 1.9 %collective-permute-start.4 = (f32[24,8,128]{2,1,0:T(8,128)S(1)}, f32[24,8,128]{2,1,0:T(8,128)S(1)}, u32[]{:S(2)}, u32[]{:S(2)}) collective-permute-start(f32[24,8,128]{2,1,0:T(8,128)S(1)} %shard_map.144.after), channel_id=1, source_target_pairs={{16,32},{48,64},{80,96},{112,128},{144,160},{176,192},{208,224},{2... | collective-permute-start | bytes 294920 | tf_op jit(solution)/shard_map/ppermute | solution.py:550
  52.6 17.1 %collective-permute-start.5 = (f32[24,8,128]{2,1,0:T(8,128)S(1)}, f32[24,8,128]{2,1,0:T(8,128)S(1)}, u32[]{:S(2)}, u32[]{:S(2)}) collective-permute-start(f32[24,8,128]{2,1,0:T(8,128)S(1)} %get-tuple-element.39), channel_id=1, source_target_pairs={{0,16},{32,48},{64,80},{96,112},{128,144},{160,176},{192,208},{224... | collective-permute-start | bytes 294920 | tf_op jit(solution)/shard_map/ppermute | solution.py:550
  69.7 0.0 copy-done.6
  69.7 0.0 copy-start.1
  69.7 9.5 %shard_map.145 = (bf16[96,128,128]{2,1,0:T(8,128)(2,1)S(1)}, bf16[384,16,128]{2,1,0:T(8,128)(2,1)S(1)}, bf16[192,32,256]{2,1,0:T(8,128)(2,1)S(1)}, f32[192,8,128]{2,1,0:T(8,128)S(1)}, s32[640]{0:T(1024)S(1)}) custom-call(s32[2,512]{1,0:T(2,128)S(1)} %bitcast.21, ...), custom_call_target="tpu_custom_call", output_to_operand_aliasing={{0}: (5, {}), {1}: (6, {}), {2}: (7, {}), {3}: (8, {})} | custom-call | flops 100000000 | bytes 1000000 | tf_op jit(solution)/shard_map/pallas_call | solution.py:613
  79.3 0.0 collective-permute-done.4.in_o
  79.3 0.0 collective-permute-done.5.in_e
  79.3 0.1 shard_map.146
  79.4 3.3 %collective-permute-start.6 = (f32[34,8,128]{2,1,0:T(8,128)S(1)}, f32[34,8,128]{2,1,0:T(8,128)S(1)}, u32[]{:S(2)}, u32[]{:S(2)}) collective-permute-start(f32[34,8,128]{2,1,0:T(8,128)S(1)} %get-tuple-element.49), channel_id=1, source_target_pairs={{0,1},{2,3},{4,5},{6,7},{8,9},{10,11},{12,13},{14,15},{1,0},{3,2},... | collective-permute-start | bytes 417800 | tf_op jit(solution)/shard_map/ppermute | solution.py:550
  82.7 1.9 %collective-permute-start.7 = (f32[34,8,128]{2,1,0:T(8,128)S(1)}, f32[34,8,128]{2,1,0:T(8,128)S(1)}, u32[]{:S(2)}, u32[]{:S(2)}) collective-permute-start(f32[34,8,128]{2,1,0:T(8,128)S(1)} %get-tuple-element.50.after), channel_id=1, source_target_pairs={{1,2},{3,4},{5,6},{7,8},{9,10},{11,12},{13,14},{2,1},{4,3},{6,5},{... | collective-permute-start | bytes 417800 | tf_op jit(solution)/shard_map/ppermute | solution.py:550
  84.7 0.0 copy-done.1
  84.7 2.0 %shard_map.148 = (f32[3,384,128]{2,1,0:T(8,128)}, f32[192,8,128]{2,1,0:T(8,128)S(1)}) custom-call(s32[2,512]{1,0:T(2,128)S(1)} %bitcast.22, f32[128,8,128]{2,1,0:T(8,128)S(1)} %bitcast.18, f32[46,8,128]{2,1,0:T(8,128)S(1)} %collective-permute-done.2.in_xo, f32[46,8,128]{2,1,0:T(8,128)S(1)} %collective-permute-done.3.in_xe, ...), custom_call_target="tpu_custom_call", output_to_operand_aliasing={{1}: (12, {})} | custom-call | flops 1000000000 | bytes 1000000 | tf_op jit(solution)/shard_map/pallas_call | solution.py:630
  86.7 0.0 collective-permute-done.6.in_e
  86.7 2.5 %collective-permute-done.7.in_o = f32[34,8,128]{2,1,0:T(8,128)S(1)} collective-permute-done((f32[34,8,128]{2,1,0:T(8,128)S(1)}, f32[34,8,128]{2,1,0:T(8,128)S(1)}, u32[]{:S(2)}, u32[]{:S(2)}) %collective-permute-start.7) | collective-permute-done | bytes 139296 | tf_op jit(solution)/shard_map/ppermute | solution.py:550
  89.1 1.0 %shard_map.147 = (f32[8,8,128]{2,1,0:T(8,128)}, f32[3,8,8,128]{3,2,1,0:T(8,128)}) custom-call(f32[16,16,128]{2,1,0:T(8,128)S(1)} %get-tuple-element.44.load, f32[3,8,16,128]{3,2,1,0:T(8,128)S(1)} %get-tuple-element.45.drag, f32[16,8,128]{2,1,0:T(8,128)S(1)} %get-tuple-element.46.pres_w, f32[16,8,128]{2,1,0:T(8,128)S(1)} %get-tuple-element.47.gain_w, ...), custom_call_target="tpu_custom_call" | custom-call | flops 1000000 | bytes 1000000 | tf_op jit(solution)/shard_map/pallas_call | solution.py:637
  (1 shorter events, 0.0 us)
Async XLA Ops:
  0.6 43.5 %copy-start.11 = (s32[1,1,4,64]{3,2,1,0:T(4,128)S(1)}, s32[1,1,4,64]{3,2,1,0:T(4,128)}, u32[]{:S(2)}) copy-start(s32[1,1,4,64]{3,2,1,0:T(4,128)} %param.13) | copy-start | bytes 3076
  0.6 43.5 %copy-start.13 = (s32[1,1,2,4]{3,2,1,0:T(2,128)S(1)}, s32[1,1,2,4]{3,2,1,0:T(2,128)}, u32[]{:S(2)}) copy-start(s32[1,1,2,4]{3,2,1,0:T(2,128)} %param.14) | copy-start | bytes 100
  0.7 1.1 %copy-start = (f32[1,1,128,8,128]{4,3,2,1,0:T(8,128)S(1)}, f32[1,1,128,8,128]{4,3,2,1,0:T(8,128)}, u32[]{:S(2)}) copy-start(f32[1,1,128,8,128]{4,3,2,1,0:T(8,128)} %param.12) | copy-start | bytes 1572868
  1.7 0.9 copy-start.2
  2.6 0.7 copy-start.10
  3.3 40.8 %copy-start.3 = (f32[8,8,128]{2,1,0:T(8,128)S(1)}, f32[8,8,128]{2,1,0:T(8,128)}, u32[]{:S(2)}) copy-start(f32[8,8,128]{2,1,0:T(8,128)} %pres.5) | copy-start | bytes 98308
  3.3 40.8 %copy-start.4 = (s32[1,1,384,128]{3,2,1,0:T(8,128)S(1)}, s32[1,1,384,128]{3,2,1,0:T(8,128)}, u32[]{:S(2)}) copy-start(s32[1,1,384,128]{3,2,1,0:T(8,128)} %param.18) | copy-start | bytes 589828
  3.3 40.9 %copy-start.7 = (f32[8,8,128]{2,1,0:T(8,128)S(1)}, f32[8,8,128]{2,1,0:T(8,128)}, u32[]{:S(2)}) copy-start(f32[8,8,128]{2,1,0:T(8,128)} %screen.1) | copy-start | bytes 98308
  3.3 40.9 %copy-start.8 = (f32[8,8,128]{2,1,0:T(8,128)S(1)}, f32[8,8,128]{2,1,0:T(8,128)}, u32[]{:S(2)}) copy-start(f32[8,8,128]{2,1,0:T(8,128)} %source.1) | copy-start | bytes 98308
  3.3 40.9 %copy-start.9 = (f32[8,8,128]{2,1,0:T(8,128)S(1)}, f32[8,8,128]{2,1,0:T(8,128)}, u32[]{:S(2)}) copy-start(f32[8,8,128]{2,1,0:T(8,128)} %solid.1) | copy-start | bytes 98308
  3.3 40.9 %copy-start.12 = (s32[1,1,384,4]{2,3,1,0:T(4,128)S(1)}, s32[1,1,384,4]{2,3,1,0:T(4,128)}, u32[]{:S(2)}) copy-start(s32[1,1,384,4]{2,3,1,0:T(4,128)} %param.17) | copy-start | bytes 18436
  4.1 65.7 %copy-start.6 = (s32[1,1,512,2]{2,3,1,0:T(2,128)S(1)}, s32[1,1,512,2]{2,3,1,0:T(2,128)}, u32[]{:S(2)}) copy-start(s32[1,1,512,2]{2,3,1,0:T(2,128)} %param.15) | copy-start | bytes 12292
  4.1 6.0 %collective-permute-start = (f32[43,8,128]{2,1,0:T(8,128)S(1)}, f32[43,8,128]{2,1,0:T(8,128)S(1)}, u32[]{:S(2)}, u32[]{:S(2)}) collective-permute-start(f32[43,8,128]{2,1,0:T(8,128)S(1)} %get-tuple-element.31), channel_id=1, source_target_pairs={{0,1},{2,3},{4,5},{6,7},{8,9},{10,11},{12,13},{14,15},{1,0},{3,2},... | collective-permute-start | bytes 528392 | tf_op jit(solution)/shard_map/ppermute | solution.py:550
  6.7 6.8 %collective-permute-start.1 = (f32[43,8,128]{2,1,0:T(8,128)S(1)}, f32[43,8,128]{2,1,0:T(8,128)S(1)}, u32[]{:S(2)}, u32[]{:S(2)}) collective-permute-start(f32[43,8,128]{2,1,0:T(8,128)S(1)} %get-tuple-element.32), channel_id=1, source_target_pairs={{1,2},{3,4},{5,6},{7,8},{9,10},{11,12},{13,14},{2,1},{4,3},{6,5},{... | collective-permute-start | bytes 528392 | tf_op jit(solution)/shard_map/ppermute | solution.py:550
  14.8 29.3 %collective-permute-start.2 = (f32[46,8,128]{2,1,0:T(8,128)S(1)}, f32[46,8,128]{2,1,0:T(8,128)S(1)}, u32[]{:S(2)}, u32[]{:S(2)}) collective-permute-start(f32[46,8,128]{2,1,0:T(8,128)S(1)} %shard_map.141.after), channel_id=1, source_target_pairs={{16,32},{48,64},{80,96},{112,128},{144,160},{176,192},{208,224},{2... | collective-permute-start | bytes 565256 | tf_op jit(solution)/shard_map/ppermute | solution.py:550
  16.8 27.2 %collective-permute-start.3 = (f32[46,8,128]{2,1,0:T(8,128)S(1)}, f32[46,8,128]{2,1,0:T(8,128)S(1)}, u32[]{:S(2)}, u32[]{:S(2)}) collective-permute-start(f32[46,8,128]{2,1,0:T(8,128)S(1)} %get-tuple-element.34), channel_id=1, source_target_pairs={{0,16},{32,48},{64,80},{96,112},{128,144},{160,176},{192,208},{224... | collective-permute-start | bytes 565256 | tf_op jit(solution)/shard_map/ppermute | solution.py:550
  32.5 0.7 copy-start.5
  50.7 28.6 %collective-permute-start.4 = (f32[24,8,128]{2,1,0:T(8,128)S(1)}, f32[24,8,128]{2,1,0:T(8,128)S(1)}, u32[]{:S(2)}, u32[]{:S(2)}) collective-permute-start(f32[24,8,128]{2,1,0:T(8,128)S(1)} %shard_map.144.after), channel_id=1, source_target_pairs={{16,32},{48,64},{80,96},{112,128},{144,160},{176,192},{208,224},{2... | collective-permute-start | bytes 294920 | tf_op jit(solution)/shard_map/ppermute | solution.py:550
  52.6 26.7 %collective-permute-start.5 = (f32[24,8,128]{2,1,0:T(8,128)S(1)}, f32[24,8,128]{2,1,0:T(8,128)S(1)}, u32[]{:S(2)}, u32[]{:S(2)}) collective-permute-start(f32[24,8,128]{2,1,0:T(8,128)S(1)} %get-tuple-element.39), channel_id=1, source_target_pairs={{0,16},{32,48},{64,80},{96,112},{128,144},{160,176},{192,208},{224... | collective-permute-start | bytes 294920 | tf_op jit(solution)/shard_map/ppermute | solution.py:550
  69.7 14.9 %copy-start.1 = (f32[1,1,128,8,128]{4,3,2,1,0:T(8,128)S(1)}, f32[1,1,128,8,128]{4,3,2,1,0:T(8,128)}, u32[]{:S(2)}) copy-start(f32[1,1,128,8,128]{4,3,2,1,0:T(8,128)} %param.12) | copy-start | bytes 1572868
  79.4 7.2 %collective-permute-start.6 = (f32[34,8,128]{2,1,0:T(8,128)S(1)}, f32[34,8,128]{2,1,0:T(8,128)S(1)}, u32[]{:S(2)}, u32[]{:S(2)}) collective-permute-start(f32[34,8,128]{2,1,0:T(8,128)S(1)} %get-tuple-element.49), channel_id=1, source_target_pairs={{0,1},{2,3},{4,5},{6,7},{8,9},{10,11},{12,13},{14,15},{1,0},{3,2},... | collective-permute-start | bytes 417800 | tf_op jit(solution)/shard_map/ppermute | solution.py:550
  82.7 6.4 %collective-permute-start.7 = (f32[34,8,128]{2,1,0:T(8,128)S(1)}, f32[34,8,128]{2,1,0:T(8,128)S(1)}, u32[]{:S(2)}, u32[]{:S(2)}) collective-permute-start(f32[34,8,128]{2,1,0:T(8,128)S(1)} %get-tuple-element.50.after), channel_id=1, source_target_pairs={{1,2},{3,4},{5,6},{7,8},{9,10},{11,12},{13,14},{2,1},{4,3},{6,5},{... | collective-permute-start | bytes 417800 | tf_op jit(solution)/shard_map/ppermute | solution.py:550

commit v5 on v4

--- a/solution.py
+++ b/solution.py
@@ -104,10 +104,12 @@
 def couple(
     parts, sends_in, moves_in, tiles_in, slots, flow_x, in_xo, in_xe, in_ye, in_yo, after,
     pres, screen, source, solid,
-    drag, dep, out_e, gain, rest,
+    drag, dep, out_o, gain, rest,
     pool, table, sums, owned, sends, moves, tiles, sems,
 ):
     copies = fetch((sends_in, moves_in, tiles_in), (sends, moves, tiles), sems)
+    for k in range(NB):
+        owned[k] = 1.0
     x_even = lax.axis_index("gx") % 2 == 0
     y_even = lax.axis_index("gy") % 2 == 0
     pool[0:NB] = parts[...]
@@ -136,11 +138,6 @@
     for copy in copies:
         copy.wait()
 
-    def stay(k, carry):
-        owned[k] = 1.0
-        return carry
-
-    lax.fori_loop(0, NB, stay, 0)
     for d in range(4):
 
         def leave(s, carry, d=d):
@@ -215,7 +212,7 @@
             dep[f, n // 10, n % 10 + 3, :] = total[f]
     gain[...] = 1.0 / (6.0 + screen[...])
     rest[...] = source[...] - 2.0 * solid[...]
-    put_rims(dep, pres, gain, rest, x_even, out_e)
+    put_rims(dep, pres, gain, rest, jnp.logical_not(x_even), out_o)
 
 
 P_AT = 14
@@ -239,8 +236,8 @@
             out[at + r] = ref[start + r]
 
 
-def pack_fo(dep, pres, gain, rest, out):
-    put_rims(dep, pres, gain, rest, lax.axis_index("gx") % 2 == 1, out)
+def pack_fe(dep, pres, gain, rest, out):
+    put_rims(dep, pres, gain, rest, lax.axis_index("gx") % 2 == 0, out)
 
 
 H_DRAG = 7
@@ -589,7 +586,7 @@
     prepared = call(
         contact_near, operands, [SM, SM] + [VM] * 4, [pltpu.SMEM((LIST,), jnp.int32)], flops=10**8
     )(pairs, tile_count, parts, got_ye, got_yo, xo)
-    drag, dep, fe, gain, rest = call(
+    drag, dep, fo, gain, rest = call(
         couple,
         (shape(3, 384, 128), shape(4, 10, 16, 128), shape(D_TILES, 8, 128), shape(*cells), shape(*cells)),
         [VM, HB, HB, HB] + [VM] * 11,
@@ -607,16 +604,16 @@
         parts, sends, moves, tiles, slots, flow_x, got_xo, got_xe, got_ye, got_yo, prepared[3],
         pressure_init, screening, source, solid_old,
     )
+    got_fo = swap(fo, "gx", 1)
+    fe = call(pack_fe, shape(D_TILES, 8, 128), [VM] * 4)(dep, pressure_init, gain, rest)
     got_fe = swap(fe, "gx", 0)
-    fo = call(pack_fo, shape(D_TILES, 8, 128), [VM] * 4)(dep, pressure_init, gain, rest)
-    got_fo = swap(fo, "gx", 1)
     *more, chosen = call(
         contact_more,
         (*operands, jax.ShapeDtypeStruct((LIST,), jnp.int32)),
         [SM, SM] + [VM] * 7,
         flops=10**8,
         aliases={5: 0, 6: 1, 7: 2, 8: 3},
-    )(pairs, tile_count, got_xo, got_xe, fo, *prepared)
+    )(pairs, tile_count, got_xo, got_xe, fe, *prepared)
     load, drag_x, pres_w, gain_w, rest_w, he, ho = call(
         fold_x,
         (

time: 90.6 us -> 90 us (level)
  the two profiles are of different devices: /device:TPU:55 before, /device:TPU:63 now
where the time goes in v5:
time: 90 us; the launch traced here: 89.6 us
  starting transfers between devices  40.5 us (45%)
  Pallas kernels  32.8 us (36%)
  waiting for transfers between devices  11.4 us (13%)
  local copies, waits for them, and re-layouts  3.35 us (4%)
  between operations  1.55 us (2%)
    ppermute x8, starting transfers between devices, swap(): return lax.ppermute(array, axis, pairs_of(first, count, count - 1))  40.5 us
    ppermute x8, waiting for transfers between devices, swap(): return lax.ppermute(array, axis, pairs_of(first, count, count - 1))  11.4 us
    pallas_call x1, Pallas kernels, body(): call(contact_near, operands, [SM, SM] + [VM] * 4, [pltpu.SMEM((LIST,), jn...  10.9 us
    pallas_call x1, Pallas kernels, body(): call(contact_more, (*operands, jax.ShapeDtypeStruct((LIST,), jnp.int32)),...  9.54 us
    pallas_call x1, Pallas kernels, body(): call(couple, (shape(3, 384, 128), shape(4, 10, 16, 128), shape(D_TILES, 8...  5.76 us
    pallas_call x1, Pallas kernels, body(): call(contact_end, (shape(3, 384, 128), operands[3]), [SM] + [VM] * 10 + [...  3.38 us
    unnamed x28, local copies, waits for them, and re-layouts  3.35 us
  transfers between devices with their start and end apart: 8, of which 4 were waited for; matrix products, arithmetic and copies ran while one was open for 0% of the time, Pallas kernels for 27%

profile of v5, /device:TPU:63, one launch (start us, length us, event | category | flops | bytes accessed | tf_op | source)
XLA Modules:
  0.0 89.6 jit_solution(12587270555640917854)
XLA Ops:
  0.6 0.0 copy-start.11
  0.6 0.0 copy-start.13
  0.7 0.0 copy-start
  0.7 1.0 %copy-done = f32[1,1,128,8,128]{4,3,2,1,0:T(8,128)S(1)} copy-done((f32[1,1,128,8,128]{4,3,2,1,0:T(8,128)S(1)}, f32[1,1,128,8,128]{4,3,2,1,0:T(8,128)}, u32[]{:S(2)}) %copy-start) | copy-done | bytes 524312
  1.7 0.0 copy-start.2
  1.7 0.9 copy-done.2
  2.6 0.0 copy-start.10
  2.6 0.7 copy-done.10
  3.3 0.0 copy-start.3
  3.3 0.0 copy-start.4
  3.3 0.0 copy-start.7
  3.3 0.0 copy-start.8
  3.3 0.0 copy-start.9
  3.3 0.0 copy-start.12
  3.3 0.7 shard_map.139
  4.1 0.0 copy-start.6
  4.1 2.6 %collective-permute-start = (f32[43,8,128]{2,1,0:T(8,128)S(1)}, f32[43,8,128]{2,1,0:T(8,128)S(1)}, u32[]{:S(2)}, u32[]{:S(2)}) collective-permute-start(f32[43,8,128]{2,1,0:T(8,128)S(1)} %get-tuple-element.31), channel_id=1, source_target_pairs={{0,1},{2,3},{4,5},{6,7},{8,9},{10,11},{12,13},{14,15},{1,0},{3,2},... | collective-permute-start | bytes 528392 | tf_op jit(solution)/shard_map/ppermute | solution.py:547
  6.7 3.4 %collective-permute-start.1 = (f32[43,8,128]{2,1,0:T(8,128)S(1)}, f32[43,8,128]{2,1,0:T(8,128)S(1)}, u32[]{:S(2)}, u32[]{:S(2)}) collective-permute-start(f32[43,8,128]{2,1,0:T(8,128)S(1)} %get-tuple-element.32), channel_id=1, source_target_pairs={{1,2},{3,4},{5,6},{7,8},{9,10},{11,12},{13,14},{2,1},{4,3},{6,5},{... | collective-permute-start | bytes 528392 | tf_op jit(solution)/shard_map/ppermute | solution.py:547
  10.1 0.0 collective-permute-done.in_e.in_ye
  10.1 3.3 %collective-permute-done.1.in_o.in_yo = f32[43,8,128]{2,1,0:T(8,128)S(1)} collective-permute-done((f32[43,8,128]{2,1,0:T(8,128)S(1)}, f32[43,8,128]{2,1,0:T(8,128)S(1)}, u32[]{:S(2)}, u32[]{:S(2)}) %collective-permute-start.1) | collective-permute-done | bytes 176160 | tf_op jit(solution)/shard_map/ppermute | solution.py:547
  13.4 0.7 shard_map.140
  14.1 0.7 shard_map.141.after
  14.8 14.1 %collective-permute-start.2 = (f32[46,8,128]{2,1,0:T(8,128)S(1)}, f32[46,8,128]{2,1,0:T(8,128)S(1)}, u32[]{:S(2)}, u32[]{:S(2)}) collective-permute-start(f32[46,8,128]{2,1,0:T(8,128)S(1)} %shard_map.141.after), channel_id=1, source_target_pairs={{16,32},{48,64},{80,96},{112,128},{144,160},{176,192},{208,224},{2... | collective-permute-start | bytes 565256 | tf_op jit(solution)/shard_map/ppermute | solution.py:547
  28.9 1.9 %collective-permute-start.3 = (f32[46,8,128]{2,1,0:T(8,128)S(1)}, f32[46,8,128]{2,1,0:T(8,128)S(1)}, u32[]{:S(2)}, u32[]{:S(2)}) collective-permute-start(f32[46,8,128]{2,1,0:T(8,128)S(1)} %get-tuple-element.34), channel_id=1, source_target_pairs={{0,16},{32,48},{64,80},{96,112},{128,144},{160,176},{192,208},{224... | collective-permute-start | bytes 565256 | tf_op jit(solution)/shard_map/ppermute | solution.py:547
  31.5 0.0 copy-start.5
  31.5 0.7 copy-done.5
  32.2 10.9 %shard_map.142 = (bf16[96,128,128]{2,1,0:T(8,128)(2,1)S(1)}, bf16[384,16,128]{2,1,0:T(8,128)(2,1)S(1)}, bf16[192,32,256]{2,1,0:T(8,128)(2,1)S(1)}, f32[192,8,128]{2,1,0:T(8,128)S(1)}) custom-call(s32[2,512]{1,0:T(2,128)S(1)} %bitcast.20, s32[1,1]{1,0:T(1,128)S(6)} %copy.25.total_ref, f32[128,8,128]{2,1,0:T(8,128)S(1)} %bitcast.16, ...), custom_call_target="tpu_custom_call" | custom-call | flops 100000000 | bytes 1000000 | tf_op jit(solution)/shard_map/pallas_call | solution.py:586
  43.1 5.0 %collective-permute-done.2.in_xo = f32[46,8,128]{2,1,0:T(8,128)S(1)} collective-permute-done((f32[46,8,128]{2,1,0:T(8,128)S(1)}, f32[46,8,128]{2,1,0:T(8,128)S(1)}, u32[]{:S(2)}, u32[]{:S(2)}) %collective-permute-start.2) | collective-permute-done | bytes 188448 | tf_op jit(solution)/shard_map/ppermute | solution.py:547
  48.0 0.0 collective-permute-done.3.in_xe
  48.0 0.0 copy-done.11
  48.1 0.0 copy-done.13
  48.1 0.0 copy-done.3
  48.1 0.0 copy-done.4
  48.1 0.0 copy-done.7
  48.1 0.0 copy-done.8
  48.1 0.0 copy-done.9
  48.1 0.0 copy-done.12
  48.1 5.8 %shard_map.143 = (f32[3,384,128]{2,1,0:T(8,128)S(1)}, f32[4,10,16,128]{3,2,1,0:T(8,128)S(1)}, f32[24,8,128]{2,1,0:T(8,128)S(1)}, f32[8,8,128]{2,1,0:T(8,128)S(1)}, f32[8,8,128]{2,1,0:T(8,128)S(1)}) custom-call(f32[128,8,128]{2,1,0:T(8,128)S(1)} %bitcast.17, s32[4,64]{1,0:T(4,128)S(1)} %bitcast.26, s32[2,4]{1,0:T(2,128)S(1)} %bitcast.28, ...), custom_call_target="tpu_custom_call" | custom-call | flops 1000000 | bytes 1000000 | tf_op jit(solution)/shard_map/pallas_call | solution.py:589
  53.9 1.9 %collective-permute-start.5 = (f32[24,8,128]{2,1,0:T(8,128)S(1)}, f32[24,8,128]{2,1,0:T(8,128)S(1)}, u32[]{:S(2)}, u32[]{:S(2)}) collective-permute-start(f32[24,8,128]{2,1,0:T(8,128)S(1)} %shard_map.144.after), channel_id=1, source_target_pairs={{0,16},{32,48},{64,80},{96,112},{128,144},{160,176},{192,208},{224... | collective-permute-start | bytes 294920 | tf_op jit(solution)/shard_map/ppermute | solution.py:547
  55.8 12.2 %collective-permute-start.4 = (f32[24,8,128]{2,1,0:T(8,128)S(1)}, f32[24,8,128]{2,1,0:T(8,128)S(1)}, u32[]{:S(2)}, u32[]{:S(2)}) collective-permute-start(f32[24,8,128]{2,1,0:T(8,128)S(1)} %get-tuple-element.39), channel_id=1, source_target_pairs={{16,32},{48,64},{80,96},{112,128},{144,160},{176,192},{208,224},{2... | collective-permute-start | bytes 294920 | tf_op jit(solution)/shard_map/ppermute | solution.py:547
  68.0 0.0 copy-done.6
  68.0 0.0 copy-start.1
  68.0 9.5 %shard_map.145 = (bf16[96,128,128]{2,1,0:T(8,128)(2,1)S(1)}, bf16[384,16,128]{2,1,0:T(8,128)(2,1)S(1)}, bf16[192,32,256]{2,1,0:T(8,128)(2,1)S(1)}, f32[192,8,128]{2,1,0:T(8,128)S(1)}, s32[640]{0:T(1024)S(1)}) custom-call(s32[2,512]{1,0:T(2,128)S(1)} %bitcast.21, ...), custom_call_target="tpu_custom_call", output_to_operand_aliasing={{0}: (5, {}), {1}: (6, {}), {2}: (7, {}), {3}: (8, {})} | custom-call | flops 100000000 | bytes 1000000 | tf_op jit(solution)/shard_map/pallas_call | solution.py:610
  77.6 0.0 collective-permute-done.5.in_e
  77.6 2.1 %collective-permute-done.4.in_o = f32[24,8,128]{2,1,0:T(8,128)S(1)} collective-permute-done((f32[24,8,128]{2,1,0:T(8,128)S(1)}, f32[24,8,128]{2,1,0:T(8,128)S(1)}, u32[]{:S(2)}, u32[]{:S(2)}) %collective-permute-start.4) | collective-permute-done | bytes 98336 | tf_op jit(solution)/shard_map/ppermute | solution.py:547
  79.7 0.1 shard_map.146
  79.8 2.4 %collective-permute-start.6 = (f32[34,8,128]{2,1,0:T(8,128)S(1)}, f32[34,8,128]{2,1,0:T(8,128)S(1)}, u32[]{:S(2)}, u32[]{:S(2)}) collective-permute-start(f32[34,8,128]{2,1,0:T(8,128)S(1)} %get-tuple-element.49), channel_id=1, source_target_pairs={{0,1},{2,3},{4,5},{6,7},{8,9},{10,11},{12,13},{14,15},{1,0},{3,2},... | collective-permute-start | bytes 417800 | tf_op jit(solution)/shard_map/ppermute | solution.py:547
  82.2 1.9 %collective-permute-start.7 = (f32[34,8,128]{2,1,0:T(8,128)S(1)}, f32[34,8,128]{2,1,0:T(8,128)S(1)}, u32[]{:S(2)}, u32[]{:S(2)}) collective-permute-start(f32[34,8,128]{2,1,0:T(8,128)S(1)} %get-tuple-element.50.after), channel_id=1, source_target_pairs={{1,2},{3,4},{5,6},{7,8},{9,10},{11,12},{13,14},{2,1},{4,3},{6,5},{... | collective-permute-start | bytes 417800 | tf_op jit(solution)/shard_map/ppermute | solution.py:547
  84.1 0.0 copy-done.1
  84.1 3.4 %shard_map.148 = (f32[3,384,128]{2,1,0:T(8,128)}, f32[192,8,128]{2,1,0:T(8,128)S(1)}) custom-call(s32[2,512]{1,0:T(2,128)S(1)} %bitcast.22, f32[128,8,128]{2,1,0:T(8,128)S(1)} %bitcast.18, f32[46,8,128]{2,1,0:T(8,128)S(1)} %collective-permute-done.2.in_xo, f32[46,8,128]{2,1,0:T(8,128)S(1)} %collective-permute-done.3.in_xe, ...), custom_call_target="tpu_custom_call", output_to_operand_aliasing={{1}: (12, {})} | custom-call | flops 1000000000 | bytes 1000000 | tf_op jit(solution)/shard_map/pallas_call | solution.py:627
  87.5 0.0 collective-permute-done.6.in_e
  87.5 1.0 %collective-permute-done.7.in_o = f32[34,8,128]{2,1,0:T(8,128)S(1)} collective-permute-done((f32[34,8,128]{2,1,0:T(8,128)S(1)}, f32[34,8,128]{2,1,0:T(8,128)S(1)}, u32[]{:S(2)}, u32[]{:S(2)}) %collective-permute-start.7) | collective-permute-done | bytes 139296 | tf_op jit(solution)/shard_map/ppermute | solution.py:547
  88.6 1.0 %shard_map.147 = (f32[8,8,128]{2,1,0:T(8,128)}, f32[3,8,8,128]{3,2,1,0:T(8,128)}) custom-call(f32[16,16,128]{2,1,0:T(8,128)S(1)} %get-tuple-element.44.load, f32[3,8,16,128]{3,2,1,0:T(8,128)S(1)} %get-tuple-element.45.drag, f32[16,8,128]{2,1,0:T(8,128)S(1)} %get-tuple-element.46.pres_w, f32[16,8,128]{2,1,0:T(8,128)S(1)} %get-tuple-element.47.gain_w, ...), custom_call_target="tpu_custom_call" | custom-call | flops 1000000 | bytes 1000000 | tf_op jit(solution)/shard_map/pallas_call | solution.py:634
  (1 shorter events, 0.0 us)
Async XLA Ops:
  0.6 47.4 %copy-start.11 = (s32[1,1,4,64]{3,2,1,0:T(4,128)S(1)}, s32[1,1,4,64]{3,2,1,0:T(4,128)}, u32[]{:S(2)}) copy-start(s32[1,1,4,64]{3,2,1,0:T(4,128)} %param.13) | copy-start | bytes 3076
  0.6 47.4 %copy-start.13 = (s32[1,1,2,4]{3,2,1,0:T(2,128)S(1)}, s32[1,1,2,4]{3,2,1,0:T(2,128)}, u32[]{:S(2)}) copy-start(s32[1,1,2,4]{3,2,1,0:T(2,128)} %param.14) | copy-start | bytes 100
  0.7 1.1 %copy-start = (f32[1,1,128,8,128]{4,3,2,1,0:T(8,128)S(1)}, f32[1,1,128,8,128]{4,3,2,1,0:T(8,128)}, u32[]{:S(2)}) copy-start(f32[1,1,128,8,128]{4,3,2,1,0:T(8,128)} %param.12) | copy-start | bytes 1572868
  1.7 0.9 copy-start.2
  2.6 0.7 copy-start.10
  3.3 44.8 %copy-start.3 = (f32[8,8,128]{2,1,0:T(8,128)S(1)}, f32[8,8,128]{2,1,0:T(8,128)}, u32[]{:S(2)}) copy-start(f32[8,8,128]{2,1,0:T(8,128)} %pres.5) | copy-start | bytes 98308
  3.3 44.8 %copy-start.4 = (s32[1,1,384,128]{3,2,1,0:T(8,128)S(1)}, s32[1,1,384,128]{3,2,1,0:T(8,128)}, u32[]{:S(2)}) copy-start(s32[1,1,384,128]{3,2,1,0:T(8,128)} %param.18) | copy-start | bytes 589828
  3.3 44.8 %copy-start.7 = (f32[8,8,128]{2,1,0:T(8,128)S(1)}, f32[8,8,128]{2,1,0:T(8,128)}, u32[]{:S(2)}) copy-start(f32[8,8,128]{2,1,0:T(8,128)} %screen.1) | copy-start | bytes 98308
  3.3 44.8 %copy-start.8 = (f32[8,8,128]{2,1,0:T(8,128)S(1)}, f32[8,8,128]{2,1,0:T(8,128)}, u32[]{:S(2)}) copy-start(f32[8,8,128]{2,1,0:T(8,128)} %source.1) | copy-start | bytes 98308
  3.3 44.8 %copy-start.9 = (f32[8,8,128]{2,1,0:T(8,128)S(1)}, f32[8,8,128]{2,1,0:T(8,128)}, u32[]{:S(2)}) copy-start(f32[8,8,128]{2,1,0:T(8,128)} %solid.1) | copy-start | bytes 98308
  3.3 44.8 %copy-start.12 = (s32[1,1,384,4]{2,3,1,0:T(4,128)S(1)}, s32[1,1,384,4]{2,3,1,0:T(4,128)}, u32[]{:S(2)}) copy-start(s32[1,1,384,4]{2,3,1,0:T(4,128)} %param.17) | copy-start | bytes 18436
  4.1 64.0 %copy-start.6 = (s32[1,1,512,2]{2,3,1,0:T(2,128)S(1)}, s32[1,1,512,2]{2,3,1,0:T(2,128)}, u32[]{:S(2)}) copy-start(s32[1,1,512,2]{2,3,1,0:T(2,128)} %param.15) | copy-start | bytes 12292
  4.1 6.0 %collective-permute-start = (f32[43,8,128]{2,1,0:T(8,128)S(1)}, f32[43,8,128]{2,1,0:T(8,128)S(1)}, u32[]{:S(2)}, u32[]{:S(2)}) collective-permute-start(f32[43,8,128]{2,1,0:T(8,128)S(1)} %get-tuple-element.31), channel_id=1, source_target_pairs={{0,1},{2,3},{4,5},{6,7},{8,9},{10,11},{12,13},{14,15},{1,0},{3,2},... | collective-permute-start | bytes 528392 | tf_op jit(solution)/shard_map/ppermute | solution.py:547
  6.7 6.8 %collective-permute-start.1 = (f32[43,8,128]{2,1,0:T(8,128)S(1)}, f32[43,8,128]{2,1,0:T(8,128)S(1)}, u32[]{:S(2)}, u32[]{:S(2)}) collective-permute-start(f32[43,8,128]{2,1,0:T(8,128)S(1)} %get-tuple-element.32), channel_id=1, source_target_pairs={{1,2},{3,4},{5,6},{7,8},{9,10},{11,12},{13,14},{2,1},{4,3},{6,5},{... | collective-permute-start | bytes 528392 | tf_op jit(solution)/shard_map/ppermute | solution.py:547
  14.8 33.3 %collective-permute-start.2 = (f32[46,8,128]{2,1,0:T(8,128)S(1)}, f32[46,8,128]{2,1,0:T(8,128)S(1)}, u32[]{:S(2)}, u32[]{:S(2)}) collective-permute-start(f32[46,8,128]{2,1,0:T(8,128)S(1)} %shard_map.141.after), channel_id=1, source_target_pairs={{16,32},{48,64},{80,96},{112,128},{144,160},{176,192},{208,224},{2... | collective-permute-start | bytes 565256 | tf_op jit(solution)/shard_map/ppermute | solution.py:547
  28.9 19.2 %collective-permute-start.3 = (f32[46,8,128]{2,1,0:T(8,128)S(1)}, f32[46,8,128]{2,1,0:T(8,128)S(1)}, u32[]{:S(2)}, u32[]{:S(2)}) collective-permute-start(f32[46,8,128]{2,1,0:T(8,128)S(1)} %get-tuple-element.34), channel_id=1, source_target_pairs={{0,16},{32,48},{64,80},{96,112},{128,144},{160,176},{192,208},{224... | collective-permute-start | bytes 565256 | tf_op jit(solution)/shard_map/ppermute | solution.py:547
  31.5 0.7 copy-start.5
  53.9 23.7 %collective-permute-start.5 = (f32[24,8,128]{2,1,0:T(8,128)S(1)}, f32[24,8,128]{2,1,0:T(8,128)S(1)}, u32[]{:S(2)}, u32[]{:S(2)}) collective-permute-start(f32[24,8,128]{2,1,0:T(8,128)S(1)} %shard_map.144.after), channel_id=1, source_target_pairs={{0,16},{32,48},{64,80},{96,112},{128,144},{160,176},{192,208},{224... | collective-permute-start | bytes 294920 | tf_op jit(solution)/shard_map/ppermute | solution.py:547
  55.8 23.8 %collective-permute-start.4 = (f32[24,8,128]{2,1,0:T(8,128)S(1)}, f32[24,8,128]{2,1,0:T(8,128)S(1)}, u32[]{:S(2)}, u32[]{:S(2)}) collective-permute-start(f32[24,8,128]{2,1,0:T(8,128)S(1)} %get-tuple-element.39), channel_id=1, source_target_pairs={{16,32},{48,64},{80,96},{112,128},{144,160},{176,192},{208,224},{2... | collective-permute-start | bytes 294920 | tf_op jit(solution)/shard_map/ppermute | solution.py:547
  68.0 16.1 %copy-start.1 = (f32[1,1,128,8,128]{4,3,2,1,0:T(8,128)S(1)}, f32[1,1,128,8,128]{4,3,2,1,0:T(8,128)}, u32[]{:S(2)}) copy-start(f32[1,1,128,8,128]{4,3,2,1,0:T(8,128)} %param.12) | copy-start | bytes 1572868
  79.8 7.7 %collective-permute-start.6 = (f32[34,8,128]{2,1,0:T(8,128)S(1)}, f32[34,8,128]{2,1,0:T(8,128)S(1)}, u32[]{:S(2)}, u32[]{:S(2)}) collective-permute-start(f32[34,8,128]{2,1,0:T(8,128)S(1)} %get-tuple-element.49), channel_id=1, source_target_pairs={{0,1},{2,3},{4,5},{6,7},{8,9},{10,11},{12,13},{14,15},{1,0},{3,2},... | collective-permute-start | bytes 417800 | tf_op jit(solution)/shard_map/ppermute | solution.py:547
  82.2 6.4 %collective-permute-start.7 = (f32[34,8,128]{2,1,0:T(8,128)S(1)}, f32[34,8,128]{2,1,0:T(8,128)S(1)}, u32[]{:S(2)}, u32[]{:S(2)}) collective-permute-start(f32[34,8,128]{2,1,0:T(8,128)S(1)} %get-tuple-element.50.after), channel_id=1, source_target_pairs={{1,2},{3,4},{5,6},{7,8},{9,10},{11,12},{13,14},{2,1},{4,3},{6,5},{... | collective-permute-start | bytes 417800 | tf_op jit(solution)/shard_map/ppermute | solution.py:547

commit v6 on v5

--- a/solution.py
+++ b/solution.py
@@ -35,14 +35,13 @@
     return jax.ShapeDtypeStruct(dims, F32)
 
 
-def call(kernel, outs, in_specs, scratch=(), flops=10**6, moved=10**6, aliases=None):
+def call(kernel, outs, in_specs, scratch=(), flops=10**6, moved=10**6):
     return pl.pallas_call(
         kernel,
         out_shape=outs,
         in_specs=in_specs,
         out_specs=jax.tree.map(lambda o: SM if len(o.shape) == 1 else VM, outs),
         scratch_shapes=list(scratch),
-        input_output_aliases=aliases or {},
         compiler_params=PARAMS,
         cost_estimate=pl.CostEstimate(flops=flops, bytes_accessed=moved, transcendentals=0),
     )
@@ -105,7 +104,7 @@
     parts, sends_in, moves_in, tiles_in, slots, flow_x, in_xo, in_xe, in_ye, in_yo, after,
     pres, screen, source, solid,
     drag, dep, out_o, gain, rest,
-    pool, table, sums, owned, sends, moves, tiles, sems,
+    pool, table, sums, owned, blocks_held, sends, moves, tiles, sems,
 ):
     copies = fetch((sends_in, moves_in, tiles_in), (sends, moves, tiles), sems)
     for k in range(NB):
@@ -147,6 +146,10 @@
         lax.fori_loop(0, moves[0, d], leave, 0)
         for s in range(MOVERS):
             owned[NB + d * MOVERS + s] = jnp.where(s < moves[1, d], 1.0, 0.0)
+    held = jnp.int32(0)
+    for m in range(OWNABLE):
+        blocks_held[held] = m
+        held = held + jnp.where(owned[m] > 0.5, 1, 0)
 
     row = lax.broadcasted_iota(jnp.int32, (8, NB), 0)
     low_rows = row < 4
@@ -154,8 +157,7 @@
     half = jnp.where(low_rows, 0, 1)
     depth_rows = lax.broadcasted_iota(jnp.int32, (128, NB), 0)
 
-    def one_block(m, at):
-        own = owned[m]
+    def one_block(m, at, counts):
         state = pool[m]
         code = jnp.broadcast_to(slots[pl.ds(at, 1), :], (8, NB))
         depth = code & 127
@@ -167,7 +169,7 @@
         )
         coeff = jnp.broadcast_to(state[7:8], (8, NB))
         radius = jnp.broadcast_to(state[3:4], (8, NB))
-        values = jnp.where(last_row, radius * radius * radius, coeff * (at_particle - state)) * own
+        values = jnp.where(last_row, radius * radius * radius, coeff * (at_particle - state))
         both = jnp.where(low_rows, pltpu.roll(values, 4, 0), values)
         for c in range(3):
             drag[c, pl.ds(at, 1), :] = both[c : c + 1]
@@ -181,7 +183,7 @@
             jnp.concatenate([upper, lower], axis=0), pick, (((1,), (1,)), ((), ())),
             preferred_element_type=F32,
         )
-        spread = spread[0:16] + spread[16:32]
+        spread = (spread[0:16] + spread[16:32]) * counts
         parts_ = (
             jnp.where(low_rows, spread[0:8], 0.0), jnp.where(low_rows, 0.0, spread[0:8]),
             jnp.where(low_rows, spread[8:16], 0.0), jnp.where(low_rows, 0.0, spread[8:16]),
@@ -196,14 +198,15 @@
     def blocks(g, carry):
         made = []
         for u in range(COUPLE_UNROLL):
-            m = g * COUPLE_UNROLL + u
+            n = g * COUPLE_UNROLL + u
+            m = blocks_held[jnp.minimum(n, held - 1)]
             at = jnp.where(m < NB, m, NB + ((m - NB) // MOVERS) * SLOTS + (m - NB) % MOVERS)
-            made.append(one_block(m, at))
+            made.append(one_block(m, at, jnp.where(n < held, 1.0, 0.0)))
         for columns, pieces in made:
             add(columns, pieces)
         return carry
 
-    lax.fori_loop(0, OWNABLE // COUPLE_UNROLL, blocks, 0)
+    lax.fori_loop(0, (held + COUPLE_UNROLL - 1) // COUPLE_UNROLL, blocks, 0)
     dep[...] = jnp.zeros_like(dep)
     for n in range(100):
         total = sums[n]
@@ -497,6 +500,12 @@
     left, near, right, sums, chosen,
 ):
     total = total_ref[0, 0]
+    for made, kept, size, skip in ((left, left_in, 4, 2 * SLOTS), (near, near_in, 1, 2 * SLOTS)):
+        made[0 : NB // size] = kept[0 : NB // size]
+        made[(NB + skip) // size :] = kept[(NB + skip) // size :]
+    right[0:NB] = right_in[0:NB]
+    right[NB + 2 * MOVERS :] = right_in[NB + 2 * MOVERS :]
+    sums[...] = sums_in[...]
     four, right_of = preparers(left, near, right)
     look = lister(pairs, total, chosen, True)
     x_even = lax.axis_index("gx") % 2 == 0
@@ -512,6 +521,7 @@
 def contact_end(
     pairs, parts, in_xo, in_xe, in_ye, in_yo, drag, after, left, near, right, chosen, sums_in, force, sums
 ):
+    sums[...] = sums_in[...]
     count = chosen[LAST]
     run_tiles(pairs, chosen, count, left, near, right, sums, EARLY, count)
 
@@ -595,6 +605,7 @@
             pltpu.VMEM((100, 8, 128), F32),
             pltpu.VMEM((100, 8, 128), F32),
             pltpu.SMEM((OWNABLE,), F32),
+            pltpu.SMEM((OWNABLE + 1,), jnp.int32),
             pltpu.SMEM((4, SLOTS), jnp.int32),
             pltpu.SMEM((2, 4), jnp.int32),
             pltpu.SMEM((4, 384), jnp.int32),
@@ -612,7 +623,6 @@
         (*operands, jax.ShapeDtypeStruct((LIST,), jnp.int32)),
         [SM, SM] + [VM] * 7,
         flops=10**8,
-        aliases={5: 0, 6: 1, 7: 2, 8: 3},
     )(pairs, tile_count, got_xo, got_xe, fe, *prepared)
     load, drag_x, pres_w, gain_w, rest_w, he, ho = call(
         fold_x,
@@ -624,12 +634,12 @@
     )(dep, pressure_init, gain, rest, got_fo, got_fe, more[3])
     got_he = swap(he, "gy", 0)
     got_ho = swap(ho, "gy", 1)
-    force, unused = call(
+    force = call(
         contact_end,
-        (shape(3, 384, 128), operands[3]),
+        shape(3, 384, 128),
         [SM] + [VM] * 10 + [SM, VM],
+        [pltpu.VMEM((OWNABLE, 8, 128), F32)],
         flops=10**9,
-        aliases={12: 1},
     )(pairs, parts, got_xo, got_xe, got_ye, got_yo, drag, ho, *more[:3], chosen, more[3])
     pressure, drag_sum = call(
         finish,

time: 90 us -> 90.3 us (level)
  waiting for transfers between devices: 11.4 us -> 14.9 us
  Pallas kernels: 32.8 us -> 29.7 us
    ppermute x8, waiting for transfers between devices: 11.4 us -> 14.9 us  [swap(): return lax.ppermute(array, axis, pairs_of(first, count, count - 1))]
    pallas_call x1, Pallas kernels: 3.38 us -> 2.04 us  [body(): call(contact_end, shape(3, 384, 128), [SM] + [VM] * 10 + [SM, VM], [pltpu...]
    pallas_call x1, Pallas kernels: 9.54 us -> 8.55 us  [body(): call(contact_more, (*operands, jax.ShapeDtypeStruct((LIST,), jnp.int32)),...]
  transfers between devices with their start and end apart: 8 -> 8, of which waited for: 4 -> 4; matrix products, arithmetic and copies ran while one was open for 0% -> 0% of each run, Pallas kernels for 27% -> 24%
where the time goes in v6:
time: 90.3 us; the launch traced here: 89.9 us
  starting transfers between devices  40.4 us (45%)
  Pallas kernels  29.7 us (33%)
  waiting for transfers between devices  14.9 us (17%)
  local copies, waits for them, and re-layouts  3.35 us (4%)
  between operations  1.55 us (2%)
    ppermute x8, starting transfers between devices, swap(): return lax.ppermute(array, axis, pairs_of(first, count, count - 1))  40.4 us
    ppermute x8, waiting for transfers between devices, swap(): return lax.ppermute(array, axis, pairs_of(first, count, count - 1))  14.9 us
    pallas_call x1, Pallas kernels, body(): call(contact_near, operands, [SM, SM] + [VM] * 4, [pltpu.SMEM((LIST,), jn...  10.9 us
    pallas_call x1, Pallas kernels, body(): call(contact_more, (*operands, jax.ShapeDtypeStruct((LIST,), jnp.int32)),...  8.55 us
    pallas_call x1, Pallas kernels, body(): call(couple, (shape(3, 384, 128), shape(4, 10, 16, 128), shape(D_TILES, 8...  4.92 us
    unnamed x28, local copies, waits for them, and re-layouts  3.35 us
    pallas_call x1, Pallas kernels, body(): call(contact_end, shape(3, 384, 128), [SM] + [VM] * 10 + [SM, VM], [pltpu...  2.04 us
  transfers between devices with their start and end apart: 8, of which 4 were waited for; matrix products, arithmetic and copies ran while one was open for 0% of the time, Pallas kernels for 24%

profile of v6, /device:TPU:63, one launch (start us, length us, event | category | flops | bytes accessed | tf_op | source)
XLA Modules:
  0.0 89.9 jit_solution(314381482536928923)
XLA Ops:
  0.6 0.0 copy-start.11
  0.6 0.0 copy-start.13
  0.7 0.0 copy-start
  0.7 1.0 %copy-done = f32[1,1,128,8,128]{4,3,2,1,0:T(8,128)S(1)} copy-done((f32[1,1,128,8,128]{4,3,2,1,0:T(8,128)S(1)}, f32[1,1,128,8,128]{4,3,2,1,0:T(8,128)}, u32[]{:S(2)}) %copy-start) | copy-done | bytes 524312
  1.7 0.0 copy-start.2
  1.7 0.9 copy-done.2
  2.6 0.0 copy-start.10
  2.6 0.7 copy-done.10
  3.3 0.0 copy-start.3
  3.3 0.0 copy-start.4
  3.3 0.0 copy-start.7
  3.3 0.0 copy-start.8
  3.3 0.0 copy-start.9
  3.3 0.0 copy-start.12
  3.3 0.7 shard_map.139
  4.1 0.0 copy-start.6
  4.1 2.6 %collective-permute-start = (f32[43,8,128]{2,1,0:T(8,128)S(1)}, f32[43,8,128]{2,1,0:T(8,128)S(1)}, u32[]{:S(2)}, u32[]{:S(2)}) collective-permute-start(f32[43,8,128]{2,1,0:T(8,128)S(1)} %get-tuple-element.30), channel_id=1, source_target_pairs={{0,1},{2,3},{4,5},{6,7},{8,9},{10,11},{12,13},{14,15},{1,0},{3,2},... | collective-permute-start | bytes 528392 | tf_op jit(solution)/shard_map/ppermute | solution.py:557
  6.7 3.4 %collective-permute-start.1 = (f32[43,8,128]{2,1,0:T(8,128)S(1)}, f32[43,8,128]{2,1,0:T(8,128)S(1)}, u32[]{:S(2)}, u32[]{:S(2)}) collective-permute-start(f32[43,8,128]{2,1,0:T(8,128)S(1)} %get-tuple-element.31), channel_id=1, source_target_pairs={{1,2},{3,4},{5,6},{7,8},{9,10},{11,12},{13,14},{2,1},{4,3},{6,5},{... | collective-permute-start | bytes 528392 | tf_op jit(solution)/shard_map/ppermute | solution.py:557
  10.1 0.0 collective-permute-done.in_e.in_ye
  10.1 3.3 %collective-permute-done.1.in_o.in_yo = f32[43,8,128]{2,1,0:T(8,128)S(1)} collective-permute-done((f32[43,8,128]{2,1,0:T(8,128)S(1)}, f32[43,8,128]{2,1,0:T(8,128)S(1)}, u32[]{:S(2)}, u32[]{:S(2)}) %collective-permute-start.1) | collective-permute-done | bytes 176160 | tf_op jit(solution)/shard_map/ppermute | solution.py:557
  13.4 0.7 shard_map.140
  14.1 0.7 shard_map.141.after
  14.8 14.1 %collective-permute-start.2 = (f32[46,8,128]{2,1,0:T(8,128)S(1)}, f32[46,8,128]{2,1,0:T(8,128)S(1)}, u32[]{:S(2)}, u32[]{:S(2)}) collective-permute-start(f32[46,8,128]{2,1,0:T(8,128)S(1)} %shard_map.141.after), channel_id=1, source_target_pairs={{16,32},{48,64},{80,96},{112,128},{144,160},{176,192},{208,224},{2... | collective-permute-start | bytes 565256 | tf_op jit(solution)/shard_map/ppermute | solution.py:557
  28.9 1.9 %collective-permute-start.3 = (f32[46,8,128]{2,1,0:T(8,128)S(1)}, f32[46,8,128]{2,1,0:T(8,128)S(1)}, u32[]{:S(2)}, u32[]{:S(2)}) collective-permute-start(f32[46,8,128]{2,1,0:T(8,128)S(1)} %get-tuple-element.33), channel_id=1, source_target_pairs={{0,16},{32,48},{64,80},{96,112},{128,144},{160,176},{192,208},{224... | collective-permute-start | bytes 565256 | tf_op jit(solution)/shard_map/ppermute | solution.py:557
  31.5 0.0 copy-start.5
  31.5 0.7 copy-done.5
  32.2 10.9 %shard_map.142 = (bf16[96,128,128]{2,1,0:T(8,128)(2,1)S(1)}, bf16[384,16,128]{2,1,0:T(8,128)(2,1)S(1)}, bf16[192,32,256]{2,1,0:T(8,128)(2,1)S(1)}, f32[192,8,128]{2,1,0:T(8,128)S(1)}) custom-call(s32[2,512]{1,0:T(2,128)S(1)} %bitcast.20, s32[1,1]{1,0:T(1,128)S(6)} %copy.15.total_ref, f32[128,8,128]{2,1,0:T(8,128)S(1)} %bitcast.16, ...), custom_call_target="tpu_custom_call" | custom-call | flops 100000000 | bytes 1000000 | tf_op jit(solution)/shard_map/pallas_call | solution.py:596
  43.1 5.0 %collective-permute-done.2.in_xo = f32[46,8,128]{2,1,0:T(8,128)S(1)} collective-permute-done((f32[46,8,128]{2,1,0:T(8,128)S(1)}, f32[46,8,128]{2,1,0:T(8,128)S(1)}, u32[]{:S(2)}, u32[]{:S(2)}) %collective-permute-start.2) | collective-permute-done | bytes 188448 | tf_op jit(solution)/shard_map/ppermute | solution.py:557
  48.0 0.0 collective-permute-done.3.in_xe
  48.0 0.0 copy-done.11
  48.1 0.0 copy-done.13
  48.1 0.0 copy-done.3
  48.1 0.0 copy-done.4
  48.1 0.0 copy-done.7
  48.1 0.0 copy-done.8
  48.1 0.0 copy-done.9
  48.1 0.0 copy-done.12
  48.1 4.9 %shard_map.143 = (f32[3,384,128]{2,1,0:T(8,128)S(1)}, f32[4,10,16,128]{3,2,1,0:T(8,128)S(1)}, f32[24,8,128]{2,1,0:T(8,128)S(1)}, f32[8,8,128]{2,1,0:T(8,128)S(1)}, f32[8,8,128]{2,1,0:T(8,128)S(1)}) custom-call(f32[128,8,128]{2,1,0:T(8,128)S(1)} %bitcast.17, s32[4,64]{1,0:T(4,128)S(1)} %bitcast.26, s32[2,4]{1,0:T(2,128)S(1)} %bitcast.28, ...), custom_call_target="tpu_custom_call" | custom-call | flops 1000000 | bytes 1000000 | tf_op jit(solution)/shard_map/pallas_call | solution.py:599
  53.1 1.9 %collective-permute-start.5 = (f32[24,8,128]{2,1,0:T(8,128)S(1)}, f32[24,8,128]{2,1,0:T(8,128)S(1)}, u32[]{:S(2)}, u32[]{:S(2)}) collective-permute-start(f32[24,8,128]{2,1,0:T(8,128)S(1)} %shard_map.144.after), channel_id=1, source_target_pairs={{0,16},{32,48},{64,80},{96,112},{128,144},{160,176},{192,208},{224... | collective-permute-start | bytes 294920 | tf_op jit(solution)/shard_map/ppermute | solution.py:557
  55.0 12.1 %collective-permute-start.4 = (f32[24,8,128]{2,1,0:T(8,128)S(1)}, f32[24,8,128]{2,1,0:T(8,128)S(1)}, u32[]{:S(2)}, u32[]{:S(2)}) collective-permute-start(f32[24,8,128]{2,1,0:T(8,128)S(1)} %get-tuple-element.38), channel_id=1, source_target_pairs={{16,32},{48,64},{80,96},{112,128},{144,160},{176,192},{208,224},{2... | collective-permute-start | bytes 294920 | tf_op jit(solution)/shard_map/ppermute | solution.py:557
  67.1 0.0 copy-done.6
  67.1 0.0 copy-start.1
  67.1 8.6 %shard_map.145 = (bf16[96,128,128]{2,1,0:T(8,128)(2,1)S(1)}, bf16[384,16,128]{2,1,0:T(8,128)(2,1)S(1)}, bf16[192,32,256]{2,1,0:T(8,128)(2,1)S(1)}, f32[192,8,128]{2,1,0:T(8,128)S(1)}, s32[640]{0:T(1024)S(1)}) custom-call(s32[2,512]{1,0:T(2,128)S(1)} %bitcast.21, s32[1,1]{1,0:T(1,128)S(6)} %copy.15.total_ref, f32[46,8,128]{2,1,0:T(8,128)S(1)} %collective-permute-done.2.in_xo, ...), custom_call_target="tpu_custom_call" | custom-call | flops 100000000 | bytes 1000000 | tf_op jit(solution)/shard_map/pallas_call | solution.py:621
  75.7 0.0 collective-permute-done.5.in_e
  75.7 4.2 %collective-permute-done.4.in_o = f32[24,8,128]{2,1,0:T(8,128)S(1)} collective-permute-done((f32[24,8,128]{2,1,0:T(8,128)S(1)}, f32[24,8,128]{2,1,0:T(8,128)S(1)}, u32[]{:S(2)}, u32[]{:S(2)}) %collective-permute-start.4) | collective-permute-done | bytes 98336 | tf_op jit(solution)/shard_map/ppermute | solution.py:557
  79.9 0.1 shard_map.146
  80.0 2.4 %collective-permute-start.6 = (f32[34,8,128]{2,1,0:T(8,128)S(1)}, f32[34,8,128]{2,1,0:T(8,128)S(1)}, u32[]{:S(2)}, u32[]{:S(2)}) collective-permute-start(f32[34,8,128]{2,1,0:T(8,128)S(1)} %get-tuple-element.48), channel_id=1, source_target_pairs={{0,1},{2,3},{4,5},{6,7},{8,9},{10,11},{12,13},{14,15},{1,0},{3,2},... | collective-permute-start | bytes 417800 | tf_op jit(solution)/shard_map/ppermute | solution.py:557
  82.4 1.9 %collective-permute-start.7 = (f32[34,8,128]{2,1,0:T(8,128)S(1)}, f32[34,8,128]{2,1,0:T(8,128)S(1)}, u32[]{:S(2)}, u32[]{:S(2)}) collective-permute-start(f32[34,8,128]{2,1,0:T(8,128)S(1)} %get-tuple-element.49.after), channel_id=1, source_target_pairs={{1,2},{3,4},{5,6},{7,8},{9,10},{11,12},{13,14},{2,1},{4,3},{6,5},{... | collective-permute-start | bytes 417800 | tf_op jit(solution)/shard_map/ppermute | solution.py:557
  84.4 0.0 copy-done.1
  84.4 2.0 %shard_map.148 = f32[3,384,128]{2,1,0:T(8,128)} custom-call(s32[2,512]{1,0:T(2,128)S(1)} %bitcast.22, f32[128,8,128]{2,1,0:T(8,128)S(1)} %bitcast.18, f32[46,8,128]{2,1,0:T(8,128)S(1)} %collective-permute-done.2.in_xo, f32[46,8,128]{2,1,0:T(8,128)S(1)} %collective-permute-done.3.in_xe, f32[43,8,128]{2,1,0:T(8,128)S(1)} %collective-permute-done.in_e.in_ye, ...), custom_call_target="tpu_custom_call" | custom-call | flops 1000000000 | bytes 1000000 | tf_op jit(solution)/shard_map/pallas_call | solution.py:637
  86.4 0.0 collective-permute-done.6.in_e
  86.4 2.4 %collective-permute-done.7.in_o = f32[34,8,128]{2,1,0:T(8,128)S(1)} collective-permute-done((f32[34,8,128]{2,1,0:T(8,128)S(1)}, f32[34,8,128]{2,1,0:T(8,128)S(1)}, u32[]{:S(2)}, u32[]{:S(2)}) %collective-permute-start.7) | collective-permute-done | bytes 139296 | tf_op jit(solution)/shard_map/ppermute | solution.py:557
  88.8 1.1 %shard_map.147 = (f32[8,8,128]{2,1,0:T(8,128)}, f32[3,8,8,128]{3,2,1,0:T(8,128)}) custom-call(f32[16,16,128]{2,1,0:T(8,128)S(1)} %get-tuple-element.43.load, f32[3,8,16,128]{3,2,1,0:T(8,128)S(1)} %get-tuple-element.44.drag, f32[16,8,128]{2,1,0:T(8,128)S(1)} %get-tuple-element.45.pres_w, f32[16,8,128]{2,1,0:T(8,128)S(1)} %get-tuple-element.46.gain_w, ...), custom_call_target="tpu_custom_call" | custom-call | flops 1000000 | bytes 1000000 | tf_op jit(solution)/shard_map/pallas_call | solution.py:644
  (1 shorter events, 0.0 us)
Async XLA Ops:
  0.6 47.4 %copy-start.11 = (s32[1,1,4,64]{3,2,1,0:T(4,128)S(1)}, s32[1,1,4,64]{3,2,1,0:T(4,128)}, u32[]{:S(2)}) copy-start(s32[1,1,4,64]{3,2,1,0:T(4,128)} %param.13) | copy-start | bytes 3076
  0.6 47.4 %copy-start.13 = (s32[1,1,2,4]{3,2,1,0:T(2,128)S(1)}, s32[1,1,2,4]{3,2,1,0:T(2,128)}, u32[]{:S(2)}) copy-start(s32[1,1,2,4]{3,2,1,0:T(2,128)} %param.14) | copy-start | bytes 100
  0.7 1.1 %copy-start = (f32[1,1,128,8,128]{4,3,2,1,0:T(8,128)S(1)}, f32[1,1,128,8,128]{4,3,2,1,0:T(8,128)}, u32[]{:S(2)}) copy-start(f32[1,1,128,8,128]{4,3,2,1,0:T(8,128)} %param.12) | copy-start | bytes 1572868
  1.7 0.9 copy-start.2
  2.6 0.7 copy-start.10
  3.3 44.8 %copy-start.3 = (f32[8,8,128]{2,1,0:T(8,128)S(1)}, f32[8,8,128]{2,1,0:T(8,128)}, u32[]{:S(2)}) copy-start(f32[8,8,128]{2,1,0:T(8,128)} %pres.5) | copy-start | bytes 98308
  3.3 44.8 %copy-start.4 = (s32[1,1,384,128]{3,2,1,0:T(8,128)S(1)}, s32[1,1,384,128]{3,2,1,0:T(8,128)}, u32[]{:S(2)}) copy-start(s32[1,1,384,128]{3,2,1,0:T(8,128)} %param.18) | copy-start | bytes 589828
  3.3 44.8 %copy-start.7 = (f32[8,8,128]{2,1,0:T(8,128)S(1)}, f32[8,8,128]{2,1,0:T(8,128)}, u32[]{:S(2)}) copy-start(f32[8,8,128]{2,1,0:T(8,128)} %screen.1) | copy-start | bytes 98308
  3.3 44.8 %copy-start.8 = (f32[8,8,128]{2,1,0:T(8,128)S(1)}, f32[8,8,128]{2,1,0:T(8,128)}, u32[]{:S(2)}) copy-start(f32[8,8,128]{2,1,0:T(8,128)} %source.1) | copy-start | bytes 98308
  3.3 44.8 %copy-start.9 = (f32[8,8,128]{2,1,0:T(8,128)S(1)}, f32[8,8,128]{2,1,0:T(8,128)}, u32[]{:S(2)}) copy-start(f32[8,8,128]{2,1,0:T(8,128)} %solid.1) | copy-start | bytes 98308
  3.3 44.8 %copy-start.12 = (s32[1,1,384,4]{2,3,1,0:T(4,128)S(1)}, s32[1,1,384,4]{2,3,1,0:T(4,128)}, u32[]{:S(2)}) copy-start(s32[1,1,384,4]{2,3,1,0:T(4,128)} %param.17) | copy-start | bytes 18436
  4.1 63.0 %copy-start.6 = (s32[1,1,512,2]{2,3,1,0:T(2,128)S(1)}, s32[1,1,512,2]{2,3,1,0:T(2,128)}, u32[]{:S(2)}) copy-start(s32[1,1,512,2]{2,3,1,0:T(2,128)} %param.15) | copy-start | bytes 12292
  4.1 6.0 %collective-permute-start = (f32[43,8,128]{2,1,0:T(8,128)S(1)}, f32[43,8,128]{2,1,0:T(8,128)S(1)}, u32[]{:S(2)}, u32[]{:S(2)}) collective-permute-start(f32[43,8,128]{2,1,0:T(8,128)S(1)} %get-tuple-element.30), channel_id=1, source_target_pairs={{0,1},{2,3},{4,5},{6,7},{8,9},{10,11},{12,13},{14,15},{1,0},{3,2},... | collective-permute-start | bytes 528392 | tf_op jit(solution)/shard_map/ppermute | solution.py:557
  6.7 6.8 %collective-permute-start.1 = (f32[43,8,128]{2,1,0:T(8,128)S(1)}, f32[43,8,128]{2,1,0:T(8,128)S(1)}, u32[]{:S(2)}, u32[]{:S(2)}) collective-permute-start(f32[43,8,128]{2,1,0:T(8,128)S(1)} %get-tuple-element.31), channel_id=1, source_target_pairs={{1,2},{3,4},{5,6},{7,8},{9,10},{11,12},{13,14},{2,1},{4,3},{6,5},{... | collective-permute-start | bytes 528392 | tf_op jit(solution)/shard_map/ppermute | solution.py:557
  14.8 33.3 %collective-permute-start.2 = (f32[46,8,128]{2,1,0:T(8,128)S(1)}, f32[46,8,128]{2,1,0:T(8,128)S(1)}, u32[]{:S(2)}, u32[]{:S(2)}) collective-permute-start(f32[46,8,128]{2,1,0:T(8,128)S(1)} %shard_map.141.after), channel_id=1, source_target_pairs={{16,32},{48,64},{80,96},{112,128},{144,160},{176,192},{208,224},{2... | collective-permute-start | bytes 565256 | tf_op jit(solution)/shard_map/ppermute | solution.py:557
  28.9 19.2 %collective-permute-start.3 = (f32[46,8,128]{2,1,0:T(8,128)S(1)}, f32[46,8,128]{2,1,0:T(8,128)S(1)}, u32[]{:S(2)}, u32[]{:S(2)}) collective-permute-start(f32[46,8,128]{2,1,0:T(8,128)S(1)} %get-tuple-element.33), channel_id=1, source_target_pairs={{0,16},{32,48},{64,80},{96,112},{128,144},{160,176},{192,208},{224... | collective-permute-start | bytes 565256 | tf_op jit(solution)/shard_map/ppermute | solution.py:557
  31.5 0.7 copy-start.5
  53.1 22.6 %collective-permute-start.5 = (f32[24,8,128]{2,1,0:T(8,128)S(1)}, f32[24,8,128]{2,1,0:T(8,128)S(1)}, u32[]{:S(2)}, u32[]{:S(2)}) collective-permute-start(f32[24,8,128]{2,1,0:T(8,128)S(1)} %shard_map.144.after), channel_id=1, source_target_pairs={{0,16},{32,48},{64,80},{96,112},{128,144},{160,176},{192,208},{224... | collective-permute-start | bytes 294920 | tf_op jit(solution)/shard_map/ppermute | solution.py:557
  55.0 24.9 %collective-permute-start.4 = (f32[24,8,128]{2,1,0:T(8,128)S(1)}, f32[24,8,128]{2,1,0:T(8,128)S(1)}, u32[]{:S(2)}, u32[]{:S(2)}) collective-permute-start(f32[24,8,128]{2,1,0:T(8,128)S(1)} %get-tuple-element.38), channel_id=1, source_target_pairs={{16,32},{48,64},{80,96},{112,128},{144,160},{176,192},{208,224},{2... | collective-permute-start | bytes 294920 | tf_op jit(solution)/shard_map/ppermute | solution.py:557
  67.1 17.3 %copy-start.1 = (f32[1,1,128,8,128]{4,3,2,1,0:T(8,128)S(1)}, f32[1,1,128,8,128]{4,3,2,1,0:T(8,128)}, u32[]{:S(2)}) copy-start(f32[1,1,128,8,128]{4,3,2,1,0:T(8,128)} %param.12) | copy-start | bytes 1572868
  80.0 6.4 %collective-permute-start.6 = (f32[34,8,128]{2,1,0:T(8,128)S(1)}, f32[34,8,128]{2,1,0:T(8,128)S(1)}, u32[]{:S(2)}, u32[]{:S(2)}) collective-permute-start(f32[34,8,128]{2,1,0:T(8,128)S(1)} %get-tuple-element.48), channel_id=1, source_target_pairs={{0,1},{2,3},{4,5},{6,7},{8,9},{10,11},{12,13},{14,15},{1,0},{3,2},... | collective-permute-start | bytes 417800 | tf_op jit(solution)/shard_map/ppermute | solution.py:557
  82.4 6.4 %collective-permute-start.7 = (f32[34,8,128]{2,1,0:T(8,128)S(1)}, f32[34,8,128]{2,1,0:T(8,128)S(1)}, u32[]{:S(2)}, u32[]{:S(2)}) collective-permute-start(f32[34,8,128]{2,1,0:T(8,128)S(1)} %get-tuple-element.49.after), channel_id=1, source_target_pairs={{1,2},{3,4},{5,6},{7,8},{9,10},{11,12},{13,14},{2,1},{4,3},{6,5},{... | collective-permute-start | bytes 417800 | tf_op jit(solution)/shard_map/ppermute | solution.py:557

commit v7 on v6

--- a/solution.py
+++ b/solution.py
@@ -19,7 +19,7 @@
 MAXT = 512
 ITERS = 4
 CONTACT_UNROLL = 32
-EARLY = 96
+EARLY = 128
 LIST = 640
 LAST = LIST - 1
 PREPARE = 4

time: 90.3 us -> 90.3 us (level)
  no operation moved by 1% of the time
where the time goes in v7:
time: 90.3 us; the launch traced here: 89.9 us
  starting transfers between devices  40.5 us (45%)
  Pallas kernels  29.7 us (33%)
  waiting for transfers between devices  14.8 us (16%)
  local copies, waits for them, and re-layouts  3.35 us (4%)
  between operations  1.55 us (2%)
    ppermute x8, starting transfers between devices, swap(): return lax.ppermute(array, axis, pairs_of(first, count, count - 1))  40.5 us
    ppermute x8, waiting for transfers between devices, swap(): return lax.ppermute(array, axis, pairs_of(first, count, count - 1))  14.8 us
    pallas_call x1, Pallas kernels, body(): call(contact_near, operands, [SM, SM] + [VM] * 4, [pltpu.SMEM((LIST,), jn...  10.9 us
    pallas_call x1, Pallas kernels, body(): call(contact_more, (*operands, jax.ShapeDtypeStruct((LIST,), jnp.int32)),...  8.55 us
    pallas_call x1, Pallas kernels, body(): call(couple, (shape(3, 384, 128), shape(4, 10, 16, 128), shape(D_TILES, 8...  4.93 us
    unnamed x28, local copies, waits for them, and re-layouts  3.35 us
    pallas_call x1, Pallas kernels, body(): call(contact_end, shape(3, 384, 128), [SM] + [VM] * 10 + [SM, VM], [pltpu...  2.04 us
  transfers between devices with their start and end apart: 8, of which 4 were waited for; matrix products, arithmetic and copies ran while one was open for 0% of the time, Pallas kernels for 24%

profile of v7, /device:TPU:63, one launch (start us, length us, event | category | flops | bytes accessed | tf_op | source)
XLA Modules:
  0.0 89.9 jit_solution(14688107808138206386)
XLA Ops:
  0.6 0.0 copy-start.11
  0.6 0.0 copy-start.13
  0.7 0.0 copy-start
  0.7 1.0 %copy-done = f32[1,1,128,8,128]{4,3,2,1,0:T(8,128)S(1)} copy-done((f32[1,1,128,8,128]{4,3,2,1,0:T(8,128)S(1)}, f32[1,1,128,8,128]{4,3,2,1,0:T(8,128)}, u32[]{:S(2)}) %copy-start) | copy-done | bytes 524312
  1.7 0.0 copy-start.2
  1.7 0.9 copy-done.2
  2.6 0.0 copy-start.10
  2.6 0.7 copy-done.10
  3.3 0.0 copy-start.3
  3.3 0.0 copy-start.4
  3.3 0.0 copy-start.7
  3.3 0.0 copy-start.8
  3.3 0.0 copy-start.9
  3.3 0.0 copy-start.12
  3.3 0.7 shard_map.139
  4.1 0.0 copy-start.6
  4.1 2.6 %collective-permute-start = (f32[43,8,128]{2,1,0:T(8,128)S(1)}, f32[43,8,128]{2,1,0:T(8,128)S(1)}, u32[]{:S(2)}, u32[]{:S(2)}) collective-permute-start(f32[43,8,128]{2,1,0:T(8,128)S(1)} %get-tuple-element.30), channel_id=1, source_target_pairs={{0,1},{2,3},{4,5},{6,7},{8,9},{10,11},{12,13},{14,15},{1,0},{3,2},... | collective-permute-start | bytes 528392 | tf_op jit(solution)/shard_map/ppermute | solution.py:557
  6.7 3.4 %collective-permute-start.1 = (f32[43,8,128]{2,1,0:T(8,128)S(1)}, f32[43,8,128]{2,1,0:T(8,128)S(1)}, u32[]{:S(2)}, u32[]{:S(2)}) collective-permute-start(f32[43,8,128]{2,1,0:T(8,128)S(1)} %get-tuple-element.31), channel_id=1, source_target_pairs={{1,2},{3,4},{5,6},{7,8},{9,10},{11,12},{13,14},{2,1},{4,3},{6,5},{... | collective-permute-start | bytes 528392 | tf_op jit(solution)/shard_map/ppermute | solution.py:557
  10.1 0.0 collective-permute-done.in_e.in_ye
  10.1 3.3 %collective-permute-done.1.in_o.in_yo = f32[43,8,128]{2,1,0:T(8,128)S(1)} collective-permute-done((f32[43,8,128]{2,1,0:T(8,128)S(1)}, f32[43,8,128]{2,1,0:T(8,128)S(1)}, u32[]{:S(2)}, u32[]{:S(2)}) %collective-permute-start.1) | collective-permute-done | bytes 176160 | tf_op jit(solution)/shard_map/ppermute | solution.py:557
  13.4 0.7 shard_map.140
  14.1 0.7 shard_map.141.after
  14.8 14.1 %collective-permute-start.2 = (f32[46,8,128]{2,1,0:T(8,128)S(1)}, f32[46,8,128]{2,1,0:T(8,128)S(1)}, u32[]{:S(2)}, u32[]{:S(2)}) collective-permute-start(f32[46,8,128]{2,1,0:T(8,128)S(1)} %shard_map.141.after), channel_id=1, source_target_pairs={{16,32},{48,64},{80,96},{112,128},{144,160},{176,192},{208,224},{2... | collective-permute-start | bytes 565256 | tf_op jit(solution)/shard_map/ppermute | solution.py:557
  28.9 1.9 %collective-permute-start.3 = (f32[46,8,128]{2,1,0:T(8,128)S(1)}, f32[46,8,128]{2,1,0:T(8,128)S(1)}, u32[]{:S(2)}, u32[]{:S(2)}) collective-permute-start(f32[46,8,128]{2,1,0:T(8,128)S(1)} %get-tuple-element.33), channel_id=1, source_target_pairs={{0,16},{32,48},{64,80},{96,112},{128,144},{160,176},{192,208},{224... | collective-permute-start | bytes 565256 | tf_op jit(solution)/shard_map/ppermute | solution.py:557
  31.5 0.0 copy-start.5
  31.5 0.7 copy-done.5
  32.2 10.9 %shard_map.142 = (bf16[96,128,128]{2,1,0:T(8,128)(2,1)S(1)}, bf16[384,16,128]{2,1,0:T(8,128)(2,1)S(1)}, bf16[192,32,256]{2,1,0:T(8,128)(2,1)S(1)}, f32[192,8,128]{2,1,0:T(8,128)S(1)}) custom-call(s32[2,512]{1,0:T(2,128)S(1)} %bitcast.20, s32[1,1]{1,0:T(1,128)S(6)} %copy.15.total_ref, f32[128,8,128]{2,1,0:T(8,128)S(1)} %bitcast.16, ...), custom_call_target="tpu_custom_call" | custom-call | flops 100000000 | bytes 1000000 | tf_op jit(solution)/shard_map/pallas_call | solution.py:596
  43.1 5.0 %collective-permute-done.2.in_xo = f32[46,8,128]{2,1,0:T(8,128)S(1)} collective-permute-done((f32[46,8,128]{2,1,0:T(8,128)S(1)}, f32[46,8,128]{2,1,0:T(8,128)S(1)}, u32[]{:S(2)}, u32[]{:S(2)}) %collective-permute-start.2) | collective-permute-done | bytes 188448 | tf_op jit(solution)/shard_map/ppermute | solution.py:557
  48.0 0.0 collective-permute-done.3.in_xe
  48.0 0.0 copy-done.11
  48.1 0.0 copy-done.13
  48.1 0.0 copy-done.3
  48.1 0.0 copy-done.4
  48.1 0.0 copy-done.7
  48.1 0.0 copy-done.8
  48.1 0.0 copy-done.9
  48.1 0.0 copy-done.12
  48.1 4.9 %shard_map.143 = (f32[3,384,128]{2,1,0:T(8,128)S(1)}, f32[4,10,16,128]{3,2,1,0:T(8,128)S(1)}, f32[24,8,128]{2,1,0:T(8,128)S(1)}, f32[8,8,128]{2,1,0:T(8,128)S(1)}, f32[8,8,128]{2,1,0:T(8,128)S(1)}) custom-call(f32[128,8,128]{2,1,0:T(8,128)S(1)} %bitcast.17, s32[4,64]{1,0:T(4,128)S(1)} %bitcast.26, s32[2,4]{1,0:T(2,128)S(1)} %bitcast.28, ...), custom_call_target="tpu_custom_call" | custom-call | flops 1000000 | bytes 1000000 | tf_op jit(solution)/shard_map/pallas_call | solution.py:599
  53.1 1.9 %collective-permute-start.5 = (f32[24,8,128]{2,1,0:T(8,128)S(1)}, f32[24,8,128]{2,1,0:T(8,128)S(1)}, u32[]{:S(2)}, u32[]{:S(2)}) collective-permute-start(f32[24,8,128]{2,1,0:T(8,128)S(1)} %shard_map.144.after), channel_id=1, source_target_pairs={{0,16},{32,48},{64,80},{96,112},{128,144},{160,176},{192,208},{224... | collective-permute-start | bytes 294920 | tf_op jit(solution)/shard_map/ppermute | solution.py:557
  55.0 12.1 %collective-permute-start.4 = (f32[24,8,128]{2,1,0:T(8,128)S(1)}, f32[24,8,128]{2,1,0:T(8,128)S(1)}, u32[]{:S(2)}, u32[]{:S(2)}) collective-permute-start(f32[24,8,128]{2,1,0:T(8,128)S(1)} %get-tuple-element.38), channel_id=1, source_target_pairs={{16,32},{48,64},{80,96},{112,128},{144,160},{176,192},{208,224},{2... | collective-permute-start | bytes 294920 | tf_op jit(solution)/shard_map/ppermute | solution.py:557
  67.1 0.0 copy-done.6
  67.1 0.0 copy-start.1
  67.2 8.6 %shard_map.145 = (bf16[96,128,128]{2,1,0:T(8,128)(2,1)S(1)}, bf16[384,16,128]{2,1,0:T(8,128)(2,1)S(1)}, bf16[192,32,256]{2,1,0:T(8,128)(2,1)S(1)}, f32[192,8,128]{2,1,0:T(8,128)S(1)}, s32[640]{0:T(1024)S(1)}) custom-call(s32[2,512]{1,0:T(2,128)S(1)} %bitcast.21, s32[1,1]{1,0:T(1,128)S(6)} %copy.15.total_ref, f32[46,8,128]{2,1,0:T(8,128)S(1)} %collective-permute-done.2.in_xo, ...), custom_call_target="tpu_custom_call" | custom-call | flops 100000000 | bytes 1000000 | tf_op jit(solution)/shard_map/pallas_call | solution.py:621
  75.7 0.0 collective-permute-done.5.in_e
  75.7 4.1 %collective-permute-done.4.in_o = f32[24,8,128]{2,1,0:T(8,128)S(1)} collective-permute-done((f32[24,8,128]{2,1,0:T(8,128)S(1)}, f32[24,8,128]{2,1,0:T(8,128)S(1)}, u32[]{:S(2)}, u32[]{:S(2)}) %collective-permute-start.4) | collective-permute-done | bytes 98336 | tf_op jit(solution)/shard_map/ppermute | solution.py:557
  79.9 0.1 shard_map.146
  80.0 2.5 %collective-permute-start.6 = (f32[34,8,128]{2,1,0:T(8,128)S(1)}, f32[34,8,128]{2,1,0:T(8,128)S(1)}, u32[]{:S(2)}, u32[]{:S(2)}) collective-permute-start(f32[34,8,128]{2,1,0:T(8,128)S(1)} %get-tuple-element.48), channel_id=1, source_target_pairs={{0,1},{2,3},{4,5},{6,7},{8,9},{10,11},{12,13},{14,15},{1,0},{3,2},... | collective-permute-start | bytes 417800 | tf_op jit(solution)/shard_map/ppermute | solution.py:557
  82.5 1.9 %collective-permute-start.7 = (f32[34,8,128]{2,1,0:T(8,128)S(1)}, f32[34,8,128]{2,1,0:T(8,128)S(1)}, u32[]{:S(2)}, u32[]{:S(2)}) collective-permute-start(f32[34,8,128]{2,1,0:T(8,128)S(1)} %get-tuple-element.49.after), channel_id=1, source_target_pairs={{1,2},{3,4},{5,6},{7,8},{9,10},{11,12},{13,14},{2,1},{4,3},{6,5},{... | collective-permute-start | bytes 417800 | tf_op jit(solution)/shard_map/ppermute | solution.py:557
  84.4 0.0 copy-done.1
  84.4 2.0 %shard_map.148 = f32[3,384,128]{2,1,0:T(8,128)} custom-call(s32[2,512]{1,0:T(2,128)S(1)} %bitcast.22, f32[128,8,128]{2,1,0:T(8,128)S(1)} %bitcast.18, f32[46,8,128]{2,1,0:T(8,128)S(1)} %collective-permute-done.2.in_xo, f32[46,8,128]{2,1,0:T(8,128)S(1)} %collective-permute-done.3.in_xe, f32[43,8,128]{2,1,0:T(8,128)S(1)} %collective-permute-done.in_e.in_ye, ...), custom_call_target="tpu_custom_call" | custom-call | flops 1000000000 | bytes 1000000 | tf_op jit(solution)/shard_map/pallas_call | solution.py:637
  86.5 0.0 collective-permute-done.6.in_e
  86.5 2.4 %collective-permute-done.7.in_o = f32[34,8,128]{2,1,0:T(8,128)S(1)} collective-permute-done((f32[34,8,128]{2,1,0:T(8,128)S(1)}, f32[34,8,128]{2,1,0:T(8,128)S(1)}, u32[]{:S(2)}, u32[]{:S(2)}) %collective-permute-start.7) | collective-permute-done | bytes 139296 | tf_op jit(solution)/shard_map/ppermute | solution.py:557
  88.9 1.1 %shard_map.147 = (f32[8,8,128]{2,1,0:T(8,128)}, f32[3,8,8,128]{3,2,1,0:T(8,128)}) custom-call(f32[16,16,128]{2,1,0:T(8,128)S(1)} %get-tuple-element.43.load, f32[3,8,16,128]{3,2,1,0:T(8,128)S(1)} %get-tuple-element.44.drag, f32[16,8,128]{2,1,0:T(8,128)S(1)} %get-tuple-element.45.pres_w, f32[16,8,128]{2,1,0:T(8,128)S(1)} %get-tuple-element.46.gain_w, ...), custom_call_target="tpu_custom_call" | custom-call | flops 1000000 | bytes 1000000 | tf_op jit(solution)/shard_map/pallas_call | solution.py:644
  (1 shorter events, 0.0 us)
Async XLA Ops:
  0.6 47.4 %copy-start.11 = (s32[1,1,4,64]{3,2,1,0:T(4,128)S(1)}, s32[1,1,4,64]{3,2,1,0:T(4,128)}, u32[]{:S(2)}) copy-start(s32[1,1,4,64]{3,2,1,0:T(4,128)} %param.13) | copy-start | bytes 3076
  0.6 47.4 %copy-start.13 = (s32[1,1,2,4]{3,2,1,0:T(2,128)S(1)}, s32[1,1,2,4]{3,2,1,0:T(2,128)}, u32[]{:S(2)}) copy-start(s32[1,1,2,4]{3,2,1,0:T(2,128)} %param.14) | copy-start | bytes 100
  0.7 1.1 %copy-start = (f32[1,1,128,8,128]{4,3,2,1,0:T(8,128)S(1)}, f32[1,1,128,8,128]{4,3,2,1,0:T(8,128)}, u32[]{:S(2)}) copy-start(f32[1,1,128,8,128]{4,3,2,1,0:T(8,128)} %param.12) | copy-start | bytes 1572868
  1.7 0.9 copy-start.2
  2.6 0.7 copy-start.10
  3.3 44.8 %copy-start.3 = (f32[8,8,128]{2,1,0:T(8,128)S(1)}, f32[8,8,128]{2,1,0:T(8,128)}, u32[]{:S(2)}) copy-start(f32[8,8,128]{2,1,0:T(8,128)} %pres.5) | copy-start | bytes 98308
  3.3 44.8 %copy-start.4 = (s32[1,1,384,128]{3,2,1,0:T(8,128)S(1)}, s32[1,1,384,128]{3,2,1,0:T(8,128)}, u32[]{:S(2)}) copy-start(s32[1,1,384,128]{3,2,1,0:T(8,128)} %param.18) | copy-start | bytes 589828
  3.3 44.8 %copy-start.7 = (f32[8,8,128]{2,1,0:T(8,128)S(1)}, f32[8,8,128]{2,1,0:T(8,128)}, u32[]{:S(2)}) copy-start(f32[8,8,128]{2,1,0:T(8,128)} %screen.1) | copy-start | bytes 98308
  3.3 44.8 %copy-start.8 = (f32[8,8,128]{2,1,0:T(8,128)S(1)}, f32[8,8,128]{2,1,0:T(8,128)}, u32[]{:S(2)}) copy-start(f32[8,8,128]{2,1,0:T(8,128)} %source.1) | copy-start | bytes 98308
  3.3 44.8 %copy-start.9 = (f32[8,8,128]{2,1,0:T(8,128)S(1)}, f32[8,8,128]{2,1,0:T(8,128)}, u32[]{:S(2)}) copy-start(f32[8,8,128]{2,1,0:T(8,128)} %solid.1) | copy-start | bytes 98308
  3.3 44.8 %copy-start.12 = (s32[1,1,384,4]{2,3,1,0:T(4,128)S(1)}, s32[1,1,384,4]{2,3,1,0:T(4,128)}, u32[]{:S(2)}) copy-start(s32[1,1,384,4]{2,3,1,0:T(4,128)} %param.17) | copy-start | bytes 18436
  4.1 63.1 %copy-start.6 = (s32[1,1,512,2]{2,3,1,0:T(2,128)S(1)}, s32[1,1,512,2]{2,3,1,0:T(2,128)}, u32[]{:S(2)}) copy-start(s32[1,1,512,2]{2,3,1,0:T(2,128)} %param.15) | copy-start | bytes 12292
  4.1 6.0 %collective-permute-start = (f32[43,8,128]{2,1,0:T(8,128)S(1)}, f32[43,8,128]{2,1,0:T(8,128)S(1)}, u32[]{:S(2)}, u32[]{:S(2)}) collective-permute-start(f32[43,8,128]{2,1,0:T(8,128)S(1)} %get-tuple-element.30), channel_id=1, source_target_pairs={{0,1},{2,3},{4,5},{6,7},{8,9},{10,11},{12,13},{14,15},{1,0},{3,2},... | collective-permute-start | bytes 528392 | tf_op jit(solution)/shard_map/ppermute | solution.py:557
  6.7 6.8 %collective-permute-start.1 = (f32[43,8,128]{2,1,0:T(8,128)S(1)}, f32[43,8,128]{2,1,0:T(8,128)S(1)}, u32[]{:S(2)}, u32[]{:S(2)}) collective-permute-start(f32[43,8,128]{2,1,0:T(8,128)S(1)} %get-tuple-element.31), channel_id=1, source_target_pairs={{1,2},{3,4},{5,6},{7,8},{9,10},{11,12},{13,14},{2,1},{4,3},{6,5},{... | collective-permute-start | bytes 528392 | tf_op jit(solution)/shard_map/ppermute | solution.py:557
  14.8 33.3 %collective-permute-start.2 = (f32[46,8,128]{2,1,0:T(8,128)S(1)}, f32[46,8,128]{2,1,0:T(8,128)S(1)}, u32[]{:S(2)}, u32[]{:S(2)}) collective-permute-start(f32[46,8,128]{2,1,0:T(8,128)S(1)} %shard_map.141.after), channel_id=1, source_target_pairs={{16,32},{48,64},{80,96},{112,128},{144,160},{176,192},{208,224},{2... | collective-permute-start | bytes 565256 | tf_op jit(solution)/shard_map/ppermute | solution.py:557
  28.9 19.2 %collective-permute-start.3 = (f32[46,8,128]{2,1,0:T(8,128)S(1)}, f32[46,8,128]{2,1,0:T(8,128)S(1)}, u32[]{:S(2)}, u32[]{:S(2)}) collective-permute-start(f32[46,8,128]{2,1,0:T(8,128)S(1)} %get-tuple-element.33), channel_id=1, source_target_pairs={{0,16},{32,48},{64,80},{96,112},{128,144},{160,176},{192,208},{224... | collective-permute-start | bytes 565256 | tf_op jit(solution)/shard_map/ppermute | solution.py:557
  31.5 0.7 copy-start.5
  53.1 22.6 %collective-permute-start.5 = (f32[24,8,128]{2,1,0:T(8,128)S(1)}, f32[24,8,128]{2,1,0:T(8,128)S(1)}, u32[]{:S(2)}, u32[]{:S(2)}) collective-permute-start(f32[24,8,128]{2,1,0:T(8,128)S(1)} %shard_map.144.after), channel_id=1, source_target_pairs={{0,16},{32,48},{64,80},{96,112},{128,144},{160,176},{192,208},{224... | collective-permute-start | bytes 294920 | tf_op jit(solution)/shard_map/ppermute | solution.py:557
  55.0 24.9 %collective-permute-start.4 = (f32[24,8,128]{2,1,0:T(8,128)S(1)}, f32[24,8,128]{2,1,0:T(8,128)S(1)}, u32[]{:S(2)}, u32[]{:S(2)}) collective-permute-start(f32[24,8,128]{2,1,0:T(8,128)S(1)} %get-tuple-element.38), channel_id=1, source_target_pairs={{16,32},{48,64},{80,96},{112,128},{144,160},{176,192},{208,224},{2... | collective-permute-start | bytes 294920 | tf_op jit(solution)/shard_map/ppermute | solution.py:557
  67.1 17.3 %copy-start.1 = (f32[1,1,128,8,128]{4,3,2,1,0:T(8,128)S(1)}, f32[1,1,128,8,128]{4,3,2,1,0:T(8,128)}, u32[]{:S(2)}) copy-start(f32[1,1,128,8,128]{4,3,2,1,0:T(8,128)} %param.12) | copy-start | bytes 1572868
  80.0 6.5 %collective-permute-start.6 = (f32[34,8,128]{2,1,0:T(8,128)S(1)}, f32[34,8,128]{2,1,0:T(8,128)S(1)}, u32[]{:S(2)}, u32[]{:S(2)}) collective-permute-start(f32[34,8,128]{2,1,0:T(8,128)S(1)} %get-tuple-element.48), channel_id=1, source_target_pairs={{0,1},{2,3},{4,5},{6,7},{8,9},{10,11},{12,13},{14,15},{1,0},{3,2},... | collective-permute-start | bytes 417800 | tf_op jit(solution)/shard_map/ppermute | solution.py:557
  82.5 6.4 %collective-permute-start.7 = (f32[34,8,128]{2,1,0:T(8,128)S(1)}, f32[34,8,128]{2,1,0:T(8,128)S(1)}, u32[]{:S(2)}, u32[]{:S(2)}) collective-permute-start(f32[34,8,128]{2,1,0:T(8,128)S(1)} %get-tuple-element.49.after), channel_id=1, source_target_pairs={{1,2},{3,4},{5,6},{7,8},{9,10},{11,12},{13,14},{2,1},{4,3},{6,5},{... | collective-permute-start | bytes 417800 | tf_op jit(solution)/shard_map/ppermute | solution.py:557
